TPU v7x, 256 devices: a whole 4x4x8 slice. The times are simulated.
256 devices in a mesh: pp: 4 (over y_lo, core), ep: 64 (over x, y_hi, z).
Axes of the slice: x: 4, y: 4 (y_hi: 2, y_lo: 2; y = y_hi * 2 + y_lo), z: 8, core: 2. Of those that a mesh axis runs over, the one named last changes fastest.
Arguments:
- fwd_in: bfloat16 [4, 4096, 7168], P('pp', 'ep'), may hold values from -6 to 6
- fwd_ids: int32 [4, 4096, 1], P('pp', 'ep'), may hold values from 0 to 7
- fwd_gates: float32 [4, 4096, 1], P('pp', 'ep'), may hold values from 0.2 to 1.5
- bwd_x: bfloat16 [4, 4096, 7168], P('pp', 'ep'), may hold values from -6 to 6
- bwd_grad: bfloat16 [4, 4096, 7168], P('pp', 'ep'), may hold values from -6 to 6
- bwd_ids: int32 [4, 4096, 1], P('pp', 'ep'), may hold values from 0 to 7
- bwd_gates: float32 [4, 4096, 1], P('pp', 'ep'), may hold values from 0.2 to 1.5
- norm_gain: float32 [4, 7168], P('pp'), may hold values from 0.25 to 1.75
- w_gate: bfloat16 [4, 64, 7168, 128], P('pp', 'ep'), may hold values from -0.0625 to 0.0625
- w_up: bfloat16 [4, 64, 7168, 128], P('pp', 'ep'), may hold values from -0.0625 to 0.0625
- w_down: bfloat16 [4, 64, 128, 7168], P('pp', 'ep'), may hold values from -0.1875 to 0.1875
Outputs:
- fwd_out: bfloat16 [4, 4096, 7168], P('pp', 'ep')
- bwd_out: bfloat16 [4, 4096, 7168], P('pp', 'ep')
Inputs may be any that keep to these rules, and one draw needn't show every extreme that they name: `fwd_ids`: each row names one expert. `bwd_ids`: as for fwd_ids.
All inputs are finite; a program needn't handle non-finite values.
Results may differ from a plain program's by a relative error of at most 0.0053.
Values may be sent and summed in bfloat16 or wider, within the bound.
No kernel may reach another device: no remote copies, remote signals or barrier semaphores. Data moves between devices by JAX's collectives and lax.ppermute only.
A program may use at most 128 MiB of HBM per device.

v0:
```python
import functools

import jax
import jax.numpy as jnp
from jax import lax
from jax.experimental import pallas as pl
from jax.experimental.pallas import tpu as pltpu
from jax.sharding import Mesh, PartitionSpec as P

EPSILON = 1e-06
BF16 = jnp.bfloat16
F32 = jnp.float32
CHUNK = 1024
NT = (((1,), (1,)), ((), ()))
TN = (((0,), (0,)), ((), ()))


def shifted(block, axis, distance):
    count = lax.axis_size(axis)
    route = [(i, (i + distance) % count) for i in range(count)]
    return lax.ppermute(block, axis, route)


def call(kernel, outs, *args):
    return pl.pallas_call(
        kernel,
        out_shape=outs,
        in_specs=[pl.BlockSpec(memory_space=pltpu.VMEM)] * len(args),
        out_specs=[pl.BlockSpec(memory_space=pltpu.VMEM)] * len(outs),
        compiler_params=pltpu.CompilerParams(vmem_limit_bytes=12 << 20),
    )(*args)


def like(blocks):
    return [jax.ShapeDtypeStruct(block.shape, block.dtype) for block in blocks]


def chunks(features, step, start):
    def at(i, carry):
        return step(pl.multiple_of(i * CHUNK, CHUNK), carry)

    return lax.fori_loop(0, features // CHUNK, at, start)


def selector(ids_ref, experts, capacity):
    ids = ids_ref[...]
    tok_count = ids.shape[1]
    onehot = (lax.broadcasted_iota(jnp.int32, (experts, tok_count), 0) == ids).astype(F32)
    order = (tok_count, tok_count)
    earlier = lax.broadcasted_iota(jnp.int32, order, 0) < lax.broadcasted_iota(jnp.int32, order, 1)
    before = jnp.dot(onehot, earlier.astype(F32), preferred_element_type=F32)
    slot_index = jnp.sum(before * onehot, axis=0, keepdims=True).astype(jnp.int32)
    target = jnp.where(slot_index < capacity, ids * capacity + slot_index, -1)
    slots = lax.broadcasted_iota(jnp.int32, (experts * capacity, tok_count), 0)
    return (slots == target).astype(F32)


def row_scale(x_ref):
    rows, features = x_ref.shape

    def step(at, total):
        values = x_ref[:, pl.ds(at, CHUNK)].astype(F32)
        return total + jnp.sum(values * values, axis=1, keepdims=True)

    total = chunks(features, step, jnp.zeros((rows, 1), F32))
    return lax.rsqrt(total / features + EPSILON)


def deal(out_ref, at, rows):
    experts, capacity = out_ref.shape[:2]
    for e in range(experts):
        out_ref[e, :, pl.ds(at, CHUNK)] = rows[e * capacity : (e + 1) * capacity].astype(BF16)


def collect(in_ref, at):
    return jnp.concatenate(
        [in_ref[e, :, pl.ds(at, CHUNK)].astype(F32) for e in range(in_ref.shape[0])], axis=0
    )


def norm_slots(x_ref, ids_ref, gain_ref, out_ref, base=0):
    select = selector(ids_ref, *out_ref.shape[:2]).astype(BF16)
    scale = row_scale(x_ref)

    def step(at, carry):
        part = pl.ds(at, CHUNK)
        normed = (x_ref[:, part].astype(F32) * scale * gain_ref[:, part]).astype(BF16)
        deal(out_ref, at + base, jnp.dot(select, normed, preferred_element_type=F32))
        return carry

    chunks(x_ref.shape[1], step, 0)


def scaled_slots(x_ref, ids_ref, gates_ref, out_ref, base):
    select = selector(ids_ref, *out_ref.shape[:2])
    gate = jnp.sum(select * gates_ref[...], axis=1, keepdims=True)
    select = select.astype(BF16)

    def step(at, carry):
        rows = jnp.dot(select, x_ref[:, pl.ds(at, CHUNK)], preferred_element_type=F32)
        deal(out_ref, at + base, rows * gate)
        return carry

    chunks(x_ref.shape[1], step, 0)


def send_kernel(a_ref, a_ids_ref, gain_ref, b_ref, b_ids_ref, b_gates_ref, out_ref):
    norm_slots(a_ref, a_ids_ref, gain_ref, out_ref)
    scaled_slots(b_ref, b_ids_ref, b_gates_ref, out_ref, a_ref.shape[1])


def unpack_kernel(in_ref, *outs):
    features = outs[0].shape[1]
    for n, out in enumerate(outs):

        def step(at, carry, out=out, n=n):
            out[:, pl.ds(at, CHUNK)] = collect(in_ref, at + n * features).astype(BF16)
            return carry

        chunks(features, step, 0)


def total_kernel(*refs):
    out_ref = refs[-1]
    features = refs[0].shape[1]
    for n in range(len(refs) // 3):
        trio = refs[3 * n : 3 * n + 3]

        def step(at, carry, trio=trio, n=n):
            part = pl.ds(at, CHUNK)
            total = sum(ref[:, part].astype(F32) for ref in trio)
            deal(out_ref, at + n * features, total)
            return carry

        chunks(features, step, 0)


def column(row, count):
    diagonal = lax.broadcasted_iota(jnp.int32, (count, count), 0) == lax.broadcasted_iota(
        jnp.int32, (count, count), 1
    )
    return jnp.sum(jnp.where(diagonal, row, 0.0), axis=1, keepdims=True)


def result_kernel(
    back_ref, a_ref, a_ids_ref, a_gates_ref, x_ref, b_ref, b_ids_ref, gain_ref, a_out, b_out, held
):
    rows, features = a_ref.shape
    a_select = selector(a_ids_ref, *back_ref.shape[:2]).astype(BF16)
    b_select = selector(b_ids_ref, *back_ref.shape[:2]).astype(BF16)
    a_gate = column(a_gates_ref[...], rows)

    def first(at, carry):
        squares, products = carry
        part = pl.ds(at, CHUNK)
        mix = lax.dot_general(
            a_select, collect(back_ref, at).astype(BF16), TN, preferred_element_type=F32
        )
        a_out[:, part] = (a_ref[:, part].astype(F32) + mix * a_gate).astype(BF16)
        grad = lax.dot_general(
            b_select, collect(back_ref, at + features).astype(BF16), TN, preferred_element_type=F32
        )
        grad = grad * gain_ref[:, part]
        held[:, part] = grad
        values = x_ref[:, part].astype(F32)
        squares += jnp.sum(values * values, axis=1, keepdims=True)
        products += jnp.sum(values * grad, axis=1, keepdims=True)
        return squares, products

    zero = jnp.zeros((rows, 1), F32)
    squares, products = chunks(features, first, (zero, zero))
    scale = lax.rsqrt(squares / features + EPSILON)
    pull = scale**3 * (products / features)

    def second(at, carry):
        part = pl.ds(at, CHUNK)
        back = scale * held[:, part] - x_ref[:, part].astype(F32) * pull
        b_out[:, part] = (b_ref[:, part].astype(F32) + back).astype(BF16)
        return carry

    chunks(features, second, 0)


def ring_gather(block, far_way):
    far = lax.axis_size("k") // 2
    blocks = {0: block}
    for step in range(1, far):
        for way in (1, -1):
            blocks[-way * step] = shifted(blocks[-way * (step - 1)], "k", way)
    blocks[far] = shifted(blocks[-far_way * (far - 1)], "k", far_way)
    return blocks


def add(a, b):
    return (a.astype(F32) + b.astype(F32)).astype(BF16)


def ring_reduce(parts, far_way):
    far = lax.axis_size("k") // 2
    sums = []
    for way in (far_way, -far_way):
        held = parts[far] if way == far_way else parts[way * (far - 1)]
        for step in range(far - 1 if way == far_way else far - 2, -1, -1):
            held = shifted(held, "k", way)
            if step:
                held = add(held, parts[way * step])
        sums.append(held)
    return [parts[0], *sums]


def stacked(blocks, part):
    return jnp.concatenate([block[:, part].astype(F32) for block in blocks], axis=0).astype(BF16)


def put(outs, part, value):
    at = 0
    for out in outs:
        out[:, part] = value[at : at + out.shape[0]].astype(BF16)
        at += out.shape[0]


def activations(blocks, gate_ref, up_ref):
    features, width = gate_ref.shape
    rows = sum(block.shape[0] for block in blocks)

    def step(at, total):
        part = pl.ds(at, CHUNK)
        right = jnp.concatenate([gate_ref[part, :], up_ref[part, :]], axis=1)
        return total + jnp.dot(stacked(blocks, part), right, preferred_element_type=F32)

    total = chunks(features, step, jnp.zeros((rows, 2 * width), F32))
    return total[:, :width], total[:, width:]


def forward_kernel(count, *refs):
    blocks, outs = refs[:count], refs[count + 3 :]
    gate_ref, up_ref, down_ref = refs[count : count + 3]
    act_gate, act_up = activations(blocks, gate_ref, up_ref)
    hidden = (act_gate * jax.nn.sigmoid(act_gate) * act_up).astype(BF16)

    def step(at, carry):
        part = pl.ds(at, CHUNK)
        put(outs, part, jnp.dot(hidden, down_ref[:, part], preferred_element_type=F32))
        return carry

    chunks(down_ref.shape[1], step, 0)


def act_kernel(count, *refs):
    blocks, (gate_ref, up_ref), outs = refs[:count], refs[count : count + 2], refs[count + 2 :]
    at = 0
    acts = activations(blocks, gate_ref, up_ref)
    for block, gate_out, up_out in zip(blocks, outs[::2], outs[1::2]):
        rows = block.shape[0]
        gate_out[...], up_out[...] = (act[at : at + rows] for act in acts)
        at += rows


def backward_kernel(count, *refs):
    blocks, acts, rest, outs = (
        refs[:count],
        refs[count : 3 * count],
        refs[3 * count : 3 * count + 3],
        refs[3 * count + 3 :],
    )
    gate_ref, up_ref, down_ref = rest
    rows = sum(block.shape[0] for block in blocks)

    def inner(at, total):
        part = pl.ds(at, CHUNK)
        return total + lax.dot_general(
            stacked(blocks, part), down_ref[:, part], NT, preferred_element_type=F32
        )

    zero = jnp.zeros((rows, down_ref.shape[0]), F32)
    back = chunks(down_ref.shape[1], inner, zero)
    act_gate = jnp.concatenate([ref[...] for ref in acts[::2]], axis=0)
    act_up = jnp.concatenate([ref[...] for ref in acts[1::2]], axis=0)
    sigma = jax.nn.sigmoid(act_gate)
    grad_gate = (back * act_up * sigma * (1.0 + act_gate * (1.0 - sigma))).astype(BF16)
    grad_up = (back * act_gate * sigma).astype(BF16)
    left = jnp.concatenate([grad_gate, grad_up], axis=1)

    def outer(at, carry):
        part = pl.ds(at, CHUNK)
        right = jnp.concatenate([gate_ref[part, :], up_ref[part, :]], axis=1)
        put(outs, part, lax.dot_general(left, right, NT, preferred_element_type=F32))
        return carry

    chunks(gate_ref.shape[0], outer, 0)


def forward_parts(blocks, keys, weights):
    rows = [blocks[key] for key in keys]
    outs = call(functools.partial(forward_kernel, len(rows)), like(rows), *rows, *weights)
    return dict(zip(keys, outs))


def gate_and_up(blocks, keys, gate_mat, up_mat):
    rows = [blocks[key] for key in keys]
    width = gate_mat.shape[1]
    outs = [jax.ShapeDtypeStruct((row.shape[0], width), F32) for row in rows for _ in range(2)]
    outs = call(functools.partial(act_kernel, len(rows)), outs, *rows, gate_mat, up_mat)
    return {key: outs[2 * i : 2 * i + 2] for i, key in enumerate(keys)}


def backward_parts(blocks, acts, keys, weights):
    rows = [blocks[key] for key in keys]
    pairs = [act for key in keys for act in acts[key]]
    outs = call(functools.partial(backward_kernel, len(rows)), like(rows), *rows, *pairs, *weights)
    return dict(zip(keys, outs))


def exchange(slots):
    return lax.all_to_all(slots, "e", split_axis=0, concat_axis=0, tiled=True)


def body(
    fwd_in, fwd_ids, fwd_gates, bwd_x, bwd_grad, bwd_ids, bwd_gates, norm_gain, w_gate, w_up, w_down
):
    experts = lax.axis_size("e")
    tok_count, features = fwd_in.shape[1:]
    capacity = max(2, tok_count * fwd_ids.shape[2] // 20)
    weights = gate_mat, up_mat, down_mat = w_gate[0, 0], w_up[0, 0], w_down[0, 0]
    fwd_ids, fwd_gates = fwd_ids.reshape(1, tok_count), fwd_gates.reshape(1, tok_count)
    bwd_ids, bwd_gates = bwd_ids.reshape(1, tok_count), bwd_gates.reshape(1, tok_count)
    bwd_x = bwd_x[0]

    def slots(width):
        return jax.ShapeDtypeStruct((experts, capacity, width), BF16)

    rows = jax.ShapeDtypeStruct((experts * capacity, features), BF16)
    arrived = shifted(fwd_in[0], "pp", 1)
    upstream = shifted(bwd_grad[0], "pp", -1)

    (bwd_send,) = call(norm_slots, [slots(features)], bwd_x, bwd_ids, norm_gain)
    (bwd_slots,) = call(unpack_kernel, [rows], exchange(bwd_send))
    (send,) = call(
        send_kernel,
        [slots(2 * features)],
        *(arrived, fwd_ids, norm_gain, upstream, bwd_ids, bwd_gates),
    )
    fwd_slots, grad_slots = call(unpack_kernel, [rows, rows], exchange(send))

    bwd_blocks = ring_gather(bwd_slots, 1)
    fwd_blocks = ring_gather(fwd_slots, -1)
    grad_blocks = ring_gather(grad_slots, 1)

    near, last = [0, 1, -1, 2, -2, 3, -3], [4]
    fwd_parts = forward_parts(fwd_blocks, near, weights)
    fwd_parts |= forward_parts(fwd_blocks, last, weights)
    fwd_sums = ring_reduce(fwd_parts, -1)

    acts = gate_and_up(bwd_blocks, near + last, gate_mat, up_mat)
    bwd_parts = backward_parts(grad_blocks, acts, near, weights)
    bwd_parts |= backward_parts(grad_blocks, acts, last, weights)
    bwd_sums = ring_reduce(bwd_parts, 1)

    (back,) = call(total_kernel, [slots(2 * features)], *fwd_sums, *bwd_sums)
    back = exchange(back)

    out = jax.ShapeDtypeStruct((tok_count, features), BF16)
    forward_result, backward_result = pl.pallas_call(
        result_kernel,
        out_shape=[out, out],
        in_specs=[pl.BlockSpec(memory_space=pltpu.VMEM)] * 8,
        out_specs=[pl.BlockSpec(memory_space=pltpu.VMEM)] * 2,
        scratch_shapes=[pltpu.VMEM((tok_count, features), F32)],
        compiler_params=pltpu.CompilerParams(vmem_limit_bytes=12 << 20),
    )(back, arrived, fwd_ids, fwd_gates, bwd_x, upstream, bwd_ids, norm_gain)
    return (forward_result[None], backward_result[None])


def solution(mesh):
    sections, devices = mesh.devices.shape
    slices = devices // max(2, devices // 8)
    grid = Mesh(mesh.devices.reshape(sections, devices // slices, slices), ("pp", "e", "k"))
    tokens = P("pp", ("e", "k"), None)
    weights = P("pp", ("e", "k"), None, None)
    placed = (tokens,) * 7 + (P("pp", None),) + (weights,) * 3
    return jax.shard_map(
        body, mesh=grid, in_specs=placed, out_specs=(tokens, tokens), check_vma=False
    )
```

profile of v0, /device:TPU:2, one launch (start us, length us, event | category | flops | bytes accessed | tf_op | source)
XLA Modules:
  0.0 213.3 jit_solution(11440540742367976988)
XLA Ops:
  0.7 1.7 collective-permute-start.1
  2.5 1.2 copy-done.5
  5.1 2.1 shard_map.126
  7.2 23.8 %all_to_all.15.in_ref = bf16[8,3,7168]{2,1,0:T(4,128)(2,1)S(1)} all-to-all(bf16[8,3,7168]{2,1,0:T(4,128)(2,1)S(1)} %shard_map.126), channel_id=1, replica_groups=mesh['pp'=4,'e'=8,'k'=8] {'e'}, dimensions={0} | all-to-all | bytes 688128 | tf_op jit(solution)/shard_map/all_to_all | solution.py:315
  31.2 2.0 collective-permute-start.23
  33.2 3.4 %shard_map.122 = bf16[8,3,14336]{2,1,0:T(4,128)(2,1)S(1)} custom-call(bf16[64,7168]{1,0:T(8,128)(2,1)S(1)} %collective-permute-done.a_ref, s32[1,64]{1,0:T(1,128)S(1)} %bitcast.31, f32[1,7168]{1,0:T(1,128)S(1)} %copy-done.11, bf16[64,7168]{1,0:T(8,128)(2,1)S(1)} %collective-permute-done.1.b_ref, s32[1,64]{1,0:T(1,128)S(1)} %bitcast.29, f32[1,64]{1,0:T(1,128)S(1)} %bitcast.33), custom_call_target="tpu_custom_call" | custom-call | tf_op jit(solution)/shard_map/pallas_call | solution.py:25
  38.5 1.0 copy-done.9
  39.4 5.0 %all-to-all-start = ((bf16[8,3,14336]{2,1,0:T(4,128)(2,1)}), bf16[8,3,14336]{2,1,0:T(4,128)(2,1)S(1)}, u32[]{:S(2)}, u32[]{:S(2)}) async-start(bf16[8,3,14336]{2,1,0:T(4,128)(2,1)} %copy-done.4), calls=%async_computation | async-start | bytes 1835008 | tf_op jit(solution)/shard_map/all_to_all | solution.py:315
  44.5 4.0 %collective-permute-start.22 = (bf16[24,7168]{1,0:T(8,128)(2,1)S(1)}, bf16[24,7168]{1,0:T(8,128)(2,1)}, u32[]{:S(2)}, u32[]{:S(2)}) collective-permute-start(bf16[24,7168]{1,0:T(8,128)(2,1)S(1)} %shard_map.127.refs_0_), channel_id=1, source_target_pairs={{0,7},{1,0},{2,1},{3,2},{4,3},{5,4},{6,5},{7,6},{8,15},{9,8},{10,9... | collective-permute-start | bytes 1032200 | tf_op jit(solution)/shard_map/ppermute | solution.py:21
  48.4 6.2 %collective-permute-done.22.refs_1_ = bf16[24,7168]{1,0:T(8,128)(2,1)} collective-permute-done((bf16[24,7168]{1,0:T(8,128)(2,1)S(1)}, bf16[24,7168]{1,0:T(8,128)(2,1)}, u32[]{:S(2)}, u32[]{:S(2)}) %collective-permute-start.22) | collective-permute-done | bytes 344096 | tf_op jit(solution)/shard_map/ppermute | solution.py:21
  54.6 3.8 %collective-permute-start.24 = (bf16[24,7168]{1,0:T(8,128)(2,1)}, bf16[24,7168]{1,0:T(8,128)(2,1)}, u32[]{:S(2)}, u32[]{:S(2)}) collective-permute-start(bf16[24,7168]{1,0:T(8,128)(2,1)} %collective-permute-done.22.refs_1_), channel_id=1, source_target_pairs={{0,7},{1,0},{2,1},{3,2},{4,3},{5,4},{6,5},{7,6},{8,15},{9,8},{10,9... | collective-permute-start | bytes 1032200 | tf_op jit(solution)/shard_map/ppermute | solution.py:21
  59.4 2.9 %collective-permute-start.16 = (bf16[24,7168]{1,0:T(8,128)(2,1)S(1)}, bf16[24,7168]{1,0:T(8,128)(2,1)S(1)}, u32[]{:S(2)}, u32[]{:S(2)}) collective-permute-start(bf16[24,7168]{1,0:T(8,128)(2,1)S(1)} %get-tuple-element.44.refs_0_), channel_id=1, source_target_pairs={{0,7},{1,0},{2,1},{3,2},{4,3},{5,4},{6,5},{7,6},{8,15},{9,8},{10,9... | collective-permute-start | bytes 1032200 | tf_op jit(solution)/shard_map/ppermute | solution.py:21
  62.3 5.0 %collective-permute-done.24.refs_3_ = bf16[24,7168]{1,0:T(8,128)(2,1)} collective-permute-done((bf16[24,7168]{1,0:T(8,128)(2,1)}, bf16[24,7168]{1,0:T(8,128)(2,1)}, u32[]{:S(2)}, u32[]{:S(2)}) %collective-permute-start.24) | collective-permute-done | bytes 344096 | tf_op jit(solution)/shard_map/ppermute | solution.py:21
  67.3 3.7 %collective-permute-start.26 = (bf16[24,7168]{1,0:T(8,128)(2,1)}, bf16[24,7168]{1,0:T(8,128)(2,1)S(1)}, u32[]{:S(2)}, u32[]{:S(2)}) collective-permute-start(bf16[24,7168]{1,0:T(8,128)(2,1)} %collective-permute-done.24.refs_3_), channel_id=1, source_target_pairs={{0,7},{1,0},{2,1},{3,2},{4,3},{5,4},{6,5},{7,6},{8,15},{9,8},{10,9... | collective-permute-start | bytes 1032200 | tf_op jit(solution)/shard_map/ppermute | solution.py:21
  71.0 2.0 collective-permute-start.3
  73.0 5.2 %collective-permute-done.17.refs_2_ = bf16[24,7168]{1,0:T(8,128)(2,1)S(1)} collective-permute-done((bf16[24,7168]{1,0:T(8,128)(2,1)S(1)}, bf16[24,7168]{1,0:T(8,128)(2,1)S(1)}, u32[]{:S(2)}, u32[]{:S(2)}) %collective-permute-start.17) | collective-permute-done | bytes 344096 | tf_op jit(solution)/shard_map/ppermute | solution.py:21
  78.2 3.2 %collective-permute-start.18 = (bf16[24,7168]{1,0:T(8,128)(2,1)S(1)}, bf16[24,7168]{1,0:T(8,128)(2,1)S(1)}, u32[]{:S(2)}, u32[]{:S(2)}) collective-permute-start(bf16[24,7168]{1,0:T(8,128)(2,1)S(1)} %collective-permute-done.16.refs_1_), channel_id=1, source_target_pairs={{0,7},{1,0},{2,1},{3,2},{4,3},{5,4},{6,5},{7,6},{8,15},{9,8},{10,9... | collective-permute-start | bytes 1032200 | tf_op jit(solution)/shard_map/ppermute | solution.py:21
  82.0 7.3 %collective-permute-done.2.refs_1_ = bf16[24,7168]{1,0:T(8,128)(2,1)S(1)} collective-permute-done((bf16[24,7168]{1,0:T(8,128)(2,1)S(1)}, bf16[24,7168]{1,0:T(8,128)(2,1)S(1)}, u32[]{:S(2)}, u32[]{:S(2)}) %collective-permute-start.2) | collective-permute-done | bytes 344096 | tf_op jit(solution)/shard_map/ppermute | solution.py:21
  89.3 3.7 %collective-permute-start.4 = (bf16[24,7168]{1,0:T(8,128)(2,1)S(1)}, bf16[24,7168]{1,0:T(8,128)(2,1)S(1)}, u32[]{:S(2)}, u32[]{:S(2)}) collective-permute-start(bf16[24,7168]{1,0:T(8,128)(2,1)S(1)} %collective-permute-done.2.refs_1_), channel_id=1, source_target_pairs={{0,7},{1,0},{2,1},{3,2},{4,3},{5,4},{6,5},{7,6},{8,15},{9,8},{10,9... | collective-permute-start | bytes 1032200 | tf_op jit(solution)/shard_map/ppermute | solution.py:21
  93.1 3.6 %collective-permute-done.18.refs_3_ = bf16[24,7168]{1,0:T(8,128)(2,1)S(1)} collective-permute-done((bf16[24,7168]{1,0:T(8,128)(2,1)S(1)}, bf16[24,7168]{1,0:T(8,128)(2,1)S(1)}, u32[]{:S(2)}, u32[]{:S(2)}) %collective-permute-start.18) | collective-permute-done | bytes 344096 | tf_op jit(solution)/shard_map/ppermute | solution.py:21
  96.7 3.7 %collective-permute-start.20 = (bf16[24,7168]{1,0:T(8,128)(2,1)S(1)}, bf16[24,7168]{1,0:T(8,128)(2,1)S(1)}, u32[]{:S(2)}, u32[]{:S(2)}) collective-permute-start(bf16[24,7168]{1,0:T(8,128)(2,1)S(1)} %collective-permute-done.18.refs_3_), channel_id=1, source_target_pairs={{0,7},{1,0},{2,1},{3,2},{4,3},{5,4},{6,5},{7,6},{8,15},{9,8},{10,9... | collective-permute-start | bytes 1032200 | tf_op jit(solution)/shard_map/ppermute | solution.py:21
  100.4 1.5 copy-done.1
  101.9 3.4 %shard_map.128 = (f32[24,128]{1,0:T(8,128)S(1)}, f32[24,128]{1,0:T(8,128)S(1)}, f32[24,128]{1,0:T(8,128)S(1)}, f32[24,128]{1,0:T(8,128)S(1)}, f32[24,128]{1,0:T(...) custom-call(bf16[24,7168]{1,0:T(8,128)(2,1)S(1)} %shard_map.127.refs, ...), custom_call_target="tpu_custom_call" | custom-call | tf_op jit(solution)/shard_map/pallas_call | solution.py:25
  105.3 2.4 %collective-permute-start.6 = (bf16[24,7168]{1,0:T(8,128)(2,1)S(1)}, bf16[24,7168]{1,0:T(8,128)(2,1)S(1)}, u32[]{:S(2)}, u32[]{:S(2)}) collective-permute-start(bf16[24,7168]{1,0:T(8,128)(2,1)S(1)} %collective-permute-done.4.refs_3_), channel_id=1, source_target_pairs={{0,7},{1,0},{2,1},{3,2},{4,3},{5,4},{6,5},{7,6},{8,15},{9,8},{10,9... | collective-permute-start | bytes 1032200 | tf_op jit(solution)/shard_map/ppermute | solution.py:21
  107.7 7.4 %collective-permute-done.21.refs_6_ = bf16[24,7168]{1,0:T(8,128)(2,1)S(1)} collective-permute-done((bf16[24,7168]{1,0:T(8,128)(2,1)S(1)}, bf16[24,7168]{1,0:T(8,128)(2,1)S(1)}, u32[]{:S(2)}, u32[]{:S(2)}) %collective-permute-start.21) | collective-permute-done | bytes 344096 | tf_op jit(solution)/shard_map/ppermute | solution.py:21
  115.1 4.1 %shard_map.129 = (bf16[24,7168]{1,0:T(8,128)(2,1)S(1)}, bf16[24,7168]{1,0:T(8,128)(2,1)S(1)}, bf16[24,7168]{1,0:T(8,128)(2,1)S(1)}, bf16[24,7168]{1,0:T(8,128)(2...) custom-call(bf16[24,7168]{1,0:T(8,128)(2,1)S(1)} %get-tuple-element.44.refs_0_, ...), custom_call_target="tpu_custom_call" | custom-call | tf_op jit(solution)/shard_map/pallas_call | solution.py:25
  119.4 3.6 %shard_map.124 = (bf16[24,7168]{1,0:T(8,128)(2,1)S(1)}, bf16[24,7168]{1,0:T(8,128)(2,1)S(1)}, bf16[24,7168]{1,0:T(8,128)(2,1)S(1)}, bf16[24,7168]{1,0:T(8,128)(2...) custom-call(bf16[24,7168]{1,0:T(8,128)(2,1)S(1)} %get-tuple-element.36.refs_0_, ...), custom_call_target="tpu_custom_call" | custom-call | tf_op jit(solution)/shard_map/pallas_call | solution.py:25
  123.0 2.1 collective-permute-start.13
  125.1 3.1 %collective-permute-start.8 = (bf16[24,7168]{1,0:T(8,128)(2,1)S(1)}, bf16[24,7168]{1,0:T(8,128)(2,1)S(1)}, u32[]{:S(2)}, u32[]{:S(2)}) collective-permute-start(bf16[24,7168]{1,0:T(8,128)(2,1)S(1)} %collective-permute-done.6.refs_5_), channel_id=1, source_target_pairs={{0,7},{1,0},{2,1},{3,2},{4,3},{5,4},{6,5},{7,6},{8,15},{9,8},{10,9... | collective-permute-start | bytes 1032200 | tf_op jit(solution)/shard_map/ppermute | solution.py:21
  128.3 2.0 collective-permute-done.34
  130.4 7.4 %collective-permute-done.29.refs_0_ = bf16[24,7168]{1,0:T(8,128)(2,1)S(1)} collective-permute-done((bf16[24,7168]{1,0:T(8,128)(2,1)S(1)}, bf16[24,7168]{1,0:T(8,128)(2,1)S(1)}, u32[]{:S(2)}, u32[]{:S(2)}) %collective-permute-start.29) | collective-permute-done | bytes 344096 | tf_op jit(solution)/shard_map/ppermute | solution.py:21
  137.8 3.2 %shard_map.130 = bf16[24,7168]{1,0:T(8,128)(2,1)S(1)} custom-call(bf16[24,7168]{1,0:T(8,128)(2,1)S(1)} %collective-permute-done.29.refs_0_, f32[24,128]{1,0:T(8,128)S(1)} %get-tuple-element.60.refs_1_, f32[24,128]{1,0:T(8,128)S(1)} %get-tuple-element.61.refs_2_, bf16[7168,128]{1,0:T(8,128)(2,1)S(1)} %bitcast.15, bf16[7168,128]{1,0:T(8,128)(2,1)S(1)} %bitcast.20, ...), custom_call_target="tpu_custom_call" | custom-call | tf_op jit(solution)/shard_map/pallas_call | solution.py:25
  141.3 2.6 %shard_map.125 = bf16[24,7168]{1,0:T(8,128)(2,1)S(1)} custom-call(bf16[24,7168]{1,0:T(8,128)(2,1)S(1)} %collective-permute-done.8.refs_0_, bf16[7168,128]{1,0:T(8,128)(2,1)S(1)} %bitcast.16, bf16[7168,128]{1,0:T(8,128)(2,1)S(1)} %bitcast.21, bf16[128,7168]{1,0:T(8,128)(2,1)S(1)} %bitcast.25), custom_call_target="tpu_custom_call" | custom-call | tf_op jit(solution)/shard_map/pallas_call | solution.py:25
  143.9 3.3 %collective-permute-start.9 = (bf16[24,7168]{1,0:T(8,128)(2,1)S(1)}, bf16[24,7168]{1,0:T(8,128)(2,1)S(1)}, u32[]{:S(2)}, u32[]{:S(2)}) collective-permute-start(bf16[24,7168]{1,0:T(8,128)(2,1)S(1)} %shard_map.125), channel_id=1, source_target_pairs={{0,7},{1,0},{2,1},{3,2},{4,3},{5,4},{6,5},{7,6},{8,15},{9,8},{10,9... | collective-permute-start | bytes 1032200 | tf_op jit(solution)/shard_map/ppermute | solution.py:21
  147.2 2.3 %collective-permute-start.36 = (bf16[24,7168]{1,0:T(8,128)(2,1)S(1)}, bf16[24,7168]{1,0:T(8,128)(2,1)S(1)}, u32[]{:S(2)}, u32[]{:S(2)}) collective-permute-start(bf16[24,7168]{1,0:T(8,128)(2,1)S(1)} %add_convert_fusion), channel_id=1, source_target_pairs={{0,7},{1,0},{2,1},{3,2},{4,3},{5,4},{6,5},{7,6},{8,15},{9,8},{10,9... | collective-permute-start | bytes 1032200 | tf_op jit(solution)/shard_map/ppermute | solution.py:21
  149.5 3.7 %collective-permute-done.30 = bf16[24,7168]{1,0:T(8,128)(2,1)S(1)} collective-permute-done((bf16[24,7168]{1,0:T(8,128)(2,1)S(1)}, bf16[24,7168]{1,0:T(8,128)(2,1)S(1)}, u32[]{:S(2)}, u32[]{:S(2)}) %collective-permute-start.30) | collective-permute-done | bytes 344096 | tf_op jit(solution)/shard_map/ppermute | solution.py:21
  153.4 7.2 %collective-permute-done.14 = bf16[24,7168]{1,0:T(8,128)(2,1)S(1)} collective-permute-done((bf16[24,7168]{1,0:T(8,128)(2,1)S(1)}, bf16[24,7168]{1,0:T(8,128)(2,1)S(1)}, u32[]{:S(2)}, u32[]{:S(2)}) %collective-permute-start.14) | collective-permute-done | bytes 344096 | tf_op jit(solution)/shard_map/ppermute | solution.py:21
  160.9 3.3 %collective-permute-start.10 = (bf16[24,7168]{1,0:T(8,128)(2,1)S(1)}, bf16[24,7168]{1,0:T(8,128)(2,1)S(1)}, u32[]{:S(2)}, u32[]{:S(2)}) collective-permute-start(bf16[24,7168]{1,0:T(8,128)(2,1)S(1)} %add_convert_fusion.9), channel_id=1, source_target_pairs={{0,7},{1,0},{2,1},{3,2},{4,3},{5,4},{6,5},{7,6},{8,15},{9,8},{10,9... | collective-permute-start | bytes 1032200 | tf_op jit(solution)/shard_map/ppermute | solution.py:21
  164.2 3.8 %collective-permute-done.31 = bf16[24,7168]{1,0:T(8,128)(2,1)S(1)} collective-permute-done((bf16[24,7168]{1,0:T(8,128)(2,1)S(1)}, bf16[24,7168]{1,0:T(8,128)(2,1)S(1)}, u32[]{:S(2)}, u32[]{:S(2)}) %collective-permute-start.31) | collective-permute-done | bytes 344096 | tf_op jit(solution)/shard_map/ppermute | solution.py:21
  168.2 3.3 %collective-permute-done.10 = bf16[24,7168]{1,0:T(8,128)(2,1)S(1)} collective-permute-done((bf16[24,7168]{1,0:T(8,128)(2,1)S(1)}, bf16[24,7168]{1,0:T(8,128)(2,1)S(1)}, u32[]{:S(2)}, u32[]{:S(2)}) %collective-permute-start.10) | collective-permute-done | bytes 344096 | tf_op jit(solution)/shard_map/ppermute | solution.py:21
  171.6 3.8 %collective-permute-start.11 = (bf16[24,7168]{1,0:T(8,128)(2,1)S(1)}, bf16[24,7168]{1,0:T(8,128)(2,1)S(1)}, u32[]{:S(2)}, u32[]{:S(2)}) collective-permute-start(bf16[24,7168]{1,0:T(8,128)(2,1)S(1)} %add_convert_fusion.8), channel_id=1, source_target_pairs={{0,7},{1,0},{2,1},{3,2},{4,3},{5,4},{6,5},{7,6},{8,15},{9,8},{10,9... | collective-permute-start | bytes 1032200 | tf_op jit(solution)/shard_map/ppermute | solution.py:21
  175.3 3.3 %collective-permute-done.32 = bf16[24,7168]{1,0:T(8,128)(2,1)S(1)} collective-permute-done((bf16[24,7168]{1,0:T(8,128)(2,1)S(1)}, bf16[24,7168]{1,0:T(8,128)(2,1)S(1)}, u32[]{:S(2)}, u32[]{:S(2)}) %collective-permute-start.32) | collective-permute-done | bytes 344096 | tf_op jit(solution)/shard_map/ppermute | solution.py:21
  178.8 3.3 %collective-permute-done.11 = bf16[24,7168]{1,0:T(8,128)(2,1)S(1)} collective-permute-done((bf16[24,7168]{1,0:T(8,128)(2,1)S(1)}, bf16[24,7168]{1,0:T(8,128)(2,1)S(1)}, u32[]{:S(2)}, u32[]{:S(2)}) %collective-permute-start.11) | collective-permute-done | bytes 344096 | tf_op jit(solution)/shard_map/ppermute | solution.py:21
  182.2 3.8 %collective-permute-start.12 = (bf16[24,7168]{1,0:T(8,128)(2,1)S(1)}, bf16[24,7168]{1,0:T(8,128)(2,1)S(1)}, u32[]{:S(2)}, u32[]{:S(2)}) collective-permute-start(bf16[24,7168]{1,0:T(8,128)(2,1)S(1)} %add_convert_fusion.7), channel_id=1, source_target_pairs={{0,7},{1,0},{2,1},{3,2},{4,3},{5,4},{6,5},{7,6},{8,15},{9,8},{10,9... | collective-permute-start | bytes 1032200 | tf_op jit(solution)/shard_map/ppermute | solution.py:21
  185.9 1.3 collective-permute-done.33.refs_4_
  187.2 3.5 %collective-permute-done.12.refs_1_ = bf16[24,7168]{1,0:T(8,128)(2,1)S(1)} collective-permute-done((bf16[24,7168]{1,0:T(8,128)(2,1)S(1)}, bf16[24,7168]{1,0:T(8,128)(2,1)S(1)}, u32[]{:S(2)}, u32[]{:S(2)}) %collective-permute-start.12) | collective-permute-done | bytes 344096 | tf_op jit(solution)/shard_map/ppermute | solution.py:21
  191.3 17.8 %all_to_all.16.back_ref = bf16[8,3,14336]{2,1,0:T(4,128)(2,1)S(1)} all-to-all(bf16[8,3,14336]{2,1,0:T(4,128)(2,1)S(1)} %shard_map.131), channel_id=1, replica_groups=mesh['pp'=4,'e'=8,'k'=8] {'e'}, dimensions={0} | all-to-all | bytes 1376256 | tf_op jit(solution)/shard_map/all_to_all | solution.py:315
  209.1 4.2 %shard_map.132 = (bf16[64,7168]{1,0:T(8,128)(2,1)}, bf16[64,7168]{1,0:T(8,128)(2,1)}) custom-call(bf16[8,3,14336]{2,1,0:T(4,128)(2,1)S(1)} %all_to_all.16.back_ref, bf16[64,7168]{1,0:T(8,128)(2,1)S(1)} %copy-done.8, s32[1,64]{1,0:T(1,128)S(1)} %bitcast.32, f32[1,64]{1,0:T(1,128)S(1)} %bitcast.34, bf16[64,7168]{1,0:T(8,128)(2,1)S(1)} %bitcast.27, ...), custom_call_target="tpu_custom_call" | custom-call | tf_op jit(solution)/shard_map/pallas_call | solution.py:363
  (87 shorter events, 7.4 us)
Async XLA Ops:
  0.6 32.5 %copy-start.15 = (s32[1,64,1]{1,2,0:T(1,128)S(1)}, s32[1,64,1]{1,2,0:T(1,128)}, u32[]{:S(2)}) copy-start(s32[1,64,1]{1,2,0:T(1,128)} %param.12) | copy-start | bytes 772
  0.6 32.5 %copy-start.16 = (f32[1,64,1]{1,2,0:T(1,128)S(1)}, f32[1,64,1]{1,2,0:T(1,128)}, u32[]{:S(2)}) copy-start(f32[1,64,1]{1,2,0:T(1,128)} %param.17) | copy-start | bytes 772
  0.7 32.5 %collective-permute-start = (bf16[64,7168]{1,0:T(8,128)(2,1)}, bf16[64,7168]{1,0:T(8,128)(2,1)S(1)}, u32[]{:S(2)}, u32[]{:S(2)}) collective-permute-start(bf16[64,7168]{1,0:T(8,128)(2,1)} %bitcast.35), channel_id=1, source_target_pairs={{0,64},{64,128},{128,192},{192,0},{1,65},{65,129},{129,193},{193,1... | collective-permute-start | bytes 2752520 | tf_op jit(solution)/shard_map/ppermute | solution.py:21
  0.7 32.4 %collective-permute-start.1 = (bf16[64,7168]{1,0:T(8,128)(2,1)}, bf16[64,7168]{1,0:T(8,128)(2,1)S(1)}, u32[]{:S(2)}, u32[]{:S(2)}) collective-permute-start(bf16[64,7168]{1,0:T(8,128)(2,1)} %bitcast.36), channel_id=1, source_target_pairs={{0,192},{64,0},{128,64},{192,128},{1,193},{65,1},{129,65},{193,129... | collective-permute-start | bytes 2752520 | tf_op jit(solution)/shard_map/ppermute | solution.py:21
  31.2 17.3 %collective-permute-start.23 = (bf16[24,7168]{1,0:T(8,128)(2,1)S(1)}, bf16[24,7168]{1,0:T(8,128)(2,1)S(1)}, u32[]{:S(2)}, u32[]{:S(2)}) collective-permute-start(bf16[24,7168]{1,0:T(8,128)(2,1)S(1)} %shard_map.127.refs_0_), channel_id=1, source_target_pairs={{0,1},{1,2},{2,3},{3,4},{4,5},{5,6},{6,7},{7,0},{8,9},{9,10},{10,1... | collective-permute-start | bytes 1032200 | tf_op jit(solution)/shard_map/ppermute | solution.py:21
  39.4 60.9 %copy-start = (bf16[1,1,7168,128]{3,2,1,0:T(8,128)(2,1)S(1)}, bf16[1,1,7168,128]{3,2,1,0:T(8,128)(2,1)}, u32[]{:S(2)}) copy-start(bf16[1,1,7168,128]{3,2,1,0:T(8,128)(2,1)} %param.19) | copy-start | bytes 5505028
  39.4 19.0 %all-to-all-start = ((bf16[8,3,14336]{2,1,0:T(4,128)(2,1)}), bf16[8,3,14336]{2,1,0:T(4,128)(2,1)S(1)}, u32[]{:S(2)}, u32[]{:S(2)}) async-start(bf16[8,3,14336]{2,1,0:T(4,128)(2,1)} %copy-done.4), calls=%async_computation | async-start | bytes 1835008 | tf_op jit(solution)/shard_map/all_to_all | solution.py:315
  44.5 10.2 %collective-permute-start.22 = (bf16[24,7168]{1,0:T(8,128)(2,1)S(1)}, bf16[24,7168]{1,0:T(8,128)(2,1)}, u32[]{:S(2)}, u32[]{:S(2)}) collective-permute-start(bf16[24,7168]{1,0:T(8,128)(2,1)S(1)} %shard_map.127.refs_0_), channel_id=1, source_target_pairs={{0,7},{1,0},{2,1},{3,2},{4,3},{5,4},{6,5},{7,6},{8,15},{9,8},{10,9... | collective-permute-start | bytes 1032200 | tf_op jit(solution)/shard_map/ppermute | solution.py:21
  48.4 10.0 %collective-permute-start.25 = (bf16[24,7168]{1,0:T(8,128)(2,1)S(1)}, bf16[24,7168]{1,0:T(8,128)(2,1)}, u32[]{:S(2)}, u32[]{:S(2)}) collective-permute-start(bf16[24,7168]{1,0:T(8,128)(2,1)S(1)} %collective-permute-done.23.refs_2_), channel_id=1, source_target_pairs={{0,1},{1,2},{2,3},{3,4},{4,5},{5,6},{6,7},{7,0},{8,9},{9,10},{10,1... | collective-permute-start | bytes 1032200 | tf_op jit(solution)/shard_map/ppermute | solution.py:21
  54.6 12.6 %collective-permute-start.24 = (bf16[24,7168]{1,0:T(8,128)(2,1)}, bf16[24,7168]{1,0:T(8,128)(2,1)}, u32[]{:S(2)}, u32[]{:S(2)}) collective-permute-start(bf16[24,7168]{1,0:T(8,128)(2,1)} %collective-permute-done.22.refs_1_), channel_id=1, source_target_pairs={{0,7},{1,0},{2,1},{3,2},{4,3},{5,4},{6,5},{7,6},{8,15},{9,8},{10,9... | collective-permute-start | bytes 1032200 | tf_op jit(solution)/shard_map/ppermute | solution.py:21
  58.4 12.6 %collective-permute-start.27 = (bf16[24,7168]{1,0:T(8,128)(2,1)}, bf16[24,7168]{1,0:T(8,128)(2,1)}, u32[]{:S(2)}, u32[]{:S(2)}) collective-permute-start(bf16[24,7168]{1,0:T(8,128)(2,1)} %collective-permute-done.25.refs_4_), channel_id=1, source_target_pairs={{0,1},{1,2},{2,3},{3,4},{4,5},{5,6},{6,7},{7,0},{8,9},{9,10},{10,1... | collective-permute-start | bytes 1032200 | tf_op jit(solution)/shard_map/ppermute | solution.py:21
  58.9 19.4 %collective-permute-start.17 = (bf16[24,7168]{1,0:T(8,128)(2,1)S(1)}, bf16[24,7168]{1,0:T(8,128)(2,1)S(1)}, u32[]{:S(2)}, u32[]{:S(2)}) collective-permute-start(bf16[24,7168]{1,0:T(8,128)(2,1)S(1)} %get-tuple-element.44.refs_0_), channel_id=1, source_target_pairs={{0,1},{1,2},{2,3},{3,4},{4,5},{5,6},{6,7},{7,0},{8,9},{9,10},{10,1... | collective-permute-start | bytes 1032200 | tf_op jit(solution)/shard_map/ppermute | solution.py:21
  59.4 18.9 %collective-permute-start.16 = (bf16[24,7168]{1,0:T(8,128)(2,1)S(1)}, bf16[24,7168]{1,0:T(8,128)(2,1)S(1)}, u32[]{:S(2)}, u32[]{:S(2)}) collective-permute-start(bf16[24,7168]{1,0:T(8,128)(2,1)S(1)} %get-tuple-element.44.refs_0_), channel_id=1, source_target_pairs={{0,7},{1,0},{2,1},{3,2},{4,3},{5,4},{6,5},{7,6},{8,15},{9,8},{10,9... | collective-permute-start | bytes 1032200 | tf_op jit(solution)/shard_map/ppermute | solution.py:21
  67.3 14.7 %collective-permute-start.26 = (bf16[24,7168]{1,0:T(8,128)(2,1)}, bf16[24,7168]{1,0:T(8,128)(2,1)S(1)}, u32[]{:S(2)}, u32[]{:S(2)}) collective-permute-start(bf16[24,7168]{1,0:T(8,128)(2,1)} %collective-permute-done.24.refs_3_), channel_id=1, source_target_pairs={{0,7},{1,0},{2,1},{3,2},{4,3},{5,4},{6,5},{7,6},{8,15},{9,8},{10,9... | collective-permute-start | bytes 1032200 | tf_op jit(solution)/shard_map/ppermute | solution.py:21
  71.0 18.3 %collective-permute-start.2 = (bf16[24,7168]{1,0:T(8,128)(2,1)S(1)}, bf16[24,7168]{1,0:T(8,128)(2,1)S(1)}, u32[]{:S(2)}, u32[]{:S(2)}) collective-permute-start(bf16[24,7168]{1,0:T(8,128)(2,1)S(1)} %get-tuple-element.36.refs_0_), channel_id=1, source_target_pairs={{0,7},{1,0},{2,1},{3,2},{4,3},{5,4},{6,5},{7,6},{8,15},{9,8},{10,9... | collective-permute-start | bytes 1032200 | tf_op jit(solution)/shard_map/ppermute | solution.py:21
  71.0 22.0 %collective-permute-start.3 = (bf16[24,7168]{1,0:T(8,128)(2,1)S(1)}, bf16[24,7168]{1,0:T(8,128)(2,1)S(1)}, u32[]{:S(2)}, u32[]{:S(2)}) collective-permute-start(bf16[24,7168]{1,0:T(8,128)(2,1)S(1)} %get-tuple-element.36.refs_0_), channel_id=1, source_target_pairs={{0,1},{1,2},{2,3},{3,4},{4,5},{5,6},{6,7},{7,0},{8,9},{9,10},{10,1... | collective-permute-start | bytes 1032200 | tf_op jit(solution)/shard_map/ppermute | solution.py:21
  78.2 14.8 %collective-permute-start.19 = (bf16[24,7168]{1,0:T(8,128)(2,1)S(1)}, bf16[24,7168]{1,0:T(8,128)(2,1)S(1)}, u32[]{:S(2)}, u32[]{:S(2)}) collective-permute-start(bf16[24,7168]{1,0:T(8,128)(2,1)S(1)} %collective-permute-done.17.refs_2_), channel_id=1, source_target_pairs={{0,1},{1,2},{2,3},{3,4},{4,5},{5,6},{6,7},{7,0},{8,9},{9,10},{10,1... | collective-permute-start | bytes 1032200 | tf_op jit(solution)/shard_map/ppermute | solution.py:21
  78.2 18.4 %collective-permute-start.18 = (bf16[24,7168]{1,0:T(8,128)(2,1)S(1)}, bf16[24,7168]{1,0:T(8,128)(2,1)S(1)}, u32[]{:S(2)}, u32[]{:S(2)}) collective-permute-start(bf16[24,7168]{1,0:T(8,128)(2,1)S(1)} %collective-permute-done.16.refs_1_), channel_id=1, source_target_pairs={{0,7},{1,0},{2,1},{3,2},{4,3},{5,4},{6,5},{7,6},{8,15},{9,8},{10,9... | collective-permute-start | bytes 1032200 | tf_op jit(solution)/shard_map/ppermute | solution.py:21
  82.0 18.3 %collective-permute-start.28 = (bf16[24,7168]{1,0:T(8,128)(2,1)}, bf16[24,7168]{1,0:T(8,128)(2,1)S(1)}, u32[]{:S(2)}, u32[]{:S(2)}) collective-permute-start(bf16[24,7168]{1,0:T(8,128)(2,1)} %collective-permute-done.27.refs_6_), channel_id=1, source_target_pairs={{0,1},{1,2},{2,3},{3,4},{4,5},{5,6},{6,7},{7,0},{8,9},{9,10},{10,1... | collective-permute-start | bytes 1032200 | tf_op jit(solution)/shard_map/ppermute | solution.py:21
  89.3 16.0 %collective-permute-start.4 = (bf16[24,7168]{1,0:T(8,128)(2,1)S(1)}, bf16[24,7168]{1,0:T(8,128)(2,1)S(1)}, u32[]{:S(2)}, u32[]{:S(2)}) collective-permute-start(bf16[24,7168]{1,0:T(8,128)(2,1)S(1)} %collective-permute-done.2.refs_1_), channel_id=1, source_target_pairs={{0,7},{1,0},{2,1},{3,2},{4,3},{5,4},{6,5},{7,6},{8,15},{9,8},{10,9... | collective-permute-start | bytes 1032200 | tf_op jit(solution)/shard_map/ppermute | solution.py:21
  93.0 14.7 %collective-permute-start.5 = (bf16[24,7168]{1,0:T(8,128)(2,1)S(1)}, bf16[24,7168]{1,0:T(8,128)(2,1)S(1)}, u32[]{:S(2)}, u32[]{:S(2)}) collective-permute-start(bf16[24,7168]{1,0:T(8,128)(2,1)S(1)} %collective-permute-done.3.refs_2_), channel_id=1, source_target_pairs={{0,1},{1,2},{2,3},{3,4},{4,5},{5,6},{6,7},{7,0},{8,9},{9,10},{10,1... | collective-permute-start | bytes 1032200 | tf_op jit(solution)/shard_map/ppermute | solution.py:21
  93.0 22.1 %collective-permute-start.21 = (bf16[24,7168]{1,0:T(8,128)(2,1)S(1)}, bf16[24,7168]{1,0:T(8,128)(2,1)S(1)}, u32[]{:S(2)}, u32[]{:S(2)}) collective-permute-start(bf16[24,7168]{1,0:T(8,128)(2,1)S(1)} %collective-permute-done.19.refs_4_), channel_id=1, source_target_pairs={{0,1},{1,2},{2,3},{3,4},{4,5},{5,6},{6,7},{7,0},{8,9},{9,10},{10,1... | collective-permute-start | bytes 1032200 | tf_op jit(solution)/shard_map/ppermute | solution.py:21
  96.7 18.4 %collective-permute-start.20 = (bf16[24,7168]{1,0:T(8,128)(2,1)S(1)}, bf16[24,7168]{1,0:T(8,128)(2,1)S(1)}, u32[]{:S(2)}, u32[]{:S(2)}) collective-permute-start(bf16[24,7168]{1,0:T(8,128)(2,1)S(1)} %collective-permute-done.18.refs_3_), channel_id=1, source_target_pairs={{0,7},{1,0},{2,1},{3,2},{4,3},{5,4},{6,5},{7,6},{8,15},{9,8},{10,9... | collective-permute-start | bytes 1032200 | tf_op jit(solution)/shard_map/ppermute | solution.py:21
  101.9 13.2 %copy-start.3 = (bf16[1,1,128,7168]{3,2,1,0:T(8,128)(2,1)S(1)}, bf16[1,1,128,7168]{3,2,1,0:T(8,128)(2,1)}, u32[]{:S(2)}) copy-start(bf16[1,1,128,7168]{3,2,1,0:T(8,128)(2,1)} %param.21) | copy-start | bytes 5505028
  105.3 14.0 %collective-permute-start.6 = (bf16[24,7168]{1,0:T(8,128)(2,1)S(1)}, bf16[24,7168]{1,0:T(8,128)(2,1)S(1)}, u32[]{:S(2)}, u32[]{:S(2)}) collective-permute-start(bf16[24,7168]{1,0:T(8,128)(2,1)S(1)} %collective-permute-done.4.refs_3_), channel_id=1, source_target_pairs={{0,7},{1,0},{2,1},{3,2},{4,3},{5,4},{6,5},{7,6},{8,15},{9,8},{10,9... | collective-permute-start | bytes 1032200 | tf_op jit(solution)/shard_map/ppermute | solution.py:21
  107.7 11.6 %collective-permute-start.7 = (bf16[24,7168]{1,0:T(8,128)(2,1)S(1)}, bf16[24,7168]{1,0:T(8,128)(2,1)S(1)}, u32[]{:S(2)}, u32[]{:S(2)}) collective-permute-start(bf16[24,7168]{1,0:T(8,128)(2,1)S(1)} %collective-permute-done.5.refs_4_), channel_id=1, source_target_pairs={{0,1},{1,2},{2,3},{3,4},{4,5},{5,6},{6,7},{7,0},{8,9},{9,10},{10,1... | collective-permute-start | bytes 1032200 | tf_op jit(solution)/shard_map/ppermute | solution.py:21
  119.2 11.0 %collective-permute-start.34 = (bf16[24,7168]{1,0:T(8,128)(2,1)S(1)}, bf16[24,7168]{1,0:T(8,128)(2,1)S(1)}, u32[]{:S(2)}, u32[]{:S(2)}) collective-permute-start(bf16[24,7168]{1,0:T(8,128)(2,1)S(1)} %get-tuple-element.65), channel_id=1, source_target_pairs={{0,7},{1,0},{2,1},{3,2},{4,3},{5,4},{6,5},{7,6},{8,15},{9,8},{10,9... | collective-permute-start | bytes 1032200 | tf_op jit(solution)/shard_map/ppermute | solution.py:21
  123.0 18.1 %collective-permute-start.13 = (bf16[24,7168]{1,0:T(8,128)(2,1)S(1)}, bf16[24,7168]{1,0:T(8,128)(2,1)S(1)}, u32[]{:S(2)}, u32[]{:S(2)}) collective-permute-start(bf16[24,7168]{1,0:T(8,128)(2,1)S(1)} %get-tuple-element.41), channel_id=1, source_target_pairs={{0,1},{1,2},{2,3},{3,4},{4,5},{5,6},{6,7},{7,0},{8,9},{9,10},{10,1... | collective-permute-start | bytes 1032200 | tf_op jit(solution)/shard_map/ppermute | solution.py:21
  125.0 12.7 %collective-permute-start.29 = (bf16[24,7168]{1,0:T(8,128)(2,1)S(1)}, bf16[24,7168]{1,0:T(8,128)(2,1)S(1)}, u32[]{:S(2)}, u32[]{:S(2)}) collective-permute-start(bf16[24,7168]{1,0:T(8,128)(2,1)S(1)} %collective-permute-done.21.refs_6_), channel_id=1, source_target_pairs={{0,1},{1,2},{2,3},{3,4},{4,5},{5,6},{6,7},{7,0},{8,9},{9,10},{10,1... | collective-permute-start | bytes 1032200 | tf_op jit(solution)/shard_map/ppermute | solution.py:21
  125.1 16.1 %collective-permute-start.8 = (bf16[24,7168]{1,0:T(8,128)(2,1)S(1)}, bf16[24,7168]{1,0:T(8,128)(2,1)S(1)}, u32[]{:S(2)}, u32[]{:S(2)}) collective-permute-start(bf16[24,7168]{1,0:T(8,128)(2,1)S(1)} %collective-permute-done.6.refs_5_), channel_id=1, source_target_pairs={{0,7},{1,0},{2,1},{3,2},{4,3},{5,4},{6,5},{7,6},{8,15},{9,8},{10,9... | collective-permute-start | bytes 1032200 | tf_op jit(solution)/shard_map/ppermute | solution.py:21
  130.3 16.8 %collective-permute-start.35 = (bf16[24,7168]{1,0:T(8,128)(2,1)S(1)}, bf16[24,7168]{1,0:T(8,128)(2,1)S(1)}, u32[]{:S(2)}, u32[]{:S(2)}) collective-permute-start(bf16[24,7168]{1,0:T(8,128)(2,1)S(1)} %add_convert_fusion.1), channel_id=1, source_target_pairs={{0,7},{1,0},{2,1},{3,2},{4,3},{5,4},{6,5},{7,6},{8,15},{9,8},{10,9... | collective-permute-start | bytes 1032200 | tf_op jit(solution)/shard_map/ppermute | solution.py:21
  141.0 12.2 %collective-permute-start.30 = (bf16[24,7168]{1,0:T(8,128)(2,1)S(1)}, bf16[24,7168]{1,0:T(8,128)(2,1)S(1)}, u32[]{:S(2)}, u32[]{:S(2)}) collective-permute-start(bf16[24,7168]{1,0:T(8,128)(2,1)S(1)} %shard_map.130), channel_id=1, source_target_pairs={{0,1},{1,2},{2,3},{3,4},{4,5},{5,6},{6,7},{7,0},{8,9},{9,10},{10,1... | collective-permute-start | bytes 1032200 | tf_op jit(solution)/shard_map/ppermute | solution.py:21
  141.2 19.5 %collective-permute-start.14 = (bf16[24,7168]{1,0:T(8,128)(2,1)S(1)}, bf16[24,7168]{1,0:T(8,128)(2,1)S(1)}, u32[]{:S(2)}, u32[]{:S(2)}) collective-permute-start(bf16[24,7168]{1,0:T(8,128)(2,1)S(1)} %add_convert_fusion.6), channel_id=1, source_target_pairs={{0,1},{1,2},{2,3},{3,4},{4,5},{5,6},{6,7},{7,0},{8,9},{9,10},{10,1... | collective-permute-start | bytes 1032200 | tf_op jit(solution)/shard_map/ppermute | solution.py:21
  143.9 17.0 %collective-permute-start.9 = (bf16[24,7168]{1,0:T(8,128)(2,1)S(1)}, bf16[24,7168]{1,0:T(8,128)(2,1)S(1)}, u32[]{:S(2)}, u32[]{:S(2)}) collective-permute-start(bf16[24,7168]{1,0:T(8,128)(2,1)S(1)} %shard_map.125), channel_id=1, source_target_pairs={{0,7},{1,0},{2,1},{3,2},{4,3},{5,4},{6,5},{7,6},{8,15},{9,8},{10,9... | collective-permute-start | bytes 1032200 | tf_op jit(solution)/shard_map/ppermute | solution.py:21
  147.2 38.7 %collective-permute-start.36 = (bf16[24,7168]{1,0:T(8,128)(2,1)S(1)}, bf16[24,7168]{1,0:T(8,128)(2,1)S(1)}, u32[]{:S(2)}, u32[]{:S(2)}) collective-permute-start(bf16[24,7168]{1,0:T(8,128)(2,1)S(1)} %add_convert_fusion), channel_id=1, source_target_pairs={{0,7},{1,0},{2,1},{3,2},{4,3},{5,4},{6,5},{7,6},{8,15},{9,8},{10,9... | collective-permute-start | bytes 1032200 | tf_op jit(solution)/shard_map/ppermute | solution.py:21
  153.4 14.7 %collective-permute-start.31 = (bf16[24,7168]{1,0:T(8,128)(2,1)S(1)}, bf16[24,7168]{1,0:T(8,128)(2,1)S(1)}, u32[]{:S(2)}, u32[]{:S(2)}) collective-permute-start(bf16[24,7168]{1,0:T(8,128)(2,1)S(1)} %add_convert_fusion.4), channel_id=1, source_target_pairs={{0,1},{1,2},{2,3},{3,4},{4,5},{5,6},{6,7},{7,0},{8,9},{9,10},{10,1... | collective-permute-start | bytes 1032200 | tf_op jit(solution)/shard_map/ppermute | solution.py:21
  160.7 25.2 %collective-permute-start.15 = (bf16[24,7168]{1,0:T(8,128)(2,1)S(1)}, bf16[24,7168]{1,0:T(8,128)(2,1)S(1)}, u32[]{:S(2)}, u32[]{:S(2)}) collective-permute-start(bf16[24,7168]{1,0:T(8,128)(2,1)S(1)} %add_convert_fusion.5), channel_id=1, source_target_pairs={{0,1},{1,2},{2,3},{3,4},{4,5},{5,6},{6,7},{7,0},{8,9},{9,10},{10,1... | collective-permute-start | bytes 1032200 | tf_op jit(solution)/shard_map/ppermute | solution.py:21
  160.9 10.6 %collective-permute-start.10 = (bf16[24,7168]{1,0:T(8,128)(2,1)S(1)}, bf16[24,7168]{1,0:T(8,128)(2,1)S(1)}, u32[]{:S(2)}, u32[]{:S(2)}) collective-permute-start(bf16[24,7168]{1,0:T(8,128)(2,1)S(1)} %add_convert_fusion.9), channel_id=1, source_target_pairs={{0,7},{1,0},{2,1},{3,2},{4,3},{5,4},{6,5},{7,6},{8,15},{9,8},{10,9... | collective-permute-start | bytes 1032200 | tf_op jit(solution)/shard_map/ppermute | solution.py:21
  168.1 10.5 %collective-permute-start.32 = (bf16[24,7168]{1,0:T(8,128)(2,1)S(1)}, bf16[24,7168]{1,0:T(8,128)(2,1)S(1)}, u32[]{:S(2)}, u32[]{:S(2)}) collective-permute-start(bf16[24,7168]{1,0:T(8,128)(2,1)S(1)} %add_convert_fusion.3), channel_id=1, source_target_pairs={{0,1},{1,2},{2,3},{3,4},{4,5},{5,6},{6,7},{7,0},{8,9},{9,10},{10,1... | collective-permute-start | bytes 1032200 | tf_op jit(solution)/shard_map/ppermute | solution.py:21
  171.6 10.5 %collective-permute-start.11 = (bf16[24,7168]{1,0:T(8,128)(2,1)S(1)}, bf16[24,7168]{1,0:T(8,128)(2,1)S(1)}, u32[]{:S(2)}, u32[]{:S(2)}) collective-permute-start(bf16[24,7168]{1,0:T(8,128)(2,1)S(1)} %add_convert_fusion.8), channel_id=1, source_target_pairs={{0,7},{1,0},{2,1},{3,2},{4,3},{5,4},{6,5},{7,6},{8,15},{9,8},{10,9... | collective-permute-start | bytes 1032200 | tf_op jit(solution)/shard_map/ppermute | solution.py:21
  178.7 8.5 %collective-permute-start.33 = (bf16[24,7168]{1,0:T(8,128)(2,1)S(1)}, bf16[24,7168]{1,0:T(8,128)(2,1)S(1)}, u32[]{:S(2)}, u32[]{:S(2)}) collective-permute-start(bf16[24,7168]{1,0:T(8,128)(2,1)S(1)} %add_convert_fusion.2), channel_id=1, source_target_pairs={{0,1},{1,2},{2,3},{3,4},{4,5},{5,6},{6,7},{7,0},{8,9},{9,10},{10,1... | collective-permute-start | bytes 1032200 | tf_op jit(solution)/shard_map/ppermute | solution.py:21
  182.2 8.5 %collective-permute-start.12 = (bf16[24,7168]{1,0:T(8,128)(2,1)S(1)}, bf16[24,7168]{1,0:T(8,128)(2,1)S(1)}, u32[]{:S(2)}, u32[]{:S(2)}) collective-permute-start(bf16[24,7168]{1,0:T(8,128)(2,1)S(1)} %add_convert_fusion.7), channel_id=1, source_target_pairs={{0,7},{1,0},{2,1},{3,2},{4,3},{5,4},{6,5},{7,6},{8,15},{9,8},{10,9... | collective-permute-start | bytes 1032200 | tf_op jit(solution)/shard_map/ppermute | solution.py:21
  190.7 18.4 %copy-start.6 = (bf16[1,64,7168]{2,1,0:T(8,128)(2,1)S(1)}, bf16[1,64,7168]{2,1,0:T(8,128)(2,1)}, u32[]{:S(2)}) copy-start(bf16[1,64,7168]{2,1,0:T(8,128)(2,1)} %param.14) | copy-start | bytes 2752516
  190.7 18.4 %copy-start.8 = (bf16[64,7168]{1,0:T(8,128)(2,1)S(1)}, bf16[64,7168]{1,0:T(8,128)(2,1)}, u32[]{:S(2)}) copy-start(bf16[64,7168]{1,0:T(8,128)(2,1)} %copy-done.7) | copy-start | bytes 2752516
  190.7 18.4 %copy-start.10 = (bf16[64,7168]{1,0:T(8,128)(2,1)S(1)}, bf16[64,7168]{1,0:T(8,128)(2,1)}, u32[]{:S(2)}) copy-start(bf16[64,7168]{1,0:T(8,128)(2,1)} %copy-done.9) | copy-start | bytes 2752516
  190.7 18.4 %copy-start.12 = (f32[1,7168]{1,0:T(1,128)S(1)}, f32[1,7168]{1,0:T(1,128)}, u32[]{:S(2)}) copy-start(f32[1,7168]{1,0:T(1,128)} %gain_ref.5) | copy-start | bytes 86020
  190.7 18.4 %copy-start.14 = (s32[1,64,1]{1,2,0:T(1,128)S(1)}, s32[1,64,1]{1,2,0:T(1,128)}, u32[]{:S(2)}) copy-start(s32[1,64,1]{1,2,0:T(1,128)} %param.16) | copy-start | bytes 772
  190.7 18.4 %copy-start.17 = (f32[1,64,1]{1,2,0:T(1,128)S(1)}, f32[1,64,1]{1,2,0:T(1,128)}, u32[]{:S(2)}) copy-start(f32[1,64,1]{1,2,0:T(1,128)} %param.13) | copy-start | bytes 772
  (8 other events, 20.1 us)
where the time goes:
time: 216 us; the launch traced here: 213 us
  waiting for transfers between devices  73.9 us (34%)
  starting transfers between devices  61.2 us (28%)
  blocking collectives  41.5 us (19%)
  Pallas kernels  27.9 us (13%)
  local copies, waits for them, and re-layouts  6.92 us (3%)
    ppermute x37, waiting for transfers between devices, shifted(): return lax.ppermute(block, axis, route)  73.9 us
    ppermute x37, starting transfers between devices, shifted(): return lax.ppermute(block, axis, route)  56.2 us
    all_to_all x2, blocking collectives, exchange(): return lax.all_to_all(slots, 'e', split_axis=0, concat_axis=0, tiled=True)  41.5 us
    pallas_call x10, Pallas kernels, call(): pl.pallas_call(kernel, out_shape=outs, in_specs=[pl.BlockSpec(memory_spac...  23.7 us
    unnamed x36, local copies, waits for them, and re-layouts  6.92 us
    all_to_all x1, starting transfers between devices, exchange(): return lax.all_to_all(slots, 'e', split_axis=0, concat_axis=0, tiled=True)  5.03 us
  transfers between devices with their start and end apart: 38, of which 17 were waited for; matrix products, arithmetic and copies ran while one was open for 0% of the time, Pallas kernels for 11%

commit v1 on v0

--- a/solution.py
+++ b/solution.py
@@ -91,22 +91,35 @@
     chunks(x_ref.shape[1], step, 0)
 
 
-def scaled_slots(x_ref, ids_ref, gates_ref, out_ref, base):
-    select = selector(ids_ref, *out_ref.shape[:2])
-    gate = jnp.sum(select * gates_ref[...], axis=1, keepdims=True)
-    select = select.astype(BF16)
+def pick_kernel(experts, a_ref, a_ids_ref, b_ref, b_ids_ref, b_gates_ref, a_out, b_out):
+    shape = (experts, a_out.shape[0] // experts)
+    a_select = selector(a_ids_ref, *shape).astype(BF16)
+    b_select = selector(b_ids_ref, *shape)
+    gate = jnp.sum(b_select * b_gates_ref[...], axis=1, keepdims=True)
+    b_select = b_select.astype(BF16)
 
     def step(at, carry):
-        rows = jnp.dot(select, x_ref[:, pl.ds(at, CHUNK)], preferred_element_type=F32)
-        deal(out_ref, at + base, rows * gate)
-        return carry
-
-    chunks(x_ref.shape[1], step, 0)
-
-
-def send_kernel(a_ref, a_ids_ref, gain_ref, b_ref, b_ids_ref, b_gates_ref, out_ref):
-    norm_slots(a_ref, a_ids_ref, gain_ref, out_ref)
-    scaled_slots(b_ref, b_ids_ref, b_gates_ref, out_ref, a_ref.shape[1])
+        part = pl.ds(at, CHUNK)
+        a_rows = jnp.dot(a_select, a_ref[:, part], preferred_element_type=F32)
+        a_out[:, part] = a_rows.astype(BF16)
+        b_rows = jnp.dot(b_select, b_ref[:, part], preferred_element_type=F32)
+        b_out[:, part] = (b_rows * gate).astype(BF16)
+        return carry
+
+    chunks(a_ref.shape[1], step, 0)
+
+
+def pack_kernel(a_ref, gain_ref, b_ref, out_ref):
+    features = a_ref.shape[1]
+    scale = row_scale(a_ref)
+
+    def step(at, carry):
+        part = pl.ds(at, CHUNK)
+        deal(out_ref, at, a_ref[:, part].astype(F32) * scale * gain_ref[:, part])
+        deal(out_ref, at + features, b_ref[:, part])
+        return carry
+
+    chunks(features, step, 0)
 
 
 def unpack_kernel(in_ref, *outs):
@@ -330,30 +343,34 @@
         return jax.ShapeDtypeStruct((experts, capacity, width), BF16)
 
     rows = jax.ShapeDtypeStruct((experts * capacity, features), BF16)
+    near_ids = shifted(fwd_ids, "pp", -1)
+    far_ids, far_gates = shifted(bwd_ids, "pp", 1), shifted(bwd_gates, "pp", 1)
+    (bwd_send,) = call(norm_slots, [slots(features)], bwd_x, bwd_ids, norm_gain)
+    (bwd_slots,) = call(unpack_kernel, [rows], exchange(bwd_send))
+    fwd_rows, grad_rows = call(
+        functools.partial(pick_kernel, experts),
+        [rows, rows],
+        *(fwd_in[0], near_ids, bwd_grad[0], far_ids, far_gates),
+    )
+    fwd_rows, grad_rows = shifted(fwd_rows, "pp", 1), shifted(grad_rows, "pp", -1)
+    (send,) = call(pack_kernel, [slots(2 * features)], fwd_rows, norm_gain, grad_rows)
+    fwd_slots, grad_slots = call(unpack_kernel, [rows, rows], exchange(send))
     arrived = shifted(fwd_in[0], "pp", 1)
     upstream = shifted(bwd_grad[0], "pp", -1)
-
-    (bwd_send,) = call(norm_slots, [slots(features)], bwd_x, bwd_ids, norm_gain)
-    (bwd_slots,) = call(unpack_kernel, [rows], exchange(bwd_send))
-    (send,) = call(
-        send_kernel,
-        [slots(2 * features)],
-        *(arrived, fwd_ids, norm_gain, upstream, bwd_ids, bwd_gates),
-    )
-    fwd_slots, grad_slots = call(unpack_kernel, [rows, rows], exchange(send))
 
     bwd_blocks = ring_gather(bwd_slots, 1)
     fwd_blocks = ring_gather(fwd_slots, -1)
     grad_blocks = ring_gather(grad_slots, 1)
-
-    near, last = [0, 1, -1, 2, -2, 3, -3], [4]
-    fwd_parts = forward_parts(fwd_blocks, near, weights)
-    fwd_parts |= forward_parts(fwd_blocks, last, weights)
+    arrived, upstream, fwd_blocks[3] = lax.optimization_barrier(
+        (arrived, upstream, fwd_blocks[3])
+    )
+
+    keys = list(fwd_blocks)
+    fwd_parts = forward_parts(fwd_blocks, keys, weights)
     fwd_sums = ring_reduce(fwd_parts, -1)
 
-    acts = gate_and_up(bwd_blocks, near + last, gate_mat, up_mat)
-    bwd_parts = backward_parts(grad_blocks, acts, near, weights)
-    bwd_parts |= backward_parts(grad_blocks, acts, last, weights)
+    acts = gate_and_up(bwd_blocks, keys, gate_mat, up_mat)
+    bwd_parts = backward_parts(grad_blocks, acts, keys, weights)
     bwd_sums = ring_reduce(bwd_parts, 1)
 
     (back,) = call(total_kernel, [slots(2 * features)], *fwd_sums, *bwd_sums)

time: 216 us -> 201 us (0.931)
  blocking collectives: 41.5 us -> 18.1 us
  waiting for transfers between devices: 73.9 us -> 94 us
  Pallas kernels: 27.9 us -> 22.8 us
  local copies, waits for them, and re-layouts: 6.92 us -> 3.9 us
    all_to_all x2 -> x1, blocking collectives: 41.5 us -> 18.1 us  [exchange(): return lax.all_to_all(slots, 'e', split_axis=0, concat_axis=0, tiled=True)]
    ppermute x37 -> x42, waiting for transfers between devices: 73.9 us -> 87.3 us  [shifted(): return lax.ppermute(block, axis, route)]
    ppermute x37 -> x42, starting transfers between devices: 56.2 us -> 47.5 us  [shifted(): return lax.ppermute(block, axis, route)]
    all_to_all x1 -> x2, starting transfers between devices: 5.03 us -> 12.4 us  [exchange(): return lax.all_to_all(slots, 'e', split_axis=0, concat_axis=0, tiled=True)]
    all_to_all x1 -> x2, waiting for transfers between devices: 0.01 us -> 6.71 us  [exchange(): return lax.all_to_all(slots, 'e', split_axis=0, concat_axis=0, tiled=True)]
    pallas_call x10 -> x9, Pallas kernels: 23.7 us -> 18.6 us  [call(): pl.pallas_call(kernel, out_shape=outs, in_specs=[pl.BlockSpec(memory_spac...]
    unnamed x36 -> x28, local copies, waits for them, and re-layouts: 6.92 us -> 3.9 us
  transfers between devices with their start and end apart: 38 -> 44, of which waited for: 17 -> 24; matrix products, arithmetic and copies ran while one was open for 0% -> 0% of each run, Pallas kernels for 11% -> 8%
where the time goes in v1:
time: 201 us; the launch traced here: 200 us
  waiting for transfers between devices  94 us (47%)
  starting transfers between devices  59.8 us (30%)
  Pallas kernels  22.8 us (11%)
  blocking collectives  18.1 us (9%)
  local copies, waits for them, and re-layouts  3.9 us (2%)
    ppermute x42, waiting for transfers between devices, shifted(): return lax.ppermute(block, axis, route)  87.3 us
    ppermute x42, starting transfers between devices, shifted(): return lax.ppermute(block, axis, route)  47.5 us
    pallas_call x9, Pallas kernels, call(): pl.pallas_call(kernel, out_shape=outs, in_specs=[pl.BlockSpec(memory_spac...  18.6 us
    all_to_all x1, blocking collectives, exchange(): return lax.all_to_all(slots, 'e', split_axis=0, concat_axis=0, tiled=True)  18.1 us
    all_to_all x2, starting transfers between devices, exchange(): return lax.all_to_all(slots, 'e', split_axis=0, concat_axis=0, tiled=True)  12.4 us
    all_to_all x2, waiting for transfers between devices, exchange(): return lax.all_to_all(slots, 'e', split_axis=0, concat_axis=0, tiled=True)  6.71 us
    pallas_call x1, Pallas kernels, body(): pl.pallas_call(result_kernel, out_shape=[out, out], in_specs=[pl.BlockSpe...  4.14 us
  transfers between devices with their start and end apart: 44, of which 24 were waited for; matrix products, arithmetic and copies ran while one was open for 0% of the time, Pallas kernels for 8%

profile of v1, /device:TPU:2, one launch (start us, length us, event | category | flops | bytes accessed | tf_op | source)
XLA Modules:
  0.0 200.3 jit_solution(2061287192286805793)
XLA Ops:
  0.7 1.7 collective-permute-start
  2.5 1.4 collective-permute-done.1.b_ids_ref
  3.9 1.7 collective-permute-done.2.b_gates_ref
  7.9 1.4 shard_map.122
  9.4 1.7 collective-permute-start.4
  11.2 2.9 %shard_map.126 = bf16[8,3,7168]{2,1,0:T(4,128)(2,1)} custom-call(bf16[64,7168]{1,0:T(8,128)(2,1)S(1)} %bitcast.20, s32[1,64]{1,0:T(1,128)S(1)} %bitcast.27, f32[1,7168]{1,0:T(1,128)S(1)} %copy-done.8), custom_call_target="tpu_custom_call" | custom-call | tf_op jit(solution)/shard_map/pallas_call | solution.py:25
  14.0 7.5 %all-to-all-start.1 = ((bf16[8,3,7168]{2,1,0:T(4,128)(2,1)}), bf16[8,3,7168]{2,1,0:T(4,128)(2,1)S(1)}, u32[]{:S(2)}, u32[]{:S(2)}) async-start(bf16[8,3,7168]{2,1,0:T(4,128)(2,1)} %shard_map.126), calls=%async_computation.1 | async-start | bytes 917504 | tf_op jit(solution)/shard_map/all_to_all | solution.py:328
  21.5 1.9 shard_map.123
  23.5 6.7 %all-to-all-done.1.in_ref = bf16[8,3,7168]{2,1,0:T(4,128)(2,1)S(1)} async-done(((bf16[8,3,7168]{2,1,0:T(4,128)(2,1)}), bf16[8,3,7168]{2,1,0:T(4,128)(2,1)S(1)}, u32[]{:S(2)}, u32[]{:S(2)}) %all-to-all-start.1) | async-done | bytes 344096 | tf_op jit(solution)/shard_map/all_to_all | solution.py:328
  30.2 4.9 %all-to-all-start = ((bf16[8,3,14336]{2,1,0:T(4,128)(2,1)}), bf16[8,3,14336]{2,1,0:T(4,128)(2,1)S(1)}, u32[]{:S(2)}, u32[]{:S(2)}) async-start(bf16[8,3,14336]{2,1,0:T(4,128)(2,1)} %shard_map.123), calls=%async_computation | async-start | bytes 1835008 | tf_op jit(solution)/shard_map/all_to_all | solution.py:328
  35.3 2.0 collective-permute-start.28
  37.3 4.0 %collective-permute-start.29 = (bf16[24,7168]{1,0:T(8,128)(2,1)S(1)}, bf16[24,7168]{1,0:T(8,128)(2,1)}, u32[]{:S(2)}, u32[]{:S(2)}) collective-permute-start(bf16[24,7168]{1,0:T(8,128)(2,1)S(1)} %shard_map.127.refs_0_), channel_id=1, source_target_pairs={{0,7},{1,0},{2,1},{3,2},{4,3},{5,4},{6,5},{7,6},{8,15},{9,8},{10,9... | collective-permute-start | bytes 1032200 | tf_op jit(solution)/shard_map/ppermute | solution.py:21
  41.3 6.9 %collective-permute-done.28.refs_1_ = bf16[24,7168]{1,0:T(8,128)(2,1)S(1)} collective-permute-done((bf16[24,7168]{1,0:T(8,128)(2,1)S(1)}, bf16[24,7168]{1,0:T(8,128)(2,1)S(1)}, u32[]{:S(2)}, u32[]{:S(2)}) %collective-permute-start.28) | collective-permute-done | bytes 344096 | tf_op jit(solution)/shard_map/ppermute | solution.py:21
  48.2 3.2 %collective-permute-start.31 = (bf16[24,7168]{1,0:T(8,128)(2,1)}, bf16[24,7168]{1,0:T(8,128)(2,1)}, u32[]{:S(2)}, u32[]{:S(2)}) collective-permute-start(bf16[24,7168]{1,0:T(8,128)(2,1)} %collective-permute-done.29.refs_2_), channel_id=1, source_target_pairs={{0,7},{1,0},{2,1},{3,2},{4,3},{5,4},{6,5},{7,6},{8,15},{9,8},{10,9... | collective-permute-start | bytes 1032200 | tf_op jit(solution)/shard_map/ppermute | solution.py:21
  51.9 3.2 %collective-permute-start.22 = (bf16[24,7168]{1,0:T(8,128)(2,1)S(1)}, bf16[24,7168]{1,0:T(8,128)(2,1)S(1)}, u32[]{:S(2)}, u32[]{:S(2)}) collective-permute-start(bf16[24,7168]{1,0:T(8,128)(2,1)S(1)} %get-tuple-element.55.refs_0_), channel_id=1, source_target_pairs={{0,7},{1,0},{2,1},{3,2},{4,3},{5,4},{6,5},{7,6},{8,15},{9,8},{10,9... | collective-permute-start | bytes 1032200 | tf_op jit(solution)/shard_map/ppermute | solution.py:21
  56.4 4.1 %collective-permute-done.30.refs_3_ = bf16[24,7168]{1,0:T(8,128)(2,1)} collective-permute-done((bf16[24,7168]{1,0:T(8,128)(2,1)S(1)}, bf16[24,7168]{1,0:T(8,128)(2,1)}, u32[]{:S(2)}, u32[]{:S(2)}) %collective-permute-start.30) | collective-permute-done | bytes 344096 | tf_op jit(solution)/shard_map/ppermute | solution.py:21
  60.5 7.3 %collective-permute-done.21.refs_1_ = bf16[24,7168]{1,0:T(8,128)(2,1)S(1)} collective-permute-done((bf16[24,7168]{1,0:T(8,128)(2,1)S(1)}, bf16[24,7168]{1,0:T(8,128)(2,1)S(1)}, u32[]{:S(2)}, u32[]{:S(2)}) %collective-permute-start.21) | collective-permute-done | bytes 344096 | tf_op jit(solution)/shard_map/ppermute | solution.py:21
  68.0 1.8 collective-permute-start.23
  69.8 5.1 %collective-permute-done.6.refs_2_ = bf16[24,7168]{1,0:T(8,128)(2,1)S(1)} collective-permute-done((bf16[24,7168]{1,0:T(8,128)(2,1)S(1)}, bf16[24,7168]{1,0:T(8,128)(2,1)S(1)}, u32[]{:S(2)}, u32[]{:S(2)}) %collective-permute-start.6) | collective-permute-done | bytes 344096 | tf_op jit(solution)/shard_map/ppermute | solution.py:21
  74.9 3.7 %collective-permute-start.24 = (bf16[24,7168]{1,0:T(8,128)(2,1)S(1)}, bf16[24,7168]{1,0:T(8,128)(2,1)S(1)}, u32[]{:S(2)}, u32[]{:S(2)}) collective-permute-start(bf16[24,7168]{1,0:T(8,128)(2,1)S(1)} %collective-permute-done.22.refs_2_), channel_id=1, source_target_pairs={{0,7},{1,0},{2,1},{3,2},{4,3},{5,4},{6,5},{7,6},{8,15},{9,8},{10,9... | collective-permute-start | bytes 1032200 | tf_op jit(solution)/shard_map/ppermute | solution.py:21
  78.6 3.9 %collective-permute-done.32.refs_5_ = bf16[24,7168]{1,0:T(8,128)(2,1)S(1)} collective-permute-done((bf16[24,7168]{1,0:T(8,128)(2,1)}, bf16[24,7168]{1,0:T(8,128)(2,1)S(1)}, u32[]{:S(2)}, u32[]{:S(2)}) %collective-permute-start.32) | collective-permute-done | bytes 344096 | tf_op jit(solution)/shard_map/ppermute | solution.py:21
  82.5 7.4 %collective-permute-done.23.refs_3_ = bf16[24,7168]{1,0:T(8,128)(2,1)S(1)} collective-permute-done((bf16[24,7168]{1,0:T(8,128)(2,1)S(1)}, bf16[24,7168]{1,0:T(8,128)(2,1)S(1)}, u32[]{:S(2)}, u32[]{:S(2)}) %collective-permute-start.23) | collective-permute-done | bytes 344096 | tf_op jit(solution)/shard_map/ppermute | solution.py:21
  89.9 3.9 %collective-permute-done.8.refs_4_ = bf16[24,7168]{1,0:T(8,128)(2,1)S(1)} collective-permute-done((bf16[24,7168]{1,0:T(8,128)(2,1)S(1)}, bf16[24,7168]{1,0:T(8,128)(2,1)S(1)}, u32[]{:S(2)}, u32[]{:S(2)}) %collective-permute-start.8) | collective-permute-done | bytes 344096 | tf_op jit(solution)/shard_map/ppermute | solution.py:21
  93.8 3.5 %collective-permute-done.7.refs_3_ = bf16[24,7168]{1,0:T(8,128)(2,1)S(1)} collective-permute-done((bf16[24,7168]{1,0:T(8,128)(2,1)S(1)}, bf16[24,7168]{1,0:T(8,128)(2,1)S(1)}, u32[]{:S(2)}, u32[]{:S(2)}) %collective-permute-start.7) | collective-permute-done | bytes 344096 | tf_op jit(solution)/shard_map/ppermute | solution.py:21
  97.5 7.1 %collective-permute-done.34.refs_7_ = bf16[24,7168]{1,0:T(8,128)(2,1)S(1)} collective-permute-done((bf16[24,7168]{1,0:T(8,128)(2,1)S(1)}, bf16[24,7168]{1,0:T(8,128)(2,1)S(1)}, u32[]{:S(2)}, u32[]{:S(2)}) %collective-permute-start.34) | collective-permute-done | bytes 344096 | tf_op jit(solution)/shard_map/ppermute | solution.py:21
  104.9 4.2 %collective-permute-done.25.refs_5_ = bf16[24,7168]{1,0:T(8,128)(2,1)S(1)} collective-permute-done((bf16[24,7168]{1,0:T(8,128)(2,1)S(1)}, bf16[24,7168]{1,0:T(8,128)(2,1)S(1)}, u32[]{:S(2)}, u32[]{:S(2)}) %collective-permute-start.25) | collective-permute-done | bytes 344096 | tf_op jit(solution)/shard_map/ppermute | solution.py:21
  109.1 1.5 copy-done.1
  110.6 3.3 %shard_map.128 = (f32[24,128]{1,0:T(8,128)S(1)}, f32[24,128]{1,0:T(8,128)S(1)}, f32[24,128]{1,0:T(8,128)S(1)}, f32[24,128]{1,0:T(8,128)S(1)}, f32[24,128]{1,0:T(...) custom-call(bf16[24,7168]{1,0:T(8,128)(2,1)S(1)} %shard_map.127.refs, ...), custom_call_target="tpu_custom_call" | custom-call | tf_op jit(solution)/shard_map/pallas_call | solution.py:25
  114.0 3.3 %collective-permute-start.13 = (bf16[24,7168]{1,0:T(8,128)(2,1)S(1)}, bf16[24,7168]{1,0:T(8,128)(2,1)S(1)}, u32[]{:S(2)}, u32[]{:S(2)}) collective-permute-start(bf16[24,7168]{1,0:T(8,128)(2,1)S(1)} %collective-permute-done.12.refs_6_), channel_id=1, source_target_pairs={{0,7},{1,0},{2,1},{3,2},{4,3},{5,4},{6,5},{7,6},{8,15},{9,8},{10,9... | collective-permute-start | bytes 1032200 | tf_op jit(solution)/shard_map/ppermute | solution.py:21
  117.3 2.8 %collective-permute-done.27.refs_7_ = bf16[24,7168]{1,0:T(8,128)(2,1)S(1)} collective-permute-done((bf16[24,7168]{1,0:T(8,128)(2,1)S(1)}, bf16[24,7168]{1,0:T(8,128)(2,1)S(1)}, u32[]{:S(2)}, u32[]{:S(2)}) %collective-permute-start.27) | collective-permute-done | bytes 344096 | tf_op jit(solution)/shard_map/ppermute | solution.py:21
  120.1 4.2 %shard_map.129 = (bf16[24,7168]{1,0:T(8,128)(2,1)S(1)}, bf16[24,7168]{1,0:T(8,128)(2,1)S(1)}, bf16[24,7168]{1,0:T(8,128)(2,1)S(1)}, bf16[24,7168]{1,0:T(8,128)(2...) custom-call(bf16[24,7168]{1,0:T(8,128)(2,1)S(1)} %get-tuple-element., ...), custom_call_target="tpu_custom_call" | custom-call | tf_op jit(solution)/shard_map/pallas_call | solution.py:25
  124.5 2.0 collective-permute-start.35
  126.5 3.7 %shard_map.125 = (bf16[24,7168]{1,0:T(8,128)(2,1)S(1)}, bf16[24,7168]{1,0:T(8,128)(2,1)S(1)}, bf16[24,7168]{1,0:T(8,128)(2,1)S(1)}, bf16[24,7168]{1,0:T(8,128)(2...) custom-call(bf16[24,7168]{1,0:T(8,128)(2,1)S(1)} %get-tuple-element., ...), custom_call_target="tpu_custom_call" | custom-call | tf_op jit(solution)/shard_map/pallas_call | solution.py:25
  130.2 2.1 %collective-permute-start.18 = (bf16[24,7168]{1,0:T(8,128)(2,1)S(1)}, bf16[24,7168]{1,0:T(8,128)(2,1)S(1)}, u32[]{:S(2)}, u32[]{:S(2)}) collective-permute-start(bf16[24,7168]{1,0:T(8,128)(2,1)S(1)} %get-tuple-element.52), channel_id=1, source_target_pairs={{0,1},{1,2},{2,3},{3,4},{4,5},{5,6},{6,7},{7,0},{8,9},{9,10},{10,1... | collective-permute-start | bytes 1032200 | tf_op jit(solution)/shard_map/ppermute | solution.py:21
  134.5 1.9 collective-permute-start.40
  137.5 6.3 %collective-permute-done.18 = bf16[24,7168]{1,0:T(8,128)(2,1)S(1)} collective-permute-done((bf16[24,7168]{1,0:T(8,128)(2,1)S(1)}, bf16[24,7168]{1,0:T(8,128)(2,1)S(1)}, u32[]{:S(2)}, u32[]{:S(2)}) %collective-permute-start.18) | collective-permute-done | bytes 344096 | tf_op jit(solution)/shard_map/ppermute | solution.py:21
  145.0 2.4 %collective-permute-start.15 = (bf16[24,7168]{1,0:T(8,128)(2,1)S(1)}, bf16[24,7168]{1,0:T(8,128)(2,1)S(1)}, u32[]{:S(2)}, u32[]{:S(2)}) collective-permute-start(bf16[24,7168]{1,0:T(8,128)(2,1)S(1)} %add_convert_fusion.9), channel_id=1, source_target_pairs={{0,7},{1,0},{2,1},{3,2},{4,3},{5,4},{6,5},{7,6},{8,15},{9,8},{10,9... | collective-permute-start | bytes 1032200 | tf_op jit(solution)/shard_map/ppermute | solution.py:21
  147.4 3.3 %collective-permute-done.40 = bf16[24,7168]{1,0:T(8,128)(2,1)S(1)} collective-permute-done((bf16[24,7168]{1,0:T(8,128)(2,1)S(1)}, bf16[24,7168]{1,0:T(8,128)(2,1)S(1)}, u32[]{:S(2)}, u32[]{:S(2)}) %collective-permute-start.40) | collective-permute-done | bytes 344096 | tf_op jit(solution)/shard_map/ppermute | solution.py:21
  150.8 2.5 %collective-permute-start.41 = (bf16[24,7168]{1,0:T(8,128)(2,1)S(1)}, bf16[24,7168]{1,0:T(8,128)(2,1)S(1)}, u32[]{:S(2)}, u32[]{:S(2)}) collective-permute-start(bf16[24,7168]{1,0:T(8,128)(2,1)S(1)} %add_convert_fusion), channel_id=1, source_target_pairs={{0,7},{1,0},{2,1},{3,2},{4,3},{5,4},{6,5},{7,6},{8,15},{9,8},{10,9... | collective-permute-start | bytes 1032200 | tf_op jit(solution)/shard_map/ppermute | solution.py:21
  153.4 5.2 %collective-permute-done.19 = bf16[24,7168]{1,0:T(8,128)(2,1)S(1)} collective-permute-done((bf16[24,7168]{1,0:T(8,128)(2,1)S(1)}, bf16[24,7168]{1,0:T(8,128)(2,1)S(1)}, u32[]{:S(2)}, u32[]{:S(2)}) %collective-permute-start.19) | collective-permute-done | bytes 344096 | tf_op jit(solution)/shard_map/ppermute | solution.py:21
  159.7 2.4 %collective-permute-start.16 = (bf16[24,7168]{1,0:T(8,128)(2,1)S(1)}, bf16[24,7168]{1,0:T(8,128)(2,1)S(1)}, u32[]{:S(2)}, u32[]{:S(2)}) collective-permute-start(bf16[24,7168]{1,0:T(8,128)(2,1)S(1)} %add_convert_fusion.8), channel_id=1, source_target_pairs={{0,7},{1,0},{2,1},{3,2},{4,3},{5,4},{6,5},{7,6},{8,15},{9,8},{10,9... | collective-permute-start | bytes 1032200 | tf_op jit(solution)/shard_map/ppermute | solution.py:21
  162.2 3.8 %collective-permute-done.37 = bf16[24,7168]{1,0:T(8,128)(2,1)S(1)} collective-permute-done((bf16[24,7168]{1,0:T(8,128)(2,1)S(1)}, bf16[24,7168]{1,0:T(8,128)(2,1)S(1)}, u32[]{:S(2)}, u32[]{:S(2)}) %collective-permute-start.37) | collective-permute-done | bytes 344096 | tf_op jit(solution)/shard_map/ppermute | solution.py:21
  167.0 2.8 %collective-permute-done.16 = bf16[24,7168]{1,0:T(8,128)(2,1)S(1)} collective-permute-done((bf16[24,7168]{1,0:T(8,128)(2,1)S(1)}, bf16[24,7168]{1,0:T(8,128)(2,1)S(1)}, u32[]{:S(2)}, u32[]{:S(2)}) %collective-permute-start.16) | collective-permute-done | bytes 344096 | tf_op jit(solution)/shard_map/ppermute | solution.py:21
  170.0 1.7 collective-permute-start.17
  171.7 1.7 collective-permute-done.20.refs_2_
  173.3 4.1 %collective-permute-done.38.refs_4_ = bf16[24,7168]{1,0:T(8,128)(2,1)S(1)} collective-permute-done((bf16[24,7168]{1,0:T(8,128)(2,1)S(1)}, bf16[24,7168]{1,0:T(8,128)(2,1)S(1)}, u32[]{:S(2)}, u32[]{:S(2)}) %collective-permute-start.38) | collective-permute-done | bytes 344096 | tf_op jit(solution)/shard_map/ppermute | solution.py:21
  178.1 18.1 %all_to_all.15.back_ref = bf16[8,3,14336]{2,1,0:T(4,128)(2,1)S(1)} all-to-all(bf16[8,3,14336]{2,1,0:T(4,128)(2,1)S(1)} %shard_map.130), channel_id=1, replica_groups=mesh['pp'=4,'e'=8,'k'=8] {'e'}, dimensions={0} | all-to-all | bytes 1376256 | tf_op jit(solution)/shard_map/all_to_all | solution.py:328
  196.2 4.1 %shard_map.131 = (bf16[64,7168]{1,0:T(8,128)(2,1)}, bf16[64,7168]{1,0:T(8,128)(2,1)}) custom-call(bf16[8,3,14336]{2,1,0:T(4,128)(2,1)S(1)} %all_to_all.15.back_ref, bf16[64,7168]{1,0:T(8,128)(2,1)S(1)} %collective-permute-done.10.a_ref, s32[1,64]{1,0:T(1,128)S(1)} %bitcast.30, f32[1,64]{1,0:T(1,128)S(1)} %bitcast.31, bf16[64,7168]{1,0:T(8,128)(2,1)S(1)} %bitcast.21, ...), custom_call_target="tpu_custom_call" | custom-call | tf_op jit(solution)/shard_map/pallas_call | solution.py:380
  (89 shorter events, 13.3 us)
Async XLA Ops:
  0.6 3.2 %collective-permute-start.1 = (s32[1,64]{1,0:T(1,128)}, s32[1,64]{1,0:T(1,128)S(1)}, u32[]{:S(2)}, u32[]{:S(2)}) collective-permute-start(s32[1,64]{1,0:T(1,128)} %bitcast.26), channel_id=1, source_target_pairs={{0,64},{64,128},{128,192},{192,0},{1,65},{65,129},{129,193},{193,1... | collective-permute-start | bytes 776 | tf_op jit(solution)/shard_map/ppermute | solution.py:21
  0.7 3.2 %collective-permute-start = (s32[1,64]{1,0:T(1,128)}, s32[1,64]{1,0:T(1,128)S(1)}, u32[]{:S(2)}, u32[]{:S(2)}) collective-permute-start(s32[1,64]{1,0:T(1,128)} %bitcast.29), channel_id=1, source_target_pairs={{0,192},{64,0},{128,64},{192,128},{1,193},{65,1},{129,65},{193,129... | collective-permute-start | bytes 776 | tf_op jit(solution)/shard_map/ppermute | solution.py:21
  2.5 3.1 %collective-permute-start.2 = (f32[1,64]{1,0:T(1,128)}, f32[1,64]{1,0:T(1,128)S(1)}, u32[]{:S(2)}, u32[]{:S(2)}) collective-permute-start(f32[1,64]{1,0:T(1,128)} %bitcast.34), channel_id=1, source_target_pairs={{0,64},{64,128},{128,192},{192,0},{1,65},{65,129},{129,193},{193,1... | collective-permute-start | bytes 776 | tf_op jit(solution)/shard_map/ppermute | solution.py:21
  9.3 12.2 %collective-permute-start.3 = (bf16[24,7168]{1,0:T(8,128)(2,1)S(1)}, bf16[24,7168]{1,0:T(8,128)(2,1)S(1)}, u32[]{:S(2)}, u32[]{:S(2)}) collective-permute-start(bf16[24,7168]{1,0:T(8,128)(2,1)S(1)} %get-tuple-element.43), channel_id=1, source_target_pairs={{0,64},{64,128},{128,192},{192,0},{1,65},{65,129},{129,193},{193,1... | collective-permute-start | bytes 1032200 | tf_op jit(solution)/shard_map/ppermute | solution.py:21
  9.4 12.1 %collective-permute-start.4 = (bf16[24,7168]{1,0:T(8,128)(2,1)S(1)}, bf16[24,7168]{1,0:T(8,128)(2,1)S(1)}, u32[]{:S(2)}, u32[]{:S(2)}) collective-permute-start(bf16[24,7168]{1,0:T(8,128)(2,1)S(1)} %get-tuple-element.44), channel_id=1, source_target_pairs={{0,192},{64,0},{128,64},{192,128},{1,193},{65,1},{129,65},{193,129... | collective-permute-start | bytes 1032200 | tf_op jit(solution)/shard_map/ppermute | solution.py:21
  14.0 16.1 %all-to-all-start.1 = ((bf16[8,3,7168]{2,1,0:T(4,128)(2,1)}), bf16[8,3,7168]{2,1,0:T(4,128)(2,1)S(1)}, u32[]{:S(2)}, u32[]{:S(2)}) async-start(bf16[8,3,7168]{2,1,0:T(4,128)(2,1)} %shard_map.126), calls=%async_computation.1 | async-start | bytes 917504 | tf_op jit(solution)/shard_map/all_to_all | solution.py:328
  23.5 85.6 %copy-start = (bf16[1,1,7168,128]{3,2,1,0:T(8,128)(2,1)S(1)}, bf16[1,1,7168,128]{3,2,1,0:T(8,128)(2,1)}, u32[]{:S(2)}) copy-start(bf16[1,1,7168,128]{3,2,1,0:T(8,128)(2,1)} %param.19) | copy-start | bytes 5505028
  30.2 21.3 %all-to-all-start = ((bf16[8,3,14336]{2,1,0:T(4,128)(2,1)}), bf16[8,3,14336]{2,1,0:T(4,128)(2,1)S(1)}, u32[]{:S(2)}, u32[]{:S(2)}) async-start(bf16[8,3,14336]{2,1,0:T(4,128)(2,1)} %shard_map.123), calls=%async_computation | async-start | bytes 1835008 | tf_op jit(solution)/shard_map/all_to_all | solution.py:328
  35.3 12.9 %collective-permute-start.28 = (bf16[24,7168]{1,0:T(8,128)(2,1)S(1)}, bf16[24,7168]{1,0:T(8,128)(2,1)S(1)}, u32[]{:S(2)}, u32[]{:S(2)}) collective-permute-start(bf16[24,7168]{1,0:T(8,128)(2,1)S(1)} %shard_map.127.refs_0_), channel_id=1, source_target_pairs={{0,1},{1,2},{2,3},{3,4},{4,5},{5,6},{6,7},{7,0},{8,9},{9,10},{10,1... | collective-permute-start | bytes 1032200 | tf_op jit(solution)/shard_map/ppermute | solution.py:21
  37.3 10.9 %collective-permute-start.29 = (bf16[24,7168]{1,0:T(8,128)(2,1)S(1)}, bf16[24,7168]{1,0:T(8,128)(2,1)}, u32[]{:S(2)}, u32[]{:S(2)}) collective-permute-start(bf16[24,7168]{1,0:T(8,128)(2,1)S(1)} %shard_map.127.refs_0_), channel_id=1, source_target_pairs={{0,7},{1,0},{2,1},{3,2},{4,3},{5,4},{6,5},{7,6},{8,15},{9,8},{10,9... | collective-permute-start | bytes 1032200 | tf_op jit(solution)/shard_map/ppermute | solution.py:21
  48.2 12.3 %collective-permute-start.30 = (bf16[24,7168]{1,0:T(8,128)(2,1)S(1)}, bf16[24,7168]{1,0:T(8,128)(2,1)}, u32[]{:S(2)}, u32[]{:S(2)}) collective-permute-start(bf16[24,7168]{1,0:T(8,128)(2,1)S(1)} %collective-permute-done.28.refs_1_), channel_id=1, source_target_pairs={{0,1},{1,2},{2,3},{3,4},{4,5},{5,6},{6,7},{7,0},{8,9},{9,10},{10,1... | collective-permute-start | bytes 1032200 | tf_op jit(solution)/shard_map/ppermute | solution.py:21
  48.2 12.3 %collective-permute-start.31 = (bf16[24,7168]{1,0:T(8,128)(2,1)}, bf16[24,7168]{1,0:T(8,128)(2,1)}, u32[]{:S(2)}, u32[]{:S(2)}) collective-permute-start(bf16[24,7168]{1,0:T(8,128)(2,1)} %collective-permute-done.29.refs_2_), channel_id=1, source_target_pairs={{0,7},{1,0},{2,1},{3,2},{4,3},{5,4},{6,5},{7,6},{8,15},{9,8},{10,9... | collective-permute-start | bytes 1032200 | tf_op jit(solution)/shard_map/ppermute | solution.py:21
  51.8 15.9 %collective-permute-start.21 = (bf16[24,7168]{1,0:T(8,128)(2,1)S(1)}, bf16[24,7168]{1,0:T(8,128)(2,1)S(1)}, u32[]{:S(2)}, u32[]{:S(2)}) collective-permute-start(bf16[24,7168]{1,0:T(8,128)(2,1)S(1)} %get-tuple-element.55.refs_0_), channel_id=1, source_target_pairs={{0,1},{1,2},{2,3},{3,4},{4,5},{5,6},{6,7},{7,0},{8,9},{9,10},{10,1... | collective-permute-start | bytes 1032200 | tf_op jit(solution)/shard_map/ppermute | solution.py:21
  51.9 16.1 %collective-permute-start.22 = (bf16[24,7168]{1,0:T(8,128)(2,1)S(1)}, bf16[24,7168]{1,0:T(8,128)(2,1)S(1)}, u32[]{:S(2)}, u32[]{:S(2)}) collective-permute-start(bf16[24,7168]{1,0:T(8,128)(2,1)S(1)} %get-tuple-element.55.refs_0_), channel_id=1, source_target_pairs={{0,7},{1,0},{2,1},{3,2},{4,3},{5,4},{6,5},{7,6},{8,15},{9,8},{10,9... | collective-permute-start | bytes 1032200 | tf_op jit(solution)/shard_map/ppermute | solution.py:21
  55.1 19.7 %collective-permute-start.6 = (bf16[24,7168]{1,0:T(8,128)(2,1)S(1)}, bf16[24,7168]{1,0:T(8,128)(2,1)S(1)}, u32[]{:S(2)}, u32[]{:S(2)}) collective-permute-start(bf16[24,7168]{1,0:T(8,128)(2,1)S(1)} %get-tuple-element.45.refs_0_), channel_id=1, source_target_pairs={{0,7},{1,0},{2,1},{3,2},{4,3},{5,4},{6,5},{7,6},{8,15},{9,8},{10,9... | collective-permute-start | bytes 1032200 | tf_op jit(solution)/shard_map/ppermute | solution.py:21
  60.5 18.1 %collective-permute-start.5 = (bf16[24,7168]{1,0:T(8,128)(2,1)S(1)}, bf16[24,7168]{1,0:T(8,128)(2,1)S(1)}, u32[]{:S(2)}, u32[]{:S(2)}) collective-permute-start(bf16[24,7168]{1,0:T(8,128)(2,1)S(1)} %get-tuple-element.45.refs_0_), channel_id=1, source_target_pairs={{0,1},{1,2},{2,3},{3,4},{4,5},{5,6},{6,7},{7,0},{8,9},{9,10},{10,1... | collective-permute-start | bytes 1032200 | tf_op jit(solution)/shard_map/ppermute | solution.py:21
  60.5 22.0 %collective-permute-start.32 = (bf16[24,7168]{1,0:T(8,128)(2,1)}, bf16[24,7168]{1,0:T(8,128)(2,1)S(1)}, u32[]{:S(2)}, u32[]{:S(2)}) collective-permute-start(bf16[24,7168]{1,0:T(8,128)(2,1)} %collective-permute-done.30.refs_3_), channel_id=1, source_target_pairs={{0,1},{1,2},{2,3},{3,4},{4,5},{5,6},{6,7},{7,0},{8,9},{9,10},{10,1... | collective-permute-start | bytes 1032200 | tf_op jit(solution)/shard_map/ppermute | solution.py:21
  67.8 14.8 %collective-permute-start.33 = (bf16[24,7168]{1,0:T(8,128)(2,1)}, bf16[24,7168]{1,0:T(8,128)(2,1)S(1)}, u32[]{:S(2)}, u32[]{:S(2)}) collective-permute-start(bf16[24,7168]{1,0:T(8,128)(2,1)} %collective-permute-done.31.refs_4_), channel_id=1, source_target_pairs={{0,7},{1,0},{2,1},{3,2},{4,3},{5,4},{6,5},{7,6},{8,15},{9,8},{10,9... | collective-permute-start | bytes 1032200 | tf_op jit(solution)/shard_map/ppermute | solution.py:21
  68.0 21.8 %collective-permute-start.23 = (bf16[24,7168]{1,0:T(8,128)(2,1)S(1)}, bf16[24,7168]{1,0:T(8,128)(2,1)S(1)}, u32[]{:S(2)}, u32[]{:S(2)}) collective-permute-start(bf16[24,7168]{1,0:T(8,128)(2,1)S(1)} %collective-permute-done.21.refs_1_), channel_id=1, source_target_pairs={{0,1},{1,2},{2,3},{3,4},{4,5},{5,6},{6,7},{7,0},{8,9},{9,10},{10,1... | collective-permute-start | bytes 1032200 | tf_op jit(solution)/shard_map/ppermute | solution.py:21
  74.9 15.0 %collective-permute-start.24 = (bf16[24,7168]{1,0:T(8,128)(2,1)S(1)}, bf16[24,7168]{1,0:T(8,128)(2,1)S(1)}, u32[]{:S(2)}, u32[]{:S(2)}) collective-permute-start(bf16[24,7168]{1,0:T(8,128)(2,1)S(1)} %collective-permute-done.22.refs_2_), channel_id=1, source_target_pairs={{0,7},{1,0},{2,1},{3,2},{4,3},{5,4},{6,5},{7,6},{8,15},{9,8},{10,9... | collective-permute-start | bytes 1032200 | tf_op jit(solution)/shard_map/ppermute | solution.py:21
  78.6 15.2 %collective-permute-start.8 = (bf16[24,7168]{1,0:T(8,128)(2,1)S(1)}, bf16[24,7168]{1,0:T(8,128)(2,1)S(1)}, u32[]{:S(2)}, u32[]{:S(2)}) collective-permute-start(bf16[24,7168]{1,0:T(8,128)(2,1)S(1)} %collective-permute-done.6.refs_2_), channel_id=1, source_target_pairs={{0,7},{1,0},{2,1},{3,2},{4,3},{5,4},{6,5},{7,6},{8,15},{9,8},{10,9... | collective-permute-start | bytes 1032200 | tf_op jit(solution)/shard_map/ppermute | solution.py:21
  82.5 14.7 %collective-permute-start.7 = (bf16[24,7168]{1,0:T(8,128)(2,1)S(1)}, bf16[24,7168]{1,0:T(8,128)(2,1)S(1)}, u32[]{:S(2)}, u32[]{:S(2)}) collective-permute-start(bf16[24,7168]{1,0:T(8,128)(2,1)S(1)} %collective-permute-done.5.refs_1_), channel_id=1, source_target_pairs={{0,1},{1,2},{2,3},{3,4},{4,5},{5,6},{6,7},{7,0},{8,9},{9,10},{10,1... | collective-permute-start | bytes 1032200 | tf_op jit(solution)/shard_map/ppermute | solution.py:21
  82.5 22.1 %collective-permute-start.34 = (bf16[24,7168]{1,0:T(8,128)(2,1)S(1)}, bf16[24,7168]{1,0:T(8,128)(2,1)S(1)}, u32[]{:S(2)}, u32[]{:S(2)}) collective-permute-start(bf16[24,7168]{1,0:T(8,128)(2,1)S(1)} %collective-permute-done.32.refs_5_), channel_id=1, source_target_pairs={{0,1},{1,2},{2,3},{3,4},{4,5},{5,6},{6,7},{7,0},{8,9},{9,10},{10,1... | collective-permute-start | bytes 1032200 | tf_op jit(solution)/shard_map/ppermute | solution.py:21
  89.9 19.2 %collective-permute-start.25 = (bf16[24,7168]{1,0:T(8,128)(2,1)S(1)}, bf16[24,7168]{1,0:T(8,128)(2,1)S(1)}, u32[]{:S(2)}, u32[]{:S(2)}) collective-permute-start(bf16[24,7168]{1,0:T(8,128)(2,1)S(1)} %collective-permute-done.23.refs_3_), channel_id=1, source_target_pairs={{0,1},{1,2},{2,3},{3,4},{4,5},{5,6},{6,7},{7,0},{8,9},{9,10},{10,1... | collective-permute-start | bytes 1032200 | tf_op jit(solution)/shard_map/ppermute | solution.py:21
  89.9 34.6 %collective-permute-start.10 = (bf16[64,7168]{1,0:T(8,128)(2,1)}, bf16[64,7168]{1,0:T(8,128)(2,1)S(1)}, u32[]{:S(2)}, u32[]{:S(2)}) collective-permute-start(bf16[64,7168]{1,0:T(8,128)(2,1)} %bitcast.22), channel_id=1, source_target_pairs={{0,64},{64,128},{128,192},{192,0},{1,65},{65,129},{129,193},{193,1... | collective-permute-start | bytes 2752520 | tf_op jit(solution)/shard_map/ppermute | solution.py:21
  93.8 30.7 %collective-permute-start.11 = (bf16[64,7168]{1,0:T(8,128)(2,1)}, bf16[64,7168]{1,0:T(8,128)(2,1)S(1)}, u32[]{:S(2)}, u32[]{:S(2)}) collective-permute-start(bf16[64,7168]{1,0:T(8,128)(2,1)} %bitcast.24), channel_id=1, source_target_pairs={{0,192},{64,0},{128,64},{192,128},{1,193},{65,1},{129,65},{193,129... | collective-permute-start | bytes 2752520 | tf_op jit(solution)/shard_map/ppermute | solution.py:21
  97.2 16.6 %collective-permute-start.26 = (bf16[24,7168]{1,0:T(8,128)(2,1)S(1)}, bf16[24,7168]{1,0:T(8,128)(2,1)S(1)}, u32[]{:S(2)}, u32[]{:S(2)}) collective-permute-start(bf16[24,7168]{1,0:T(8,128)(2,1)S(1)} %collective-permute-done.24.refs_4_), channel_id=1, source_target_pairs={{0,7},{1,0},{2,1},{3,2},{4,3},{5,4},{6,5},{7,6},{8,15},{9,8},{10,9... | collective-permute-start | bytes 1032200 | tf_op jit(solution)/shard_map/ppermute | solution.py:21
  104.6 9.3 %collective-permute-start.12 = (bf16[24,7168]{1,0:T(8,128)(2,1)S(1)}, bf16[24,7168]{1,0:T(8,128)(2,1)S(1)}, u32[]{:S(2)}, u32[]{:S(2)}) collective-permute-start(bf16[24,7168]{1,0:T(8,128)(2,1)S(1)} %collective-permute-done.8.refs_4_), channel_id=1, source_target_pairs={{0,7},{1,0},{2,1},{3,2},{4,3},{5,4},{6,5},{7,6},{8,15},{9,8},{10,9... | collective-permute-start | bytes 1032200 | tf_op jit(solution)/shard_map/ppermute | solution.py:21
  109.1 11.1 %collective-permute-start.27 = (bf16[24,7168]{1,0:T(8,128)(2,1)S(1)}, bf16[24,7168]{1,0:T(8,128)(2,1)S(1)}, u32[]{:S(2)}, u32[]{:S(2)}) collective-permute-start(bf16[24,7168]{1,0:T(8,128)(2,1)S(1)} %collective-permute-done.25.refs_5_), channel_id=1, source_target_pairs={{0,1},{1,2},{2,3},{3,4},{4,5},{5,6},{6,7},{7,0},{8,9},{9,10},{10,1... | collective-permute-start | bytes 1032200 | tf_op jit(solution)/shard_map/ppermute | solution.py:21
  113.9 12.6 %collective-permute-start.9 = (bf16[24,7168]{1,0:T(8,128)(2,1)S(1)}, bf16[24,7168]{1,0:T(8,128)(2,1)S(1)}, u32[]{:S(2)}, u32[]{:S(2)}) collective-permute-start(bf16[24,7168]{1,0:T(8,128)(2,1)S(1)} %collective-permute-done.7.refs_3_), channel_id=1, source_target_pairs={{0,1},{1,2},{2,3},{3,4},{4,5},{5,6},{6,7},{7,0},{8,9},{9,10},{10,1... | collective-permute-start | bytes 1032200 | tf_op jit(solution)/shard_map/ppermute | solution.py:21
  114.0 12.5 %collective-permute-start.13 = (bf16[24,7168]{1,0:T(8,128)(2,1)S(1)}, bf16[24,7168]{1,0:T(8,128)(2,1)S(1)}, u32[]{:S(2)}, u32[]{:S(2)}) collective-permute-start(bf16[24,7168]{1,0:T(8,128)(2,1)S(1)} %collective-permute-done.12.refs_6_), channel_id=1, source_target_pairs={{0,7},{1,0},{2,1},{3,2},{4,3},{5,4},{6,5},{7,6},{8,15},{9,8},{10,9... | collective-permute-start | bytes 1032200 | tf_op jit(solution)/shard_map/ppermute | solution.py:21
  124.3 10.1 %collective-permute-start.39 = (bf16[24,7168]{1,0:T(8,128)(2,1)S(1)}, bf16[24,7168]{1,0:T(8,128)(2,1)S(1)}, u32[]{:S(2)}, u32[]{:S(2)}) collective-permute-start(bf16[24,7168]{1,0:T(8,128)(2,1)S(1)} %get-tuple-element.77), channel_id=1, source_target_pairs={{0,7},{1,0},{2,1},{3,2},{4,3},{5,4},{6,5},{7,6},{8,15},{9,8},{10,9... | collective-permute-start | bytes 1032200 | tf_op jit(solution)/shard_map/ppermute | solution.py:21
  124.5 12.0 %collective-permute-start.35 = (bf16[24,7168]{1,0:T(8,128)(2,1)S(1)}, bf16[24,7168]{1,0:T(8,128)(2,1)S(1)}, u32[]{:S(2)}, u32[]{:S(2)}) collective-permute-start(bf16[24,7168]{1,0:T(8,128)(2,1)S(1)} %get-tuple-element.73), channel_id=1, source_target_pairs={{0,1},{1,2},{2,3},{3,4},{4,5},{5,6},{6,7},{7,0},{8,9},{9,10},{10,1... | collective-permute-start | bytes 1032200 | tf_op jit(solution)/shard_map/ppermute | solution.py:21
  130.2 13.7 %collective-permute-start.18 = (bf16[24,7168]{1,0:T(8,128)(2,1)S(1)}, bf16[24,7168]{1,0:T(8,128)(2,1)S(1)}, u32[]{:S(2)}, u32[]{:S(2)}) collective-permute-start(bf16[24,7168]{1,0:T(8,128)(2,1)S(1)} %get-tuple-element.52), channel_id=1, source_target_pairs={{0,1},{1,2},{2,3},{3,4},{4,5},{5,6},{6,7},{7,0},{8,9},{9,10},{10,1... | collective-permute-start | bytes 1032200 | tf_op jit(solution)/shard_map/ppermute | solution.py:21
  132.3 12.6 %collective-permute-start.14 = (bf16[24,7168]{1,0:T(8,128)(2,1)S(1)}, bf16[24,7168]{1,0:T(8,128)(2,1)S(1)}, u32[]{:S(2)}, u32[]{:S(2)}) collective-permute-start(bf16[24,7168]{1,0:T(8,128)(2,1)S(1)} %get-tuple-element.48), channel_id=1, source_target_pairs={{0,7},{1,0},{2,1},{3,2},{4,3},{5,4},{6,5},{7,6},{8,15},{9,8},{10,9... | collective-permute-start | bytes 1032200 | tf_op jit(solution)/shard_map/ppermute | solution.py:21
  134.5 16.2 %collective-permute-start.40 = (bf16[24,7168]{1,0:T(8,128)(2,1)S(1)}, bf16[24,7168]{1,0:T(8,128)(2,1)S(1)}, u32[]{:S(2)}, u32[]{:S(2)}) collective-permute-start(bf16[24,7168]{1,0:T(8,128)(2,1)S(1)} %add_convert_fusion.1), channel_id=1, source_target_pairs={{0,7},{1,0},{2,1},{3,2},{4,3},{5,4},{6,5},{7,6},{8,15},{9,8},{10,9... | collective-permute-start | bytes 1032200 | tf_op jit(solution)/shard_map/ppermute | solution.py:21
  136.6 16.7 %collective-permute-start.36 = (bf16[24,7168]{1,0:T(8,128)(2,1)S(1)}, bf16[24,7168]{1,0:T(8,128)(2,1)S(1)}, u32[]{:S(2)}, u32[]{:S(2)}) collective-permute-start(bf16[24,7168]{1,0:T(8,128)(2,1)S(1)} %add_convert_fusion.4), channel_id=1, source_target_pairs={{0,1},{1,2},{2,3},{3,4},{4,5},{5,6},{6,7},{7,0},{8,9},{9,10},{10,1... | collective-permute-start | bytes 1032200 | tf_op jit(solution)/shard_map/ppermute | solution.py:21
  143.9 14.7 %collective-permute-start.19 = (bf16[24,7168]{1,0:T(8,128)(2,1)S(1)}, bf16[24,7168]{1,0:T(8,128)(2,1)S(1)}, u32[]{:S(2)}, u32[]{:S(2)}) collective-permute-start(bf16[24,7168]{1,0:T(8,128)(2,1)S(1)} %add_convert_fusion.6), channel_id=1, source_target_pairs={{0,1},{1,2},{2,3},{3,4},{4,5},{5,6},{6,7},{7,0},{8,9},{9,10},{10,1... | collective-permute-start | bytes 1032200 | tf_op jit(solution)/shard_map/ppermute | solution.py:21
  145.0 14.7 %collective-permute-start.15 = (bf16[24,7168]{1,0:T(8,128)(2,1)S(1)}, bf16[24,7168]{1,0:T(8,128)(2,1)S(1)}, u32[]{:S(2)}, u32[]{:S(2)}) collective-permute-start(bf16[24,7168]{1,0:T(8,128)(2,1)S(1)} %add_convert_fusion.9), channel_id=1, source_target_pairs={{0,7},{1,0},{2,1},{3,2},{4,3},{5,4},{6,5},{7,6},{8,15},{9,8},{10,9... | collective-permute-start | bytes 1032200 | tf_op jit(solution)/shard_map/ppermute | solution.py:21
  150.8 20.9 %collective-permute-start.41 = (bf16[24,7168]{1,0:T(8,128)(2,1)S(1)}, bf16[24,7168]{1,0:T(8,128)(2,1)S(1)}, u32[]{:S(2)}, u32[]{:S(2)}) collective-permute-start(bf16[24,7168]{1,0:T(8,128)(2,1)S(1)} %add_convert_fusion), channel_id=1, source_target_pairs={{0,7},{1,0},{2,1},{3,2},{4,3},{5,4},{6,5},{7,6},{8,15},{9,8},{10,9... | collective-permute-start | bytes 1032200 | tf_op jit(solution)/shard_map/ppermute | solution.py:21
  153.3 12.6 %collective-permute-start.37 = (bf16[24,7168]{1,0:T(8,128)(2,1)S(1)}, bf16[24,7168]{1,0:T(8,128)(2,1)S(1)}, u32[]{:S(2)}, u32[]{:S(2)}) collective-permute-start(bf16[24,7168]{1,0:T(8,128)(2,1)S(1)} %add_convert_fusion.3), channel_id=1, source_target_pairs={{0,1},{1,2},{2,3},{3,4},{4,5},{5,6},{6,7},{7,0},{8,9},{9,10},{10,1... | collective-permute-start | bytes 1032200 | tf_op jit(solution)/shard_map/ppermute | solution.py:21
  158.7 14.7 %collective-permute-start.20 = (bf16[24,7168]{1,0:T(8,128)(2,1)S(1)}, bf16[24,7168]{1,0:T(8,128)(2,1)S(1)}, u32[]{:S(2)}, u32[]{:S(2)}) collective-permute-start(bf16[24,7168]{1,0:T(8,128)(2,1)S(1)} %add_convert_fusion.5), channel_id=1, source_target_pairs={{0,1},{1,2},{2,3},{3,4},{4,5},{5,6},{6,7},{7,0},{8,9},{9,10},{10,1... | collective-permute-start | bytes 1032200 | tf_op jit(solution)/shard_map/ppermute | solution.py:21
  159.7 10.1 %collective-permute-start.16 = (bf16[24,7168]{1,0:T(8,128)(2,1)S(1)}, bf16[24,7168]{1,0:T(8,128)(2,1)S(1)}, u32[]{:S(2)}, u32[]{:S(2)}) collective-permute-start(bf16[24,7168]{1,0:T(8,128)(2,1)S(1)} %add_convert_fusion.8), channel_id=1, source_target_pairs={{0,7},{1,0},{2,1},{3,2},{4,3},{5,4},{6,5},{7,6},{8,15},{9,8},{10,9... | collective-permute-start | bytes 1032200 | tf_op jit(solution)/shard_map/ppermute | solution.py:21
  166.0 11.4 %collective-permute-start.38 = (bf16[24,7168]{1,0:T(8,128)(2,1)S(1)}, bf16[24,7168]{1,0:T(8,128)(2,1)S(1)}, u32[]{:S(2)}, u32[]{:S(2)}) collective-permute-start(bf16[24,7168]{1,0:T(8,128)(2,1)S(1)} %add_convert_fusion.2), channel_id=1, source_target_pairs={{0,1},{1,2},{2,3},{3,4},{4,5},{5,6},{6,7},{7,0},{8,9},{9,10},{10,1... | collective-permute-start | bytes 1032200 | tf_op jit(solution)/shard_map/ppermute | solution.py:21
  170.0 7.5 %collective-permute-start.17 = (bf16[24,7168]{1,0:T(8,128)(2,1)S(1)}, bf16[24,7168]{1,0:T(8,128)(2,1)S(1)}, u32[]{:S(2)}, u32[]{:S(2)}) collective-permute-start(bf16[24,7168]{1,0:T(8,128)(2,1)S(1)} %add_convert_fusion.7), channel_id=1, source_target_pairs={{0,7},{1,0},{2,1},{3,2},{4,3},{5,4},{6,5},{7,6},{8,15},{9,8},{10,9... | collective-permute-start | bytes 1032200 | tf_op jit(solution)/shard_map/ppermute | solution.py:21
  177.5 18.7 %copy-start.5 = (bf16[1,64,7168]{2,1,0:T(8,128)(2,1)S(1)}, bf16[1,64,7168]{2,1,0:T(8,128)(2,1)}, u32[]{:S(2)}) copy-start(bf16[1,64,7168]{2,1,0:T(8,128)(2,1)} %param.14) | copy-start | bytes 2752516
  177.5 18.7 %copy-start.9 = (f32[1,7168]{1,0:T(1,128)S(1)}, f32[1,7168]{1,0:T(1,128)}, u32[]{:S(2)}) copy-start(f32[1,7168]{1,0:T(1,128)} %gain_ref.5) | copy-start | bytes 86020
  177.5 18.7 %copy-start.11 = (s32[1,64,1]{1,2,0:T(1,128)S(1)}, s32[1,64,1]{1,2,0:T(1,128)}, u32[]{:S(2)}) copy-start(s32[1,64,1]{1,2,0:T(1,128)} %param.16) | copy-start | bytes 772
  (10 other events, 77.4 us)

commit v2 on v1

--- a/solution.py
+++ b/solution.py
@@ -11,8 +11,8 @@
 BF16 = jnp.bfloat16
 F32 = jnp.float32
 CHUNK = 1024
+LANES = 128
 NT = (((1,), (1,)), ((), ()))
-TN = (((0,), (0,)), ((), ()))
 
 
 def shifted(block, axis, distance):
@@ -55,15 +55,19 @@
     return (slots == target).astype(F32)
 
 
+def fold(values):
+    return sum(values[:, i : i + LANES] for i in range(0, values.shape[1], LANES))
+
+
 def row_scale(x_ref):
     rows, features = x_ref.shape
 
     def step(at, total):
         values = x_ref[:, pl.ds(at, CHUNK)].astype(F32)
-        return total + jnp.sum(values * values, axis=1, keepdims=True)
-
-    total = chunks(features, step, jnp.zeros((rows, 1), F32))
-    return lax.rsqrt(total / features + EPSILON)
+        return total + fold(values * values)
+
+    total = chunks(features, step, jnp.zeros((rows, LANES), F32))
+    return lax.rsqrt(jnp.sum(total, axis=1, keepdims=True) / features + EPSILON)
 
 
 def deal(out_ref, at, rows):
@@ -159,29 +163,25 @@
     back_ref, a_ref, a_ids_ref, a_gates_ref, x_ref, b_ref, b_ids_ref, gain_ref, a_out, b_out, held
 ):
     rows, features = a_ref.shape
-    a_select = selector(a_ids_ref, *back_ref.shape[:2]).astype(BF16)
-    b_select = selector(b_ids_ref, *back_ref.shape[:2]).astype(BF16)
+    a_select = selector(a_ids_ref, *back_ref.shape[:2]).T.astype(BF16)
+    b_select = selector(b_ids_ref, *back_ref.shape[:2]).T.astype(BF16)
     a_gate = column(a_gates_ref[...], rows)
 
     def first(at, carry):
         squares, products = carry
         part = pl.ds(at, CHUNK)
-        mix = lax.dot_general(
-            a_select, collect(back_ref, at).astype(BF16), TN, preferred_element_type=F32
-        )
+        mix = jnp.dot(a_select, collect(back_ref, at).astype(BF16), preferred_element_type=F32)
         a_out[:, part] = (a_ref[:, part].astype(F32) + mix * a_gate).astype(BF16)
-        grad = lax.dot_general(
-            b_select, collect(back_ref, at + features).astype(BF16), TN, preferred_element_type=F32
-        )
-        grad = grad * gain_ref[:, part]
+        back = collect(back_ref, at + features).astype(BF16)
+        grad = jnp.dot(b_select, back, preferred_element_type=F32) * gain_ref[:, part]
         held[:, part] = grad
         values = x_ref[:, part].astype(F32)
-        squares += jnp.sum(values * values, axis=1, keepdims=True)
-        products += jnp.sum(values * grad, axis=1, keepdims=True)
-        return squares, products
-
-    zero = jnp.zeros((rows, 1), F32)
-    squares, products = chunks(features, first, (zero, zero))
+        return squares + fold(values * values), products + fold(values * grad)
+
+    zero = jnp.zeros((rows, LANES), F32)
+    squares, products = (
+        jnp.sum(total, axis=1, keepdims=True) for total in chunks(features, first, (zero, zero))
+    )
     scale = lax.rsqrt(squares / features + EPSILON)
     pull = scale**3 * (products / features)
 
@@ -361,8 +361,8 @@
     bwd_blocks = ring_gather(bwd_slots, 1)
     fwd_blocks = ring_gather(fwd_slots, -1)
     grad_blocks = ring_gather(grad_slots, 1)
-    arrived, upstream, fwd_blocks[3] = lax.optimization_barrier(
-        (arrived, upstream, fwd_blocks[3])
+    arrived, upstream, fwd_blocks[2] = lax.optimization_barrier(
+        (arrived, upstream, fwd_blocks[2])
     )
 
     keys = list(fwd_blocks)

time: 201 us -> 200 us (level)
  transfers between devices with their start and end apart: 44 -> 44, of which waited for: 24 -> 23; matrix products, arithmetic and copies ran while one was open for 0% -> 0% of each run, Pallas kernels for 8% -> 8%
where the time goes in v2:
time: 200 us; the launch traced here: 199 us
  waiting for transfers between devices  94.5 us (47%)
  starting transfers between devices  59.8 us (30%)
  Pallas kernels  21.2 us (11%)
  blocking collectives  18.1 us (9%)
  local copies, waits for them, and re-layouts  3.9 us (2%)
    ppermute x42, waiting for transfers between devices, shifted(): return lax.ppermute(block, axis, route)  87.3 us
    ppermute x42, starting transfers between devices, shifted(): return lax.ppermute(block, axis, route)  47.4 us
    all_to_all x1, blocking collectives, exchange(): return lax.all_to_all(slots, 'e', split_axis=0, concat_axis=0, tiled=True)  18.1 us
    pallas_call x9, Pallas kernels, call(): pl.pallas_call(kernel, out_shape=outs, in_specs=[pl.BlockSpec(memory_spac...  17.7 us
    all_to_all x2, starting transfers between devices, exchange(): return lax.all_to_all(slots, 'e', split_axis=0, concat_axis=0, tiled=True)  12.4 us
    all_to_all x2, waiting for transfers between devices, exchange(): return lax.all_to_all(slots, 'e', split_axis=0, concat_axis=0, tiled=True)  7.16 us
  transfers between devices with their start and end apart: 44, of which 23 were waited for; matrix products, arithmetic and copies ran while one was open for 0% of the time, Pallas kernels for 8%

profile of v2, /device:TPU:2, one launch (start us, length us, event | category | flops | bytes accessed | tf_op | source)
XLA Modules:
  0.0 199.2 jit_solution(4412501524819881584)
XLA Ops:
  0.7 1.7 collective-permute-start
  2.5 1.4 collective-permute-done.1.b_ids_ref
  3.9 1.7 collective-permute-done.2.b_gates_ref
  7.9 1.4 shard_map.122
  9.4 1.7 collective-permute-start.4
  11.2 2.4 %shard_map.126 = bf16[8,3,7168]{2,1,0:T(4,128)(2,1)} custom-call(bf16[64,7168]{1,0:T(8,128)(2,1)S(1)} %bitcast.20, s32[1,64]{1,0:T(1,128)S(1)} %bitcast.27, f32[1,7168]{1,0:T(1,128)S(1)} %copy-done.8), custom_call_target="tpu_custom_call" | custom-call | tf_op jit(solution)/shard_map/pallas_call | solution.py:25
  13.6 7.5 %all-to-all-start.1 = ((bf16[8,3,7168]{2,1,0:T(4,128)(2,1)}), bf16[8,3,7168]{2,1,0:T(4,128)(2,1)S(1)}, u32[]{:S(2)}, u32[]{:S(2)}) async-start(bf16[8,3,7168]{2,1,0:T(4,128)(2,1)} %shard_map.126), calls=%async_computation.1 | async-start | bytes 917504 | tf_op jit(solution)/shard_map/all_to_all | solution.py:328
  21.1 1.5 shard_map.123
  22.6 7.2 %all-to-all-done.1.in_ref = bf16[8,3,7168]{2,1,0:T(4,128)(2,1)S(1)} async-done(((bf16[8,3,7168]{2,1,0:T(4,128)(2,1)}), bf16[8,3,7168]{2,1,0:T(4,128)(2,1)S(1)}, u32[]{:S(2)}, u32[]{:S(2)}) %all-to-all-start.1) | async-done | bytes 344096 | tf_op jit(solution)/shard_map/all_to_all | solution.py:328
  29.7 4.9 %all-to-all-start = ((bf16[8,3,14336]{2,1,0:T(4,128)(2,1)}), bf16[8,3,14336]{2,1,0:T(4,128)(2,1)S(1)}, u32[]{:S(2)}, u32[]{:S(2)}) async-start(bf16[8,3,14336]{2,1,0:T(4,128)(2,1)} %shard_map.123), calls=%async_computation | async-start | bytes 1835008 | tf_op jit(solution)/shard_map/all_to_all | solution.py:328
  34.8 2.0 collective-permute-start.28
  36.8 4.0 %collective-permute-start.29 = (bf16[24,7168]{1,0:T(8,128)(2,1)S(1)}, bf16[24,7168]{1,0:T(8,128)(2,1)}, u32[]{:S(2)}, u32[]{:S(2)}) collective-permute-start(bf16[24,7168]{1,0:T(8,128)(2,1)S(1)} %shard_map.127.refs_0_), channel_id=1, source_target_pairs={{0,7},{1,0},{2,1},{3,2},{4,3},{5,4},{6,5},{7,6},{8,15},{9,8},{10,9... | collective-permute-start | bytes 1032200 | tf_op jit(solution)/shard_map/ppermute | solution.py:21
  40.8 6.9 %collective-permute-done.28.refs_1_ = bf16[24,7168]{1,0:T(8,128)(2,1)S(1)} collective-permute-done((bf16[24,7168]{1,0:T(8,128)(2,1)S(1)}, bf16[24,7168]{1,0:T(8,128)(2,1)S(1)}, u32[]{:S(2)}, u32[]{:S(2)}) %collective-permute-start.28) | collective-permute-done | bytes 344096 | tf_op jit(solution)/shard_map/ppermute | solution.py:21
  47.7 3.2 %collective-permute-start.31 = (bf16[24,7168]{1,0:T(8,128)(2,1)}, bf16[24,7168]{1,0:T(8,128)(2,1)}, u32[]{:S(2)}, u32[]{:S(2)}) collective-permute-start(bf16[24,7168]{1,0:T(8,128)(2,1)} %collective-permute-done.29.refs_2_), channel_id=1, source_target_pairs={{0,7},{1,0},{2,1},{3,2},{4,3},{5,4},{6,5},{7,6},{8,15},{9,8},{10,9... | collective-permute-start | bytes 1032200 | tf_op jit(solution)/shard_map/ppermute | solution.py:21
  51.5 3.2 %collective-permute-start.22 = (bf16[24,7168]{1,0:T(8,128)(2,1)S(1)}, bf16[24,7168]{1,0:T(8,128)(2,1)S(1)}, u32[]{:S(2)}, u32[]{:S(2)}) collective-permute-start(bf16[24,7168]{1,0:T(8,128)(2,1)S(1)} %get-tuple-element.55.refs_0_), channel_id=1, source_target_pairs={{0,7},{1,0},{2,1},{3,2},{4,3},{5,4},{6,5},{7,6},{8,15},{9,8},{10,9... | collective-permute-start | bytes 1032200 | tf_op jit(solution)/shard_map/ppermute | solution.py:21
  56.0 4.1 %collective-permute-done.30.refs_3_ = bf16[24,7168]{1,0:T(8,128)(2,1)} collective-permute-done((bf16[24,7168]{1,0:T(8,128)(2,1)S(1)}, bf16[24,7168]{1,0:T(8,128)(2,1)}, u32[]{:S(2)}, u32[]{:S(2)}) %collective-permute-start.30) | collective-permute-done | bytes 344096 | tf_op jit(solution)/shard_map/ppermute | solution.py:21
  60.0 7.3 %collective-permute-done.21.refs_1_ = bf16[24,7168]{1,0:T(8,128)(2,1)S(1)} collective-permute-done((bf16[24,7168]{1,0:T(8,128)(2,1)S(1)}, bf16[24,7168]{1,0:T(8,128)(2,1)S(1)}, u32[]{:S(2)}, u32[]{:S(2)}) %collective-permute-start.21) | collective-permute-done | bytes 344096 | tf_op jit(solution)/shard_map/ppermute | solution.py:21
  67.6 1.8 collective-permute-start.23
  69.3 5.1 %collective-permute-done.6.refs_2_ = bf16[24,7168]{1,0:T(8,128)(2,1)S(1)} collective-permute-done((bf16[24,7168]{1,0:T(8,128)(2,1)S(1)}, bf16[24,7168]{1,0:T(8,128)(2,1)S(1)}, u32[]{:S(2)}, u32[]{:S(2)}) %collective-permute-start.6) | collective-permute-done | bytes 344096 | tf_op jit(solution)/shard_map/ppermute | solution.py:21
  74.4 3.7 %collective-permute-start.24 = (bf16[24,7168]{1,0:T(8,128)(2,1)S(1)}, bf16[24,7168]{1,0:T(8,128)(2,1)S(1)}, u32[]{:S(2)}, u32[]{:S(2)}) collective-permute-start(bf16[24,7168]{1,0:T(8,128)(2,1)S(1)} %collective-permute-done.22.refs_2_), channel_id=1, source_target_pairs={{0,7},{1,0},{2,1},{3,2},{4,3},{5,4},{6,5},{7,6},{8,15},{9,8},{10,9... | collective-permute-start | bytes 1032200 | tf_op jit(solution)/shard_map/ppermute | solution.py:21
  78.2 3.9 %collective-permute-done.32.refs_5_ = bf16[24,7168]{1,0:T(8,128)(2,1)S(1)} collective-permute-done((bf16[24,7168]{1,0:T(8,128)(2,1)}, bf16[24,7168]{1,0:T(8,128)(2,1)S(1)}, u32[]{:S(2)}, u32[]{:S(2)}) %collective-permute-start.32) | collective-permute-done | bytes 344096 | tf_op jit(solution)/shard_map/ppermute | solution.py:21
  82.1 7.4 %collective-permute-done.23.refs_3_ = bf16[24,7168]{1,0:T(8,128)(2,1)S(1)} collective-permute-done((bf16[24,7168]{1,0:T(8,128)(2,1)S(1)}, bf16[24,7168]{1,0:T(8,128)(2,1)S(1)}, u32[]{:S(2)}, u32[]{:S(2)}) %collective-permute-start.23) | collective-permute-done | bytes 344096 | tf_op jit(solution)/shard_map/ppermute | solution.py:21
  89.4 3.9 %collective-permute-done.10.refs_4_ = bf16[24,7168]{1,0:T(8,128)(2,1)S(1)} collective-permute-done((bf16[24,7168]{1,0:T(8,128)(2,1)S(1)}, bf16[24,7168]{1,0:T(8,128)(2,1)S(1)}, u32[]{:S(2)}, u32[]{:S(2)}) %collective-permute-start.10) | collective-permute-done | bytes 344096 | tf_op jit(solution)/shard_map/ppermute | solution.py:21
  93.3 3.5 %collective-permute-done.7.refs_3_ = bf16[24,7168]{1,0:T(8,128)(2,1)S(1)} collective-permute-done((bf16[24,7168]{1,0:T(8,128)(2,1)S(1)}, bf16[24,7168]{1,0:T(8,128)(2,1)S(1)}, u32[]{:S(2)}, u32[]{:S(2)}) %collective-permute-start.7) | collective-permute-done | bytes 344096 | tf_op jit(solution)/shard_map/ppermute | solution.py:21
  97.1 7.1 %collective-permute-done.34.refs_7_ = bf16[24,7168]{1,0:T(8,128)(2,1)S(1)} collective-permute-done((bf16[24,7168]{1,0:T(8,128)(2,1)S(1)}, bf16[24,7168]{1,0:T(8,128)(2,1)S(1)}, u32[]{:S(2)}, u32[]{:S(2)}) %collective-permute-start.34) | collective-permute-done | bytes 344096 | tf_op jit(solution)/shard_map/ppermute | solution.py:21
  104.4 4.2 %collective-permute-done.25.refs_5_ = bf16[24,7168]{1,0:T(8,128)(2,1)S(1)} collective-permute-done((bf16[24,7168]{1,0:T(8,128)(2,1)S(1)}, bf16[24,7168]{1,0:T(8,128)(2,1)S(1)}, u32[]{:S(2)}, u32[]{:S(2)}) %collective-permute-start.25) | collective-permute-done | bytes 344096 | tf_op jit(solution)/shard_map/ppermute | solution.py:21
  108.6 1.5 copy-done.1
  110.1 3.3 %shard_map.128 = (f32[24,128]{1,0:T(8,128)S(1)}, f32[24,128]{1,0:T(8,128)S(1)}, f32[24,128]{1,0:T(8,128)S(1)}, f32[24,128]{1,0:T(8,128)S(1)}, f32[24,128]{1,0:T(...) custom-call(bf16[24,7168]{1,0:T(8,128)(2,1)S(1)} %shard_map.127.refs, ...), custom_call_target="tpu_custom_call" | custom-call | tf_op jit(solution)/shard_map/pallas_call | solution.py:25
  113.5 3.3 %collective-permute-start.13 = (bf16[24,7168]{1,0:T(8,128)(2,1)S(1)}, bf16[24,7168]{1,0:T(8,128)(2,1)S(1)}, u32[]{:S(2)}, u32[]{:S(2)}) collective-permute-start(bf16[24,7168]{1,0:T(8,128)(2,1)S(1)} %collective-permute-done.12.refs_6_), channel_id=1, source_target_pairs={{0,7},{1,0},{2,1},{3,2},{4,3},{5,4},{6,5},{7,6},{8,15},{9,8},{10,9... | collective-permute-start | bytes 1032200 | tf_op jit(solution)/shard_map/ppermute | solution.py:21
  116.8 2.8 %collective-permute-done.27.refs_7_ = bf16[24,7168]{1,0:T(8,128)(2,1)S(1)} collective-permute-done((bf16[24,7168]{1,0:T(8,128)(2,1)S(1)}, bf16[24,7168]{1,0:T(8,128)(2,1)S(1)}, u32[]{:S(2)}, u32[]{:S(2)}) %collective-permute-start.27) | collective-permute-done | bytes 344096 | tf_op jit(solution)/shard_map/ppermute | solution.py:21
  119.7 4.2 %shard_map.129 = (bf16[24,7168]{1,0:T(8,128)(2,1)S(1)}, bf16[24,7168]{1,0:T(8,128)(2,1)S(1)}, bf16[24,7168]{1,0:T(8,128)(2,1)S(1)}, bf16[24,7168]{1,0:T(8,128)(2...) custom-call(bf16[24,7168]{1,0:T(8,128)(2,1)S(1)} %get-tuple-element., ...), custom_call_target="tpu_custom_call" | custom-call | tf_op jit(solution)/shard_map/pallas_call | solution.py:25
  124.0 2.0 %collective-permute-start.35 = (bf16[24,7168]{1,0:T(8,128)(2,1)S(1)}, bf16[24,7168]{1,0:T(8,128)(2,1)S(1)}, u32[]{:S(2)}, u32[]{:S(2)}) collective-permute-start(bf16[24,7168]{1,0:T(8,128)(2,1)S(1)} %get-tuple-element.73), channel_id=1, source_target_pairs={{0,1},{1,2},{2,3},{3,4},{4,5},{5,6},{6,7},{7,0},{8,9},{9,10},{10,1... | collective-permute-start | bytes 1032200 | tf_op jit(solution)/shard_map/ppermute | solution.py:21
  126.0 3.7 %shard_map.125 = (bf16[24,7168]{1,0:T(8,128)(2,1)S(1)}, bf16[24,7168]{1,0:T(8,128)(2,1)S(1)}, bf16[24,7168]{1,0:T(8,128)(2,1)S(1)}, bf16[24,7168]{1,0:T(8,128)(2...) custom-call(bf16[24,7168]{1,0:T(8,128)(2,1)S(1)} %get-tuple-element., ...), custom_call_target="tpu_custom_call" | custom-call | tf_op jit(solution)/shard_map/pallas_call | solution.py:25
  129.7 2.2 %collective-permute-start.18 = (bf16[24,7168]{1,0:T(8,128)(2,1)S(1)}, bf16[24,7168]{1,0:T(8,128)(2,1)S(1)}, u32[]{:S(2)}, u32[]{:S(2)}) collective-permute-start(bf16[24,7168]{1,0:T(8,128)(2,1)S(1)} %get-tuple-element.52), channel_id=1, source_target_pairs={{0,1},{1,2},{2,3},{3,4},{4,5},{5,6},{6,7},{7,0},{8,9},{9,10},{10,1... | collective-permute-start | bytes 1032200 | tf_op jit(solution)/shard_map/ppermute | solution.py:21
  134.1 1.9 collective-permute-start.40
  137.1 6.3 %collective-permute-done.18 = bf16[24,7168]{1,0:T(8,128)(2,1)S(1)} collective-permute-done((bf16[24,7168]{1,0:T(8,128)(2,1)S(1)}, bf16[24,7168]{1,0:T(8,128)(2,1)S(1)}, u32[]{:S(2)}, u32[]{:S(2)}) %collective-permute-start.18) | collective-permute-done | bytes 344096 | tf_op jit(solution)/shard_map/ppermute | solution.py:21
  144.5 2.4 %collective-permute-start.15 = (bf16[24,7168]{1,0:T(8,128)(2,1)S(1)}, bf16[24,7168]{1,0:T(8,128)(2,1)S(1)}, u32[]{:S(2)}, u32[]{:S(2)}) collective-permute-start(bf16[24,7168]{1,0:T(8,128)(2,1)S(1)} %add_convert_fusion.9), channel_id=1, source_target_pairs={{0,7},{1,0},{2,1},{3,2},{4,3},{5,4},{6,5},{7,6},{8,15},{9,8},{10,9... | collective-permute-start | bytes 1032200 | tf_op jit(solution)/shard_map/ppermute | solution.py:21
  146.9 3.3 %collective-permute-done.40 = bf16[24,7168]{1,0:T(8,128)(2,1)S(1)} collective-permute-done((bf16[24,7168]{1,0:T(8,128)(2,1)S(1)}, bf16[24,7168]{1,0:T(8,128)(2,1)S(1)}, u32[]{:S(2)}, u32[]{:S(2)}) %collective-permute-start.40) | collective-permute-done | bytes 344096 | tf_op jit(solution)/shard_map/ppermute | solution.py:21
  150.3 2.4 %collective-permute-start.41 = (bf16[24,7168]{1,0:T(8,128)(2,1)S(1)}, bf16[24,7168]{1,0:T(8,128)(2,1)S(1)}, u32[]{:S(2)}, u32[]{:S(2)}) collective-permute-start(bf16[24,7168]{1,0:T(8,128)(2,1)S(1)} %add_convert_fusion), channel_id=1, source_target_pairs={{0,7},{1,0},{2,1},{3,2},{4,3},{5,4},{6,5},{7,6},{8,15},{9,8},{10,9... | collective-permute-start | bytes 1032200 | tf_op jit(solution)/shard_map/ppermute | solution.py:21
  153.0 5.2 %collective-permute-done.19 = bf16[24,7168]{1,0:T(8,128)(2,1)S(1)} collective-permute-done((bf16[24,7168]{1,0:T(8,128)(2,1)S(1)}, bf16[24,7168]{1,0:T(8,128)(2,1)S(1)}, u32[]{:S(2)}, u32[]{:S(2)}) %collective-permute-start.19) | collective-permute-done | bytes 344096 | tf_op jit(solution)/shard_map/ppermute | solution.py:21
  159.3 2.4 %collective-permute-start.16 = (bf16[24,7168]{1,0:T(8,128)(2,1)S(1)}, bf16[24,7168]{1,0:T(8,128)(2,1)S(1)}, u32[]{:S(2)}, u32[]{:S(2)}) collective-permute-start(bf16[24,7168]{1,0:T(8,128)(2,1)S(1)} %add_convert_fusion.8), channel_id=1, source_target_pairs={{0,7},{1,0},{2,1},{3,2},{4,3},{5,4},{6,5},{7,6},{8,15},{9,8},{10,9... | collective-permute-start | bytes 1032200 | tf_op jit(solution)/shard_map/ppermute | solution.py:21
  161.7 3.8 %collective-permute-done.37 = bf16[24,7168]{1,0:T(8,128)(2,1)S(1)} collective-permute-done((bf16[24,7168]{1,0:T(8,128)(2,1)S(1)}, bf16[24,7168]{1,0:T(8,128)(2,1)S(1)}, u32[]{:S(2)}, u32[]{:S(2)}) %collective-permute-start.37) | collective-permute-done | bytes 344096 | tf_op jit(solution)/shard_map/ppermute | solution.py:21
  166.6 2.9 %collective-permute-done.16 = bf16[24,7168]{1,0:T(8,128)(2,1)S(1)} collective-permute-done((bf16[24,7168]{1,0:T(8,128)(2,1)S(1)}, bf16[24,7168]{1,0:T(8,128)(2,1)S(1)}, u32[]{:S(2)}, u32[]{:S(2)}) %collective-permute-start.16) | collective-permute-done | bytes 344096 | tf_op jit(solution)/shard_map/ppermute | solution.py:21
  169.5 1.7 collective-permute-start.17
  171.2 1.6 collective-permute-done.20.refs_2_
  172.9 4.1 %collective-permute-done.38.refs_4_ = bf16[24,7168]{1,0:T(8,128)(2,1)S(1)} collective-permute-done((bf16[24,7168]{1,0:T(8,128)(2,1)S(1)}, bf16[24,7168]{1,0:T(8,128)(2,1)S(1)}, u32[]{:S(2)}, u32[]{:S(2)}) %collective-permute-start.38) | collective-permute-done | bytes 344096 | tf_op jit(solution)/shard_map/ppermute | solution.py:21
  177.6 18.1 %all_to_all.15.back_ref = bf16[8,3,14336]{2,1,0:T(4,128)(2,1)S(1)} all-to-all(bf16[8,3,14336]{2,1,0:T(4,128)(2,1)S(1)} %shard_map.130), channel_id=1, replica_groups=mesh['pp'=4,'e'=8,'k'=8] {'e'}, dimensions={0} | all-to-all | bytes 1376256 | tf_op jit(solution)/shard_map/all_to_all | solution.py:328
  195.7 3.5 %shard_map.131 = (bf16[64,7168]{1,0:T(8,128)(2,1)}, bf16[64,7168]{1,0:T(8,128)(2,1)}) custom-call(bf16[8,3,14336]{2,1,0:T(4,128)(2,1)S(1)} %all_to_all.15.back_ref, bf16[64,7168]{1,0:T(8,128)(2,1)S(1)} %collective-permute-done.8.a_ref, s32[1,64]{1,0:T(1,128)S(1)} %bitcast.30, f32[1,64]{1,0:T(1,128)S(1)} %bitcast.31, bf16[64,7168]{1,0:T(8,128)(2,1)S(1)} %bitcast.21, ...), custom_call_target="tpu_custom_call" | custom-call | tf_op jit(solution)/shard_map/pallas_call | solution.py:380
  (89 shorter events, 13.2 us)
Async XLA Ops:
  0.6 3.2 %collective-permute-start.1 = (s32[1,64]{1,0:T(1,128)}, s32[1,64]{1,0:T(1,128)S(1)}, u32[]{:S(2)}, u32[]{:S(2)}) collective-permute-start(s32[1,64]{1,0:T(1,128)} %bitcast.26), channel_id=1, source_target_pairs={{0,64},{64,128},{128,192},{192,0},{1,65},{65,129},{129,193},{193,1... | collective-permute-start | bytes 776 | tf_op jit(solution)/shard_map/ppermute | solution.py:21
  0.7 3.2 %collective-permute-start = (s32[1,64]{1,0:T(1,128)}, s32[1,64]{1,0:T(1,128)S(1)}, u32[]{:S(2)}, u32[]{:S(2)}) collective-permute-start(s32[1,64]{1,0:T(1,128)} %bitcast.29), channel_id=1, source_target_pairs={{0,192},{64,0},{128,64},{192,128},{1,193},{65,1},{129,65},{193,129... | collective-permute-start | bytes 776 | tf_op jit(solution)/shard_map/ppermute | solution.py:21
  2.5 3.1 %collective-permute-start.2 = (f32[1,64]{1,0:T(1,128)}, f32[1,64]{1,0:T(1,128)S(1)}, u32[]{:S(2)}, u32[]{:S(2)}) collective-permute-start(f32[1,64]{1,0:T(1,128)} %bitcast.34), channel_id=1, source_target_pairs={{0,64},{64,128},{128,192},{192,0},{1,65},{65,129},{129,193},{193,1... | collective-permute-start | bytes 776 | tf_op jit(solution)/shard_map/ppermute | solution.py:21
  9.3 11.7 %collective-permute-start.3 = (bf16[24,7168]{1,0:T(8,128)(2,1)S(1)}, bf16[24,7168]{1,0:T(8,128)(2,1)S(1)}, u32[]{:S(2)}, u32[]{:S(2)}) collective-permute-start(bf16[24,7168]{1,0:T(8,128)(2,1)S(1)} %get-tuple-element.43), channel_id=1, source_target_pairs={{0,64},{64,128},{128,192},{192,0},{1,65},{65,129},{129,193},{193,1... | collective-permute-start | bytes 1032200 | tf_op jit(solution)/shard_map/ppermute | solution.py:21
  9.4 11.6 %collective-permute-start.4 = (bf16[24,7168]{1,0:T(8,128)(2,1)S(1)}, bf16[24,7168]{1,0:T(8,128)(2,1)S(1)}, u32[]{:S(2)}, u32[]{:S(2)}) collective-permute-start(bf16[24,7168]{1,0:T(8,128)(2,1)S(1)} %get-tuple-element.44), channel_id=1, source_target_pairs={{0,192},{64,0},{128,64},{192,128},{1,193},{65,1},{129,65},{193,129... | collective-permute-start | bytes 1032200 | tf_op jit(solution)/shard_map/ppermute | solution.py:21
  13.6 16.1 %all-to-all-start.1 = ((bf16[8,3,7168]{2,1,0:T(4,128)(2,1)}), bf16[8,3,7168]{2,1,0:T(4,128)(2,1)S(1)}, u32[]{:S(2)}, u32[]{:S(2)}) async-start(bf16[8,3,7168]{2,1,0:T(4,128)(2,1)} %shard_map.126), calls=%async_computation.1 | async-start | bytes 917504 | tf_op jit(solution)/shard_map/all_to_all | solution.py:328
  22.5 86.1 %copy-start = (bf16[1,1,7168,128]{3,2,1,0:T(8,128)(2,1)S(1)}, bf16[1,1,7168,128]{3,2,1,0:T(8,128)(2,1)}, u32[]{:S(2)}) copy-start(bf16[1,1,7168,128]{3,2,1,0:T(8,128)(2,1)} %param.19) | copy-start | bytes 5505028
  29.7 21.3 %all-to-all-start = ((bf16[8,3,14336]{2,1,0:T(4,128)(2,1)}), bf16[8,3,14336]{2,1,0:T(4,128)(2,1)S(1)}, u32[]{:S(2)}, u32[]{:S(2)}) async-start(bf16[8,3,14336]{2,1,0:T(4,128)(2,1)} %shard_map.123), calls=%async_computation | async-start | bytes 1835008 | tf_op jit(solution)/shard_map/all_to_all | solution.py:328
  34.8 12.9 %collective-permute-start.28 = (bf16[24,7168]{1,0:T(8,128)(2,1)S(1)}, bf16[24,7168]{1,0:T(8,128)(2,1)S(1)}, u32[]{:S(2)}, u32[]{:S(2)}) collective-permute-start(bf16[24,7168]{1,0:T(8,128)(2,1)S(1)} %shard_map.127.refs_0_), channel_id=1, source_target_pairs={{0,1},{1,2},{2,3},{3,4},{4,5},{5,6},{6,7},{7,0},{8,9},{9,10},{10,1... | collective-permute-start | bytes 1032200 | tf_op jit(solution)/shard_map/ppermute | solution.py:21
  36.8 10.9 %collective-permute-start.29 = (bf16[24,7168]{1,0:T(8,128)(2,1)S(1)}, bf16[24,7168]{1,0:T(8,128)(2,1)}, u32[]{:S(2)}, u32[]{:S(2)}) collective-permute-start(bf16[24,7168]{1,0:T(8,128)(2,1)S(1)} %shard_map.127.refs_0_), channel_id=1, source_target_pairs={{0,7},{1,0},{2,1},{3,2},{4,3},{5,4},{6,5},{7,6},{8,15},{9,8},{10,9... | collective-permute-start | bytes 1032200 | tf_op jit(solution)/shard_map/ppermute | solution.py:21
  47.7 12.3 %collective-permute-start.30 = (bf16[24,7168]{1,0:T(8,128)(2,1)S(1)}, bf16[24,7168]{1,0:T(8,128)(2,1)}, u32[]{:S(2)}, u32[]{:S(2)}) collective-permute-start(bf16[24,7168]{1,0:T(8,128)(2,1)S(1)} %collective-permute-done.28.refs_1_), channel_id=1, source_target_pairs={{0,1},{1,2},{2,3},{3,4},{4,5},{5,6},{6,7},{7,0},{8,9},{9,10},{10,1... | collective-permute-start | bytes 1032200 | tf_op jit(solution)/shard_map/ppermute | solution.py:21
  47.7 12.3 %collective-permute-start.31 = (bf16[24,7168]{1,0:T(8,128)(2,1)}, bf16[24,7168]{1,0:T(8,128)(2,1)}, u32[]{:S(2)}, u32[]{:S(2)}) collective-permute-start(bf16[24,7168]{1,0:T(8,128)(2,1)} %collective-permute-done.29.refs_2_), channel_id=1, source_target_pairs={{0,7},{1,0},{2,1},{3,2},{4,3},{5,4},{6,5},{7,6},{8,15},{9,8},{10,9... | collective-permute-start | bytes 1032200 | tf_op jit(solution)/shard_map/ppermute | solution.py:21
  51.4 15.9 %collective-permute-start.21 = (bf16[24,7168]{1,0:T(8,128)(2,1)S(1)}, bf16[24,7168]{1,0:T(8,128)(2,1)S(1)}, u32[]{:S(2)}, u32[]{:S(2)}) collective-permute-start(bf16[24,7168]{1,0:T(8,128)(2,1)S(1)} %get-tuple-element.55.refs_0_), channel_id=1, source_target_pairs={{0,1},{1,2},{2,3},{3,4},{4,5},{5,6},{6,7},{7,0},{8,9},{9,10},{10,1... | collective-permute-start | bytes 1032200 | tf_op jit(solution)/shard_map/ppermute | solution.py:21
  51.5 16.1 %collective-permute-start.22 = (bf16[24,7168]{1,0:T(8,128)(2,1)S(1)}, bf16[24,7168]{1,0:T(8,128)(2,1)S(1)}, u32[]{:S(2)}, u32[]{:S(2)}) collective-permute-start(bf16[24,7168]{1,0:T(8,128)(2,1)S(1)} %get-tuple-element.55.refs_0_), channel_id=1, source_target_pairs={{0,7},{1,0},{2,1},{3,2},{4,3},{5,4},{6,5},{7,6},{8,15},{9,8},{10,9... | collective-permute-start | bytes 1032200 | tf_op jit(solution)/shard_map/ppermute | solution.py:21
  54.7 19.7 %collective-permute-start.6 = (bf16[24,7168]{1,0:T(8,128)(2,1)S(1)}, bf16[24,7168]{1,0:T(8,128)(2,1)S(1)}, u32[]{:S(2)}, u32[]{:S(2)}) collective-permute-start(bf16[24,7168]{1,0:T(8,128)(2,1)S(1)} %get-tuple-element.45.refs_0_), channel_id=1, source_target_pairs={{0,7},{1,0},{2,1},{3,2},{4,3},{5,4},{6,5},{7,6},{8,15},{9,8},{10,9... | collective-permute-start | bytes 1032200 | tf_op jit(solution)/shard_map/ppermute | solution.py:21
  60.0 18.1 %collective-permute-start.5 = (bf16[24,7168]{1,0:T(8,128)(2,1)S(1)}, bf16[24,7168]{1,0:T(8,128)(2,1)S(1)}, u32[]{:S(2)}, u32[]{:S(2)}) collective-permute-start(bf16[24,7168]{1,0:T(8,128)(2,1)S(1)} %get-tuple-element.45.refs_0_), channel_id=1, source_target_pairs={{0,1},{1,2},{2,3},{3,4},{4,5},{5,6},{6,7},{7,0},{8,9},{9,10},{10,1... | collective-permute-start | bytes 1032200 | tf_op jit(solution)/shard_map/ppermute | solution.py:21
  60.0 22.0 %collective-permute-start.32 = (bf16[24,7168]{1,0:T(8,128)(2,1)}, bf16[24,7168]{1,0:T(8,128)(2,1)S(1)}, u32[]{:S(2)}, u32[]{:S(2)}) collective-permute-start(bf16[24,7168]{1,0:T(8,128)(2,1)} %collective-permute-done.30.refs_3_), channel_id=1, source_target_pairs={{0,1},{1,2},{2,3},{3,4},{4,5},{5,6},{6,7},{7,0},{8,9},{9,10},{10,1... | collective-permute-start | bytes 1032200 | tf_op jit(solution)/shard_map/ppermute | solution.py:21
  67.3 14.8 %collective-permute-start.33 = (bf16[24,7168]{1,0:T(8,128)(2,1)}, bf16[24,7168]{1,0:T(8,128)(2,1)S(1)}, u32[]{:S(2)}, u32[]{:S(2)}) collective-permute-start(bf16[24,7168]{1,0:T(8,128)(2,1)} %collective-permute-done.31.refs_4_), channel_id=1, source_target_pairs={{0,7},{1,0},{2,1},{3,2},{4,3},{5,4},{6,5},{7,6},{8,15},{9,8},{10,9... | collective-permute-start | bytes 1032200 | tf_op jit(solution)/shard_map/ppermute | solution.py:21
  67.6 21.8 %collective-permute-start.23 = (bf16[24,7168]{1,0:T(8,128)(2,1)S(1)}, bf16[24,7168]{1,0:T(8,128)(2,1)S(1)}, u32[]{:S(2)}, u32[]{:S(2)}) collective-permute-start(bf16[24,7168]{1,0:T(8,128)(2,1)S(1)} %collective-permute-done.21.refs_1_), channel_id=1, source_target_pairs={{0,1},{1,2},{2,3},{3,4},{4,5},{5,6},{6,7},{7,0},{8,9},{9,10},{10,1... | collective-permute-start | bytes 1032200 | tf_op jit(solution)/shard_map/ppermute | solution.py:21
  74.4 15.0 %collective-permute-start.24 = (bf16[24,7168]{1,0:T(8,128)(2,1)S(1)}, bf16[24,7168]{1,0:T(8,128)(2,1)S(1)}, u32[]{:S(2)}, u32[]{:S(2)}) collective-permute-start(bf16[24,7168]{1,0:T(8,128)(2,1)S(1)} %collective-permute-done.22.refs_2_), channel_id=1, source_target_pairs={{0,7},{1,0},{2,1},{3,2},{4,3},{5,4},{6,5},{7,6},{8,15},{9,8},{10,9... | collective-permute-start | bytes 1032200 | tf_op jit(solution)/shard_map/ppermute | solution.py:21
  78.1 15.2 %collective-permute-start.10 = (bf16[24,7168]{1,0:T(8,128)(2,1)S(1)}, bf16[24,7168]{1,0:T(8,128)(2,1)S(1)}, u32[]{:S(2)}, u32[]{:S(2)}) collective-permute-start(bf16[24,7168]{1,0:T(8,128)(2,1)S(1)} %collective-permute-done.6.refs_2_), channel_id=1, source_target_pairs={{0,7},{1,0},{2,1},{3,2},{4,3},{5,4},{6,5},{7,6},{8,15},{9,8},{10,9... | collective-permute-start | bytes 1032200 | tf_op jit(solution)/shard_map/ppermute | solution.py:21
  82.0 14.7 %collective-permute-start.7 = (bf16[24,7168]{1,0:T(8,128)(2,1)S(1)}, bf16[24,7168]{1,0:T(8,128)(2,1)S(1)}, u32[]{:S(2)}, u32[]{:S(2)}) collective-permute-start(bf16[24,7168]{1,0:T(8,128)(2,1)S(1)} %collective-permute-done.5.refs_1_), channel_id=1, source_target_pairs={{0,1},{1,2},{2,3},{3,4},{4,5},{5,6},{6,7},{7,0},{8,9},{9,10},{10,1... | collective-permute-start | bytes 1032200 | tf_op jit(solution)/shard_map/ppermute | solution.py:21
  82.1 22.1 %collective-permute-start.34 = (bf16[24,7168]{1,0:T(8,128)(2,1)S(1)}, bf16[24,7168]{1,0:T(8,128)(2,1)S(1)}, u32[]{:S(2)}, u32[]{:S(2)}) collective-permute-start(bf16[24,7168]{1,0:T(8,128)(2,1)S(1)} %collective-permute-done.32.refs_5_), channel_id=1, source_target_pairs={{0,1},{1,2},{2,3},{3,4},{4,5},{5,6},{6,7},{7,0},{8,9},{9,10},{10,1... | collective-permute-start | bytes 1032200 | tf_op jit(solution)/shard_map/ppermute | solution.py:21
  89.4 19.2 %collective-permute-start.25 = (bf16[24,7168]{1,0:T(8,128)(2,1)S(1)}, bf16[24,7168]{1,0:T(8,128)(2,1)S(1)}, u32[]{:S(2)}, u32[]{:S(2)}) collective-permute-start(bf16[24,7168]{1,0:T(8,128)(2,1)S(1)} %collective-permute-done.23.refs_3_), channel_id=1, source_target_pairs={{0,1},{1,2},{2,3},{3,4},{4,5},{5,6},{6,7},{7,0},{8,9},{9,10},{10,1... | collective-permute-start | bytes 1032200 | tf_op jit(solution)/shard_map/ppermute | solution.py:21
  89.4 34.5 %collective-permute-start.8 = (bf16[64,7168]{1,0:T(8,128)(2,1)}, bf16[64,7168]{1,0:T(8,128)(2,1)S(1)}, u32[]{:S(2)}, u32[]{:S(2)}) collective-permute-start(bf16[64,7168]{1,0:T(8,128)(2,1)} %bitcast.22), channel_id=1, source_target_pairs={{0,64},{64,128},{128,192},{192,0},{1,65},{65,129},{129,193},{193,1... | collective-permute-start | bytes 2752520 | tf_op jit(solution)/shard_map/ppermute | solution.py:21
  93.3 30.6 %collective-permute-start.9 = (bf16[64,7168]{1,0:T(8,128)(2,1)}, bf16[64,7168]{1,0:T(8,128)(2,1)S(1)}, u32[]{:S(2)}, u32[]{:S(2)}) collective-permute-start(bf16[64,7168]{1,0:T(8,128)(2,1)} %bitcast.24), channel_id=1, source_target_pairs={{0,192},{64,0},{128,64},{192,128},{1,193},{65,1},{129,65},{193,129... | collective-permute-start | bytes 2752520 | tf_op jit(solution)/shard_map/ppermute | solution.py:21
  96.8 16.6 %collective-permute-start.26 = (bf16[24,7168]{1,0:T(8,128)(2,1)S(1)}, bf16[24,7168]{1,0:T(8,128)(2,1)S(1)}, u32[]{:S(2)}, u32[]{:S(2)}) collective-permute-start(bf16[24,7168]{1,0:T(8,128)(2,1)S(1)} %collective-permute-done.24.refs_4_), channel_id=1, source_target_pairs={{0,7},{1,0},{2,1},{3,2},{4,3},{5,4},{6,5},{7,6},{8,15},{9,8},{10,9... | collective-permute-start | bytes 1032200 | tf_op jit(solution)/shard_map/ppermute | solution.py:21
  104.2 9.3 %collective-permute-start.12 = (bf16[24,7168]{1,0:T(8,128)(2,1)S(1)}, bf16[24,7168]{1,0:T(8,128)(2,1)S(1)}, u32[]{:S(2)}, u32[]{:S(2)}) collective-permute-start(bf16[24,7168]{1,0:T(8,128)(2,1)S(1)} %collective-permute-done.10.refs_4_), channel_id=1, source_target_pairs={{0,7},{1,0},{2,1},{3,2},{4,3},{5,4},{6,5},{7,6},{8,15},{9,8},{10,9... | collective-permute-start | bytes 1032200 | tf_op jit(solution)/shard_map/ppermute | solution.py:21
  108.6 11.1 %collective-permute-start.27 = (bf16[24,7168]{1,0:T(8,128)(2,1)S(1)}, bf16[24,7168]{1,0:T(8,128)(2,1)S(1)}, u32[]{:S(2)}, u32[]{:S(2)}) collective-permute-start(bf16[24,7168]{1,0:T(8,128)(2,1)S(1)} %collective-permute-done.25.refs_5_), channel_id=1, source_target_pairs={{0,1},{1,2},{2,3},{3,4},{4,5},{5,6},{6,7},{7,0},{8,9},{9,10},{10,1... | collective-permute-start | bytes 1032200 | tf_op jit(solution)/shard_map/ppermute | solution.py:21
  113.4 12.6 %collective-permute-start.11 = (bf16[24,7168]{1,0:T(8,128)(2,1)S(1)}, bf16[24,7168]{1,0:T(8,128)(2,1)S(1)}, u32[]{:S(2)}, u32[]{:S(2)}) collective-permute-start(bf16[24,7168]{1,0:T(8,128)(2,1)S(1)} %collective-permute-done.7.refs_3_), channel_id=1, source_target_pairs={{0,1},{1,2},{2,3},{3,4},{4,5},{5,6},{6,7},{7,0},{8,9},{9,10},{10,1... | collective-permute-start | bytes 1032200 | tf_op jit(solution)/shard_map/ppermute | solution.py:21
  113.5 12.5 %collective-permute-start.13 = (bf16[24,7168]{1,0:T(8,128)(2,1)S(1)}, bf16[24,7168]{1,0:T(8,128)(2,1)S(1)}, u32[]{:S(2)}, u32[]{:S(2)}) collective-permute-start(bf16[24,7168]{1,0:T(8,128)(2,1)S(1)} %collective-permute-done.12.refs_6_), channel_id=1, source_target_pairs={{0,7},{1,0},{2,1},{3,2},{4,3},{5,4},{6,5},{7,6},{8,15},{9,8},{10,9... | collective-permute-start | bytes 1032200 | tf_op jit(solution)/shard_map/ppermute | solution.py:21
  123.9 10.1 %collective-permute-start.39 = (bf16[24,7168]{1,0:T(8,128)(2,1)S(1)}, bf16[24,7168]{1,0:T(8,128)(2,1)S(1)}, u32[]{:S(2)}, u32[]{:S(2)}) collective-permute-start(bf16[24,7168]{1,0:T(8,128)(2,1)S(1)} %get-tuple-element.77), channel_id=1, source_target_pairs={{0,7},{1,0},{2,1},{3,2},{4,3},{5,4},{6,5},{7,6},{8,15},{9,8},{10,9... | collective-permute-start | bytes 1032200 | tf_op jit(solution)/shard_map/ppermute | solution.py:21
  124.0 12.0 %collective-permute-start.35 = (bf16[24,7168]{1,0:T(8,128)(2,1)S(1)}, bf16[24,7168]{1,0:T(8,128)(2,1)S(1)}, u32[]{:S(2)}, u32[]{:S(2)}) collective-permute-start(bf16[24,7168]{1,0:T(8,128)(2,1)S(1)} %get-tuple-element.73), channel_id=1, source_target_pairs={{0,1},{1,2},{2,3},{3,4},{4,5},{5,6},{6,7},{7,0},{8,9},{9,10},{10,1... | collective-permute-start | bytes 1032200 | tf_op jit(solution)/shard_map/ppermute | solution.py:21
  129.7 13.7 %collective-permute-start.18 = (bf16[24,7168]{1,0:T(8,128)(2,1)S(1)}, bf16[24,7168]{1,0:T(8,128)(2,1)S(1)}, u32[]{:S(2)}, u32[]{:S(2)}) collective-permute-start(bf16[24,7168]{1,0:T(8,128)(2,1)S(1)} %get-tuple-element.52), channel_id=1, source_target_pairs={{0,1},{1,2},{2,3},{3,4},{4,5},{5,6},{6,7},{7,0},{8,9},{9,10},{10,1... | collective-permute-start | bytes 1032200 | tf_op jit(solution)/shard_map/ppermute | solution.py:21
  131.9 12.6 %collective-permute-start.14 = (bf16[24,7168]{1,0:T(8,128)(2,1)S(1)}, bf16[24,7168]{1,0:T(8,128)(2,1)S(1)}, u32[]{:S(2)}, u32[]{:S(2)}) collective-permute-start(bf16[24,7168]{1,0:T(8,128)(2,1)S(1)} %get-tuple-element.48), channel_id=1, source_target_pairs={{0,7},{1,0},{2,1},{3,2},{4,3},{5,4},{6,5},{7,6},{8,15},{9,8},{10,9... | collective-permute-start | bytes 1032200 | tf_op jit(solution)/shard_map/ppermute | solution.py:21
  134.1 16.2 %collective-permute-start.40 = (bf16[24,7168]{1,0:T(8,128)(2,1)S(1)}, bf16[24,7168]{1,0:T(8,128)(2,1)S(1)}, u32[]{:S(2)}, u32[]{:S(2)}) collective-permute-start(bf16[24,7168]{1,0:T(8,128)(2,1)S(1)} %add_convert_fusion.1), channel_id=1, source_target_pairs={{0,7},{1,0},{2,1},{3,2},{4,3},{5,4},{6,5},{7,6},{8,15},{9,8},{10,9... | collective-permute-start | bytes 1032200 | tf_op jit(solution)/shard_map/ppermute | solution.py:21
  136.1 16.7 %collective-permute-start.36 = (bf16[24,7168]{1,0:T(8,128)(2,1)S(1)}, bf16[24,7168]{1,0:T(8,128)(2,1)S(1)}, u32[]{:S(2)}, u32[]{:S(2)}) collective-permute-start(bf16[24,7168]{1,0:T(8,128)(2,1)S(1)} %add_convert_fusion.4), channel_id=1, source_target_pairs={{0,1},{1,2},{2,3},{3,4},{4,5},{5,6},{6,7},{7,0},{8,9},{9,10},{10,1... | collective-permute-start | bytes 1032200 | tf_op jit(solution)/shard_map/ppermute | solution.py:21
  143.5 14.7 %collective-permute-start.19 = (bf16[24,7168]{1,0:T(8,128)(2,1)S(1)}, bf16[24,7168]{1,0:T(8,128)(2,1)S(1)}, u32[]{:S(2)}, u32[]{:S(2)}) collective-permute-start(bf16[24,7168]{1,0:T(8,128)(2,1)S(1)} %add_convert_fusion.6), channel_id=1, source_target_pairs={{0,1},{1,2},{2,3},{3,4},{4,5},{5,6},{6,7},{7,0},{8,9},{9,10},{10,1... | collective-permute-start | bytes 1032200 | tf_op jit(solution)/shard_map/ppermute | solution.py:21
  144.5 14.7 %collective-permute-start.15 = (bf16[24,7168]{1,0:T(8,128)(2,1)S(1)}, bf16[24,7168]{1,0:T(8,128)(2,1)S(1)}, u32[]{:S(2)}, u32[]{:S(2)}) collective-permute-start(bf16[24,7168]{1,0:T(8,128)(2,1)S(1)} %add_convert_fusion.9), channel_id=1, source_target_pairs={{0,7},{1,0},{2,1},{3,2},{4,3},{5,4},{6,5},{7,6},{8,15},{9,8},{10,9... | collective-permute-start | bytes 1032200 | tf_op jit(solution)/shard_map/ppermute | solution.py:21
  150.3 20.9 %collective-permute-start.41 = (bf16[24,7168]{1,0:T(8,128)(2,1)S(1)}, bf16[24,7168]{1,0:T(8,128)(2,1)S(1)}, u32[]{:S(2)}, u32[]{:S(2)}) collective-permute-start(bf16[24,7168]{1,0:T(8,128)(2,1)S(1)} %add_convert_fusion), channel_id=1, source_target_pairs={{0,7},{1,0},{2,1},{3,2},{4,3},{5,4},{6,5},{7,6},{8,15},{9,8},{10,9... | collective-permute-start | bytes 1032200 | tf_op jit(solution)/shard_map/ppermute | solution.py:21
  152.9 12.6 %collective-permute-start.37 = (bf16[24,7168]{1,0:T(8,128)(2,1)S(1)}, bf16[24,7168]{1,0:T(8,128)(2,1)S(1)}, u32[]{:S(2)}, u32[]{:S(2)}) collective-permute-start(bf16[24,7168]{1,0:T(8,128)(2,1)S(1)} %add_convert_fusion.3), channel_id=1, source_target_pairs={{0,1},{1,2},{2,3},{3,4},{4,5},{5,6},{6,7},{7,0},{8,9},{9,10},{10,1... | collective-permute-start | bytes 1032200 | tf_op jit(solution)/shard_map/ppermute | solution.py:21
  158.2 14.7 %collective-permute-start.20 = (bf16[24,7168]{1,0:T(8,128)(2,1)S(1)}, bf16[24,7168]{1,0:T(8,128)(2,1)S(1)}, u32[]{:S(2)}, u32[]{:S(2)}) collective-permute-start(bf16[24,7168]{1,0:T(8,128)(2,1)S(1)} %add_convert_fusion.5), channel_id=1, source_target_pairs={{0,1},{1,2},{2,3},{3,4},{4,5},{5,6},{6,7},{7,0},{8,9},{9,10},{10,1... | collective-permute-start | bytes 1032200 | tf_op jit(solution)/shard_map/ppermute | solution.py:21
  159.3 10.2 %collective-permute-start.16 = (bf16[24,7168]{1,0:T(8,128)(2,1)S(1)}, bf16[24,7168]{1,0:T(8,128)(2,1)S(1)}, u32[]{:S(2)}, u32[]{:S(2)}) collective-permute-start(bf16[24,7168]{1,0:T(8,128)(2,1)S(1)} %add_convert_fusion.8), channel_id=1, source_target_pairs={{0,7},{1,0},{2,1},{3,2},{4,3},{5,4},{6,5},{7,6},{8,15},{9,8},{10,9... | collective-permute-start | bytes 1032200 | tf_op jit(solution)/shard_map/ppermute | solution.py:21
  165.6 11.4 %collective-permute-start.38 = (bf16[24,7168]{1,0:T(8,128)(2,1)S(1)}, bf16[24,7168]{1,0:T(8,128)(2,1)S(1)}, u32[]{:S(2)}, u32[]{:S(2)}) collective-permute-start(bf16[24,7168]{1,0:T(8,128)(2,1)S(1)} %add_convert_fusion.2), channel_id=1, source_target_pairs={{0,1},{1,2},{2,3},{3,4},{4,5},{5,6},{6,7},{7,0},{8,9},{9,10},{10,1... | collective-permute-start | bytes 1032200 | tf_op jit(solution)/shard_map/ppermute | solution.py:21
  169.5 7.5 %collective-permute-start.17 = (bf16[24,7168]{1,0:T(8,128)(2,1)S(1)}, bf16[24,7168]{1,0:T(8,128)(2,1)S(1)}, u32[]{:S(2)}, u32[]{:S(2)}) collective-permute-start(bf16[24,7168]{1,0:T(8,128)(2,1)S(1)} %add_convert_fusion.7), channel_id=1, source_target_pairs={{0,7},{1,0},{2,1},{3,2},{4,3},{5,4},{6,5},{7,6},{8,15},{9,8},{10,9... | collective-permute-start | bytes 1032200 | tf_op jit(solution)/shard_map/ppermute | solution.py:21
  177.0 18.7 %copy-start.5 = (bf16[1,64,7168]{2,1,0:T(8,128)(2,1)S(1)}, bf16[1,64,7168]{2,1,0:T(8,128)(2,1)}, u32[]{:S(2)}) copy-start(bf16[1,64,7168]{2,1,0:T(8,128)(2,1)} %param.14) | copy-start | bytes 2752516
  177.0 18.7 %copy-start.9 = (f32[1,7168]{1,0:T(1,128)S(1)}, f32[1,7168]{1,0:T(1,128)}, u32[]{:S(2)}) copy-start(f32[1,7168]{1,0:T(1,128)} %gain_ref.5) | copy-start | bytes 86020
  177.0 18.7 %copy-start.11 = (s32[1,64,1]{1,2,0:T(1,128)S(1)}, s32[1,64,1]{1,2,0:T(1,128)}, u32[]{:S(2)}) copy-start(s32[1,64,1]{1,2,0:T(1,128)} %param.16) | copy-start | bytes 772
  (10 other events, 77.4 us)

commit v3 on v2

--- a/solution.py
+++ b/solution.py
@@ -95,32 +95,32 @@
     chunks(x_ref.shape[1], step, 0)
 
 
-def pick_kernel(experts, a_ref, a_ids_ref, b_ref, b_ids_ref, b_gates_ref, a_out, b_out):
+def pick_kernel(experts, a_ref, a_ids_ref, b_ref, b_ids_ref, a_out, b_out):
     shape = (experts, a_out.shape[0] // experts)
     a_select = selector(a_ids_ref, *shape).astype(BF16)
-    b_select = selector(b_ids_ref, *shape)
-    gate = jnp.sum(b_select * b_gates_ref[...], axis=1, keepdims=True)
-    b_select = b_select.astype(BF16)
+    b_select = selector(b_ids_ref, *shape).astype(BF16)
 
     def step(at, carry):
         part = pl.ds(at, CHUNK)
         a_rows = jnp.dot(a_select, a_ref[:, part], preferred_element_type=F32)
         a_out[:, part] = a_rows.astype(BF16)
         b_rows = jnp.dot(b_select, b_ref[:, part], preferred_element_type=F32)
-        b_out[:, part] = (b_rows * gate).astype(BF16)
+        b_out[:, part] = b_rows.astype(BF16)
         return carry
 
     chunks(a_ref.shape[1], step, 0)
 
 
-def pack_kernel(a_ref, gain_ref, b_ref, out_ref):
+def pack_kernel(a_ref, gain_ref, b_ref, ids_ref, gates_ref, out_ref):
     features = a_ref.shape[1]
+    select = selector(ids_ref, *out_ref.shape[:2])
+    gate = jnp.sum(select * gates_ref[...], axis=1, keepdims=True)
     scale = row_scale(a_ref)
 
     def step(at, carry):
         part = pl.ds(at, CHUNK)
         deal(out_ref, at, a_ref[:, part].astype(F32) * scale * gain_ref[:, part])
-        deal(out_ref, at + features, b_ref[:, part])
+        deal(out_ref, at + features, b_ref[:, part].astype(F32) * gate)
         return carry
 
     chunks(features, step, 0)
@@ -344,16 +344,20 @@
 
     rows = jax.ShapeDtypeStruct((experts * capacity, features), BF16)
     near_ids = shifted(fwd_ids, "pp", -1)
-    far_ids, far_gates = shifted(bwd_ids, "pp", 1), shifted(bwd_gates, "pp", 1)
+    far_ids = shifted(bwd_ids, "pp", 1)
     (bwd_send,) = call(norm_slots, [slots(features)], bwd_x, bwd_ids, norm_gain)
     (bwd_slots,) = call(unpack_kernel, [rows], exchange(bwd_send))
     fwd_rows, grad_rows = call(
         functools.partial(pick_kernel, experts),
         [rows, rows],
-        *(fwd_in[0], near_ids, bwd_grad[0], far_ids, far_gates),
+        *(fwd_in[0], near_ids, bwd_grad[0], far_ids),
     )
     fwd_rows, grad_rows = shifted(fwd_rows, "pp", 1), shifted(grad_rows, "pp", -1)
-    (send,) = call(pack_kernel, [slots(2 * features)], fwd_rows, norm_gain, grad_rows)
+    (send,) = call(
+        pack_kernel,
+        [slots(2 * features)],
+        *(fwd_rows, norm_gain, grad_rows, bwd_ids, bwd_gates),
+    )
     fwd_slots, grad_slots = call(unpack_kernel, [rows, rows], exchange(send))
     arrived = shifted(fwd_in[0], "pp", 1)
     upstream = shifted(bwd_grad[0], "pp", -1)

time: 200 us -> 199 us (level)
  waiting for transfers between devices: 94.5 us -> 91.7 us
    ppermute x42 -> x41, waiting for transfers between devices: 87.3 us -> 84.5 us  [shifted(): return lax.ppermute(block, axis, route)]
    ppermute x42 -> x41, starting transfers between devices: 47.4 us -> 48.9 us  [shifted(): return lax.ppermute(block, axis, route)]
    unnamed x28 -> x32, local copies, waits for them, and re-layouts: 3.9 us -> 4.82 us
  transfers between devices with their start and end apart: 44 -> 43, of which waited for: 23 -> 23; matrix products, arithmetic and copies ran while one was open for 0% -> 0% of each run, Pallas kernels for 8% -> 8%
where the time goes in v3:
time: 199 us; the launch traced here: 198 us
  waiting for transfers between devices  91.7 us (46%)
  starting transfers between devices  61.3 us (31%)
  Pallas kernels  20.5 us (10%)
  blocking collectives  17.9 us (9%)
  local copies, waits for them, and re-layouts  4.82 us (2%)
    ppermute x41, waiting for transfers between devices, shifted(): return lax.ppermute(block, axis, route)  84.5 us
    ppermute x41, starting transfers between devices, shifted(): return lax.ppermute(block, axis, route)  48.9 us
    all_to_all x1, blocking collectives, exchange(): return lax.all_to_all(slots, 'e', split_axis=0, concat_axis=0, tiled=True)  17.9 us
    pallas_call x9, Pallas kernels, call(): pl.pallas_call(kernel, out_shape=outs, in_specs=[pl.BlockSpec(memory_spac...  17 us
    all_to_all x2, starting transfers between devices, exchange(): return lax.all_to_all(slots, 'e', split_axis=0, concat_axis=0, tiled=True)  12.4 us
    all_to_all x2, waiting for transfers between devices, exchange(): return lax.all_to_all(slots, 'e', split_axis=0, concat_axis=0, tiled=True)  7.23 us
    unnamed x32, local copies, waits for them, and re-layouts  4.82 us
  transfers between devices with their start and end apart: 43, of which 23 were waited for; matrix products, arithmetic and copies ran while one was open for 0% of the time, Pallas kernels for 8%

profile of v3, /device:TPU:2, one launch (start us, length us, event | category | flops | bytes accessed | tf_op | source)
XLA Modules:
  0.0 198.0 jit_solution(4647174292460518928)
XLA Ops:
  0.7 1.7 collective-permute-start
  2.5 1.4 collective-permute-done.1.b_ids_ref
  7.6 1.7 collective-permute-start.2
  9.4 2.4 %shard_map.126 = bf16[8,3,7168]{2,1,0:T(4,128)(2,1)} custom-call(bf16[64,7168]{1,0:T(8,128)(2,1)S(1)} %bitcast.20, s32[1,64]{1,0:T(1,128)S(1)} %bitcast.27, f32[1,7168]{1,0:T(1,128)S(1)} %copy-done.9), custom_call_target="tpu_custom_call" | custom-call | tf_op jit(solution)/shard_map/pallas_call | solution.py:25
  11.9 7.5 %all-to-all-start.1 = ((bf16[8,3,7168]{2,1,0:T(4,128)(2,1)}), bf16[8,3,7168]{2,1,0:T(4,128)(2,1)S(1)}, u32[]{:S(2)}, u32[]{:S(2)}) async-start(bf16[8,3,7168]{2,1,0:T(4,128)(2,1)} %shard_map.126), calls=%async_computation.1 | async-start | bytes 917504 | tf_op jit(solution)/shard_map/all_to_all | solution.py:328
  21.1 7.2 %all-to-all-done.1.in_ref = bf16[8,3,7168]{2,1,0:T(4,128)(2,1)S(1)} async-done(((bf16[8,3,7168]{2,1,0:T(4,128)(2,1)}), bf16[8,3,7168]{2,1,0:T(4,128)(2,1)S(1)}, u32[]{:S(2)}, u32[]{:S(2)}) %all-to-all-start.1) | async-done | bytes 344096 | tf_op jit(solution)/shard_map/all_to_all | solution.py:328
  28.3 5.0 %all-to-all-start = ((bf16[8,3,14336]{2,1,0:T(4,128)(2,1)}), bf16[8,3,14336]{2,1,0:T(4,128)(2,1)S(1)}, u32[]{:S(2)}, u32[]{:S(2)}) async-start(bf16[8,3,14336]{2,1,0:T(4,128)(2,1)} %copy-done.4), calls=%async_computation | async-start | bytes 1835008 | tf_op jit(solution)/shard_map/all_to_all | solution.py:328
  33.5 2.0 %collective-permute-start.27 = (bf16[24,7168]{1,0:T(8,128)(2,1)S(1)}, bf16[24,7168]{1,0:T(8,128)(2,1)S(1)}, u32[]{:S(2)}, u32[]{:S(2)}) collective-permute-start(bf16[24,7168]{1,0:T(8,128)(2,1)S(1)} %shard_map.127.refs_0_), channel_id=1, source_target_pairs={{0,1},{1,2},{2,3},{3,4},{4,5},{5,6},{6,7},{7,0},{8,9},{9,10},{10,1... | collective-permute-start | bytes 1032200 | tf_op jit(solution)/shard_map/ppermute | solution.py:21
  35.5 4.0 %collective-permute-start.28 = (bf16[24,7168]{1,0:T(8,128)(2,1)S(1)}, bf16[24,7168]{1,0:T(8,128)(2,1)}, u32[]{:S(2)}, u32[]{:S(2)}) collective-permute-start(bf16[24,7168]{1,0:T(8,128)(2,1)S(1)} %shard_map.127.refs_0_), channel_id=1, source_target_pairs={{0,7},{1,0},{2,1},{3,2},{4,3},{5,4},{6,5},{7,6},{8,15},{9,8},{10,9... | collective-permute-start | bytes 1032200 | tf_op jit(solution)/shard_map/ppermute | solution.py:21
  39.5 7.1 %collective-permute-done.27.refs_1_ = bf16[24,7168]{1,0:T(8,128)(2,1)S(1)} collective-permute-done((bf16[24,7168]{1,0:T(8,128)(2,1)S(1)}, bf16[24,7168]{1,0:T(8,128)(2,1)S(1)}, u32[]{:S(2)}, u32[]{:S(2)}) %collective-permute-start.27) | collective-permute-done | bytes 344096 | tf_op jit(solution)/shard_map/ppermute | solution.py:21
  46.6 3.2 %collective-permute-start.30 = (bf16[24,7168]{1,0:T(8,128)(2,1)}, bf16[24,7168]{1,0:T(8,128)(2,1)}, u32[]{:S(2)}, u32[]{:S(2)}) collective-permute-start(bf16[24,7168]{1,0:T(8,128)(2,1)} %collective-permute-done.28.refs_2_), channel_id=1, source_target_pairs={{0,7},{1,0},{2,1},{3,2},{4,3},{5,4},{6,5},{7,6},{8,15},{9,8},{10,9... | collective-permute-start | bytes 1032200 | tf_op jit(solution)/shard_map/ppermute | solution.py:21
  50.4 3.2 %collective-permute-start.21 = (bf16[24,7168]{1,0:T(8,128)(2,1)S(1)}, bf16[24,7168]{1,0:T(8,128)(2,1)S(1)}, u32[]{:S(2)}, u32[]{:S(2)}) collective-permute-start(bf16[24,7168]{1,0:T(8,128)(2,1)S(1)} %get-tuple-element.55.refs_0_), channel_id=1, source_target_pairs={{0,7},{1,0},{2,1},{3,2},{4,3},{5,4},{6,5},{7,6},{8,15},{9,8},{10,9... | collective-permute-start | bytes 1032200 | tf_op jit(solution)/shard_map/ppermute | solution.py:21
  54.9 4.0 %collective-permute-done.29.refs_3_ = bf16[24,7168]{1,0:T(8,128)(2,1)} collective-permute-done((bf16[24,7168]{1,0:T(8,128)(2,1)S(1)}, bf16[24,7168]{1,0:T(8,128)(2,1)}, u32[]{:S(2)}, u32[]{:S(2)}) %collective-permute-start.29) | collective-permute-done | bytes 344096 | tf_op jit(solution)/shard_map/ppermute | solution.py:21
  58.9 7.3 %collective-permute-done.20.refs_1_ = bf16[24,7168]{1,0:T(8,128)(2,1)S(1)} collective-permute-done((bf16[24,7168]{1,0:T(8,128)(2,1)S(1)}, bf16[24,7168]{1,0:T(8,128)(2,1)S(1)}, u32[]{:S(2)}, u32[]{:S(2)}) %collective-permute-start.20) | collective-permute-done | bytes 344096 | tf_op jit(solution)/shard_map/ppermute | solution.py:21
  66.7 1.5 collective-permute-start.22
  68.2 5.1 %collective-permute-done.5.refs_2_ = bf16[24,7168]{1,0:T(8,128)(2,1)S(1)} collective-permute-done((bf16[24,7168]{1,0:T(8,128)(2,1)S(1)}, bf16[24,7168]{1,0:T(8,128)(2,1)S(1)}, u32[]{:S(2)}, u32[]{:S(2)}) %collective-permute-start.5) | collective-permute-done | bytes 344096 | tf_op jit(solution)/shard_map/ppermute | solution.py:21
  73.3 3.7 %collective-permute-start.23 = (bf16[24,7168]{1,0:T(8,128)(2,1)S(1)}, bf16[24,7168]{1,0:T(8,128)(2,1)S(1)}, u32[]{:S(2)}, u32[]{:S(2)}) collective-permute-start(bf16[24,7168]{1,0:T(8,128)(2,1)S(1)} %collective-permute-done.21.refs_2_), channel_id=1, source_target_pairs={{0,7},{1,0},{2,1},{3,2},{4,3},{5,4},{6,5},{7,6},{8,15},{9,8},{10,9... | collective-permute-start | bytes 1032200 | tf_op jit(solution)/shard_map/ppermute | solution.py:21
  77.0 3.9 %collective-permute-done.31.refs_5_ = bf16[24,7168]{1,0:T(8,128)(2,1)S(1)} collective-permute-done((bf16[24,7168]{1,0:T(8,128)(2,1)}, bf16[24,7168]{1,0:T(8,128)(2,1)S(1)}, u32[]{:S(2)}, u32[]{:S(2)}) %collective-permute-start.31) | collective-permute-done | bytes 344096 | tf_op jit(solution)/shard_map/ppermute | solution.py:21
  80.9 7.4 %collective-permute-done.22.refs_3_ = bf16[24,7168]{1,0:T(8,128)(2,1)S(1)} collective-permute-done((bf16[24,7168]{1,0:T(8,128)(2,1)S(1)}, bf16[24,7168]{1,0:T(8,128)(2,1)S(1)}, u32[]{:S(2)}, u32[]{:S(2)}) %collective-permute-start.22) | collective-permute-done | bytes 344096 | tf_op jit(solution)/shard_map/ppermute | solution.py:21
  88.3 4.1 %collective-permute-done.9.refs_4_ = bf16[24,7168]{1,0:T(8,128)(2,1)S(1)} collective-permute-done((bf16[24,7168]{1,0:T(8,128)(2,1)S(1)}, bf16[24,7168]{1,0:T(8,128)(2,1)S(1)}, u32[]{:S(2)}, u32[]{:S(2)}) %collective-permute-start.9) | collective-permute-done | bytes 344096 | tf_op jit(solution)/shard_map/ppermute | solution.py:21
  92.4 3.2 %collective-permute-done.6.refs_3_ = bf16[24,7168]{1,0:T(8,128)(2,1)S(1)} collective-permute-done((bf16[24,7168]{1,0:T(8,128)(2,1)S(1)}, bf16[24,7168]{1,0:T(8,128)(2,1)S(1)}, u32[]{:S(2)}, u32[]{:S(2)}) %collective-permute-start.6) | collective-permute-done | bytes 344096 | tf_op jit(solution)/shard_map/ppermute | solution.py:21
  96.2 6.8 %collective-permute-done.33.refs_7_ = bf16[24,7168]{1,0:T(8,128)(2,1)S(1)} collective-permute-done((bf16[24,7168]{1,0:T(8,128)(2,1)S(1)}, bf16[24,7168]{1,0:T(8,128)(2,1)S(1)}, u32[]{:S(2)}, u32[]{:S(2)}) %collective-permute-start.33) | collective-permute-done | bytes 344096 | tf_op jit(solution)/shard_map/ppermute | solution.py:21
  103.6 4.1 %collective-permute-done.24.refs_5_ = bf16[24,7168]{1,0:T(8,128)(2,1)S(1)} collective-permute-done((bf16[24,7168]{1,0:T(8,128)(2,1)S(1)}, bf16[24,7168]{1,0:T(8,128)(2,1)S(1)}, u32[]{:S(2)}, u32[]{:S(2)}) %collective-permute-start.24) | collective-permute-done | bytes 344096 | tf_op jit(solution)/shard_map/ppermute | solution.py:21
  107.7 1.5 copy-done.1
  109.2 3.3 %shard_map.128 = (f32[24,128]{1,0:T(8,128)S(1)}, f32[24,128]{1,0:T(8,128)S(1)}, f32[24,128]{1,0:T(8,128)S(1)}, f32[24,128]{1,0:T(8,128)S(1)}, f32[24,128]{1,0:T(...) custom-call(bf16[24,7168]{1,0:T(8,128)(2,1)S(1)} %shard_map.127.refs, ...), custom_call_target="tpu_custom_call" | custom-call | tf_op jit(solution)/shard_map/pallas_call | solution.py:25
  112.6 3.3 %collective-permute-start.12 = (bf16[24,7168]{1,0:T(8,128)(2,1)S(1)}, bf16[24,7168]{1,0:T(8,128)(2,1)S(1)}, u32[]{:S(2)}, u32[]{:S(2)}) collective-permute-start(bf16[24,7168]{1,0:T(8,128)(2,1)S(1)} %collective-permute-done.11.refs_6_), channel_id=1, source_target_pairs={{0,7},{1,0},{2,1},{3,2},{4,3},{5,4},{6,5},{7,6},{8,15},{9,8},{10,9... | collective-permute-start | bytes 1032200 | tf_op jit(solution)/shard_map/ppermute | solution.py:21
  115.9 2.8 %collective-permute-done.26.refs_7_ = bf16[24,7168]{1,0:T(8,128)(2,1)S(1)} collective-permute-done((bf16[24,7168]{1,0:T(8,128)(2,1)S(1)}, bf16[24,7168]{1,0:T(8,128)(2,1)S(1)}, u32[]{:S(2)}, u32[]{:S(2)}) %collective-permute-start.26) | collective-permute-done | bytes 344096 | tf_op jit(solution)/shard_map/ppermute | solution.py:21
  118.7 4.2 %shard_map.129 = (bf16[24,7168]{1,0:T(8,128)(2,1)S(1)}, bf16[24,7168]{1,0:T(8,128)(2,1)S(1)}, bf16[24,7168]{1,0:T(8,128)(2,1)S(1)}, bf16[24,7168]{1,0:T(8,128)(2...) custom-call(bf16[24,7168]{1,0:T(8,128)(2,1)S(1)} %get-tuple-element., ...), custom_call_target="tpu_custom_call" | custom-call | tf_op jit(solution)/shard_map/pallas_call | solution.py:25
  123.1 2.0 %collective-permute-start.34 = (bf16[24,7168]{1,0:T(8,128)(2,1)S(1)}, bf16[24,7168]{1,0:T(8,128)(2,1)S(1)}, u32[]{:S(2)}, u32[]{:S(2)}) collective-permute-start(bf16[24,7168]{1,0:T(8,128)(2,1)S(1)} %get-tuple-element.73), channel_id=1, source_target_pairs={{0,1},{1,2},{2,3},{3,4},{4,5},{5,6},{6,7},{7,0},{8,9},{9,10},{10,1... | collective-permute-start | bytes 1032200 | tf_op jit(solution)/shard_map/ppermute | solution.py:21
  125.1 3.7 %shard_map.125 = (bf16[24,7168]{1,0:T(8,128)(2,1)S(1)}, bf16[24,7168]{1,0:T(8,128)(2,1)S(1)}, bf16[24,7168]{1,0:T(8,128)(2,1)S(1)}, bf16[24,7168]{1,0:T(8,128)(2...) custom-call(bf16[24,7168]{1,0:T(8,128)(2,1)S(1)} %get-tuple-element., ...), custom_call_target="tpu_custom_call" | custom-call | tf_op jit(solution)/shard_map/pallas_call | solution.py:25
  128.8 2.2 %collective-permute-start.17 = (bf16[24,7168]{1,0:T(8,128)(2,1)S(1)}, bf16[24,7168]{1,0:T(8,128)(2,1)S(1)}, u32[]{:S(2)}, u32[]{:S(2)}) collective-permute-start(bf16[24,7168]{1,0:T(8,128)(2,1)S(1)} %get-tuple-element.52), channel_id=1, source_target_pairs={{0,1},{1,2},{2,3},{3,4},{4,5},{5,6},{6,7},{7,0},{8,9},{9,10},{10,1... | collective-permute-start | bytes 1032200 | tf_op jit(solution)/shard_map/ppermute | solution.py:21
  132.6 2.0 collective-permute-start.39
  134.6 1.4 collective-permute-start.35
  136.1 5.4 %collective-permute-done.17 = bf16[24,7168]{1,0:T(8,128)(2,1)S(1)} collective-permute-done((bf16[24,7168]{1,0:T(8,128)(2,1)S(1)}, bf16[24,7168]{1,0:T(8,128)(2,1)S(1)}, u32[]{:S(2)}, u32[]{:S(2)}) %collective-permute-start.17) | collective-permute-done | bytes 344096 | tf_op jit(solution)/shard_map/ppermute | solution.py:21
  141.5 1.9 collective-permute-start.18
  143.5 1.5 collective-permute-start.14
  145.0 4.4 %collective-permute-done.39 = bf16[24,7168]{1,0:T(8,128)(2,1)S(1)} collective-permute-done((bf16[24,7168]{1,0:T(8,128)(2,1)S(1)}, bf16[24,7168]{1,0:T(8,128)(2,1)S(1)}, u32[]{:S(2)}, u32[]{:S(2)}) %collective-permute-start.39) | collective-permute-done | bytes 344096 | tf_op jit(solution)/shard_map/ppermute | solution.py:21
  149.5 2.6 %collective-permute-start.40 = (bf16[24,7168]{1,0:T(8,128)(2,1)S(1)}, bf16[24,7168]{1,0:T(8,128)(2,1)S(1)}, u32[]{:S(2)}, u32[]{:S(2)}) collective-permute-start(bf16[24,7168]{1,0:T(8,128)(2,1)S(1)} %add_convert_fusion), channel_id=1, source_target_pairs={{0,7},{1,0},{2,1},{3,2},{4,3},{5,4},{6,5},{7,6},{8,15},{9,8},{10,9... | collective-permute-start | bytes 1032200 | tf_op jit(solution)/shard_map/ppermute | solution.py:21
  152.3 3.9 %collective-permute-done.18 = bf16[24,7168]{1,0:T(8,128)(2,1)S(1)} collective-permute-done((bf16[24,7168]{1,0:T(8,128)(2,1)S(1)}, bf16[24,7168]{1,0:T(8,128)(2,1)S(1)}, u32[]{:S(2)}, u32[]{:S(2)}) %collective-permute-start.18) | collective-permute-done | bytes 344096 | tf_op jit(solution)/shard_map/ppermute | solution.py:21
  156.3 1.9 collective-permute-start.19
  158.3 1.5 collective-permute-start.15
  159.7 4.7 %collective-permute-done.36 = bf16[24,7168]{1,0:T(8,128)(2,1)S(1)} collective-permute-done((bf16[24,7168]{1,0:T(8,128)(2,1)S(1)}, bf16[24,7168]{1,0:T(8,128)(2,1)S(1)}, u32[]{:S(2)}, u32[]{:S(2)}) %collective-permute-start.36) | collective-permute-done | bytes 344096 | tf_op jit(solution)/shard_map/ppermute | solution.py:21
  165.6 3.0 %collective-permute-done.15 = bf16[24,7168]{1,0:T(8,128)(2,1)S(1)} collective-permute-done((bf16[24,7168]{1,0:T(8,128)(2,1)S(1)}, bf16[24,7168]{1,0:T(8,128)(2,1)S(1)}, u32[]{:S(2)}, u32[]{:S(2)}) %collective-permute-start.15) | collective-permute-done | bytes 344096 | tf_op jit(solution)/shard_map/ppermute | solution.py:21
  168.6 1.7 collective-permute-start.16
  170.3 1.5 collective-permute-done.19.refs_2_
  171.8 4.0 %collective-permute-done.37.refs_4_ = bf16[24,7168]{1,0:T(8,128)(2,1)S(1)} collective-permute-done((bf16[24,7168]{1,0:T(8,128)(2,1)S(1)}, bf16[24,7168]{1,0:T(8,128)(2,1)S(1)}, u32[]{:S(2)}, u32[]{:S(2)}) %collective-permute-start.37) | collective-permute-done | bytes 344096 | tf_op jit(solution)/shard_map/ppermute | solution.py:21
  176.6 17.9 %all_to_all.15.back_ref = bf16[8,3,14336]{2,1,0:T(4,128)(2,1)S(1)} all-to-all(bf16[8,3,14336]{2,1,0:T(4,128)(2,1)S(1)} %shard_map.130), channel_id=1, replica_groups=mesh['pp'=4,'e'=8,'k'=8] {'e'}, dimensions={0} | all-to-all | bytes 1376256 | tf_op jit(solution)/shard_map/all_to_all | solution.py:328
  194.5 3.5 %shard_map.131 = (bf16[64,7168]{1,0:T(8,128)(2,1)}, bf16[64,7168]{1,0:T(8,128)(2,1)}) custom-call(bf16[8,3,14336]{2,1,0:T(4,128)(2,1)S(1)} %all_to_all.15.back_ref, bf16[64,7168]{1,0:T(8,128)(2,1)S(1)} %collective-permute-done.7.a_ref, s32[1,64]{1,0:T(1,128)S(1)} %bitcast.32, f32[1,64]{1,0:T(1,128)S(1)} %bitcast.33, bf16[64,7168]{1,0:T(8,128)(2,1)S(1)} %bitcast.21, ...), custom_call_target="tpu_custom_call" | custom-call | tf_op jit(solution)/shard_map/pallas_call | solution.py:384
  (91 shorter events, 13.8 us)
Async XLA Ops:
  0.6 3.2 %collective-permute-start.1 = (s32[1,64]{1,0:T(1,128)}, s32[1,64]{1,0:T(1,128)S(1)}, u32[]{:S(2)}, u32[]{:S(2)}) collective-permute-start(s32[1,64]{1,0:T(1,128)} %bitcast.26), channel_id=1, source_target_pairs={{0,64},{64,128},{128,192},{192,0},{1,65},{65,129},{129,193},{193,1... | collective-permute-start | bytes 776 | tf_op jit(solution)/shard_map/ppermute | solution.py:21
  0.7 3.2 %collective-permute-start = (s32[1,64]{1,0:T(1,128)}, s32[1,64]{1,0:T(1,128)S(1)}, u32[]{:S(2)}, u32[]{:S(2)}) collective-permute-start(s32[1,64]{1,0:T(1,128)} %bitcast.31), channel_id=1, source_target_pairs={{0,192},{64,0},{128,64},{192,128},{1,193},{65,1},{129,65},{193,129... | collective-permute-start | bytes 776 | tf_op jit(solution)/shard_map/ppermute | solution.py:21
  7.6 11.7 %collective-permute-start.2 = (bf16[24,7168]{1,0:T(8,128)(2,1)S(1)}, bf16[24,7168]{1,0:T(8,128)(2,1)S(1)}, u32[]{:S(2)}, u32[]{:S(2)}) collective-permute-start(bf16[24,7168]{1,0:T(8,128)(2,1)S(1)} %get-tuple-element.43), channel_id=1, source_target_pairs={{0,64},{64,128},{128,192},{192,0},{1,65},{65,129},{129,193},{193,1... | collective-permute-start | bytes 1032200 | tf_op jit(solution)/shard_map/ppermute | solution.py:21
  9.3 10.1 %collective-permute-start.3 = (bf16[24,7168]{1,0:T(8,128)(2,1)S(1)}, bf16[24,7168]{1,0:T(8,128)(2,1)S(1)}, u32[]{:S(2)}, u32[]{:S(2)}) collective-permute-start(bf16[24,7168]{1,0:T(8,128)(2,1)S(1)} %get-tuple-element.44), channel_id=1, source_target_pairs={{0,192},{64,0},{128,64},{192,128},{1,193},{65,1},{129,65},{193,129... | collective-permute-start | bytes 1032200 | tf_op jit(solution)/shard_map/ppermute | solution.py:21
  11.9 16.5 %all-to-all-start.1 = ((bf16[8,3,7168]{2,1,0:T(4,128)(2,1)}), bf16[8,3,7168]{2,1,0:T(4,128)(2,1)S(1)}, u32[]{:S(2)}, u32[]{:S(2)}) async-start(bf16[8,3,7168]{2,1,0:T(4,128)(2,1)} %shard_map.126), calls=%async_computation.1 | async-start | bytes 917504 | tf_op jit(solution)/shard_map/all_to_all | solution.py:328
  21.1 86.6 %copy-start = (bf16[1,1,7168,128]{3,2,1,0:T(8,128)(2,1)S(1)}, bf16[1,1,7168,128]{3,2,1,0:T(8,128)(2,1)}, u32[]{:S(2)}) copy-start(bf16[1,1,7168,128]{3,2,1,0:T(8,128)(2,1)} %param.19) | copy-start | bytes 5505028
  28.3 21.5 %all-to-all-start = ((bf16[8,3,14336]{2,1,0:T(4,128)(2,1)}), bf16[8,3,14336]{2,1,0:T(4,128)(2,1)S(1)}, u32[]{:S(2)}, u32[]{:S(2)}) async-start(bf16[8,3,14336]{2,1,0:T(4,128)(2,1)} %copy-done.4), calls=%async_computation | async-start | bytes 1835008 | tf_op jit(solution)/shard_map/all_to_all | solution.py:328
  33.5 13.1 %collective-permute-start.27 = (bf16[24,7168]{1,0:T(8,128)(2,1)S(1)}, bf16[24,7168]{1,0:T(8,128)(2,1)S(1)}, u32[]{:S(2)}, u32[]{:S(2)}) collective-permute-start(bf16[24,7168]{1,0:T(8,128)(2,1)S(1)} %shard_map.127.refs_0_), channel_id=1, source_target_pairs={{0,1},{1,2},{2,3},{3,4},{4,5},{5,6},{6,7},{7,0},{8,9},{9,10},{10,1... | collective-permute-start | bytes 1032200 | tf_op jit(solution)/shard_map/ppermute | solution.py:21
  35.5 11.1 %collective-permute-start.28 = (bf16[24,7168]{1,0:T(8,128)(2,1)S(1)}, bf16[24,7168]{1,0:T(8,128)(2,1)}, u32[]{:S(2)}, u32[]{:S(2)}) collective-permute-start(bf16[24,7168]{1,0:T(8,128)(2,1)S(1)} %shard_map.127.refs_0_), channel_id=1, source_target_pairs={{0,7},{1,0},{2,1},{3,2},{4,3},{5,4},{6,5},{7,6},{8,15},{9,8},{10,9... | collective-permute-start | bytes 1032200 | tf_op jit(solution)/shard_map/ppermute | solution.py:21
  46.6 12.3 %collective-permute-start.29 = (bf16[24,7168]{1,0:T(8,128)(2,1)S(1)}, bf16[24,7168]{1,0:T(8,128)(2,1)}, u32[]{:S(2)}, u32[]{:S(2)}) collective-permute-start(bf16[24,7168]{1,0:T(8,128)(2,1)S(1)} %collective-permute-done.27.refs_1_), channel_id=1, source_target_pairs={{0,1},{1,2},{2,3},{3,4},{4,5},{5,6},{6,7},{7,0},{8,9},{9,10},{10,1... | collective-permute-start | bytes 1032200 | tf_op jit(solution)/shard_map/ppermute | solution.py:21
  46.6 12.3 %collective-permute-start.30 = (bf16[24,7168]{1,0:T(8,128)(2,1)}, bf16[24,7168]{1,0:T(8,128)(2,1)}, u32[]{:S(2)}, u32[]{:S(2)}) collective-permute-start(bf16[24,7168]{1,0:T(8,128)(2,1)} %collective-permute-done.28.refs_2_), channel_id=1, source_target_pairs={{0,7},{1,0},{2,1},{3,2},{4,3},{5,4},{6,5},{7,6},{8,15},{9,8},{10,9... | collective-permute-start | bytes 1032200 | tf_op jit(solution)/shard_map/ppermute | solution.py:21
  50.3 15.9 %collective-permute-start.20 = (bf16[24,7168]{1,0:T(8,128)(2,1)S(1)}, bf16[24,7168]{1,0:T(8,128)(2,1)S(1)}, u32[]{:S(2)}, u32[]{:S(2)}) collective-permute-start(bf16[24,7168]{1,0:T(8,128)(2,1)S(1)} %get-tuple-element.55.refs_0_), channel_id=1, source_target_pairs={{0,1},{1,2},{2,3},{3,4},{4,5},{5,6},{6,7},{7,0},{8,9},{9,10},{10,1... | collective-permute-start | bytes 1032200 | tf_op jit(solution)/shard_map/ppermute | solution.py:21
  50.4 16.4 %collective-permute-start.21 = (bf16[24,7168]{1,0:T(8,128)(2,1)S(1)}, bf16[24,7168]{1,0:T(8,128)(2,1)S(1)}, u32[]{:S(2)}, u32[]{:S(2)}) collective-permute-start(bf16[24,7168]{1,0:T(8,128)(2,1)S(1)} %get-tuple-element.55.refs_0_), channel_id=1, source_target_pairs={{0,7},{1,0},{2,1},{3,2},{4,3},{5,4},{6,5},{7,6},{8,15},{9,8},{10,9... | collective-permute-start | bytes 1032200 | tf_op jit(solution)/shard_map/ppermute | solution.py:21
  53.6 19.7 %collective-permute-start.5 = (bf16[24,7168]{1,0:T(8,128)(2,1)S(1)}, bf16[24,7168]{1,0:T(8,128)(2,1)S(1)}, u32[]{:S(2)}, u32[]{:S(2)}) collective-permute-start(bf16[24,7168]{1,0:T(8,128)(2,1)S(1)} %get-tuple-element.45.refs_0_), channel_id=1, source_target_pairs={{0,7},{1,0},{2,1},{3,2},{4,3},{5,4},{6,5},{7,6},{8,15},{9,8},{10,9... | collective-permute-start | bytes 1032200 | tf_op jit(solution)/shard_map/ppermute | solution.py:21
  58.9 18.1 %collective-permute-start.4 = (bf16[24,7168]{1,0:T(8,128)(2,1)S(1)}, bf16[24,7168]{1,0:T(8,128)(2,1)S(1)}, u32[]{:S(2)}, u32[]{:S(2)}) collective-permute-start(bf16[24,7168]{1,0:T(8,128)(2,1)S(1)} %get-tuple-element.45.refs_0_), channel_id=1, source_target_pairs={{0,1},{1,2},{2,3},{3,4},{4,5},{5,6},{6,7},{7,0},{8,9},{9,10},{10,1... | collective-permute-start | bytes 1032200 | tf_op jit(solution)/shard_map/ppermute | solution.py:21
  58.9 22.0 %collective-permute-start.31 = (bf16[24,7168]{1,0:T(8,128)(2,1)}, bf16[24,7168]{1,0:T(8,128)(2,1)S(1)}, u32[]{:S(2)}, u32[]{:S(2)}) collective-permute-start(bf16[24,7168]{1,0:T(8,128)(2,1)} %collective-permute-done.29.refs_3_), channel_id=1, source_target_pairs={{0,1},{1,2},{2,3},{3,4},{4,5},{5,6},{6,7},{7,0},{8,9},{9,10},{10,1... | collective-permute-start | bytes 1032200 | tf_op jit(solution)/shard_map/ppermute | solution.py:21
  66.2 14.8 %collective-permute-start.32 = (bf16[24,7168]{1,0:T(8,128)(2,1)}, bf16[24,7168]{1,0:T(8,128)(2,1)S(1)}, u32[]{:S(2)}, u32[]{:S(2)}) collective-permute-start(bf16[24,7168]{1,0:T(8,128)(2,1)} %collective-permute-done.30.refs_4_), channel_id=1, source_target_pairs={{0,7},{1,0},{2,1},{3,2},{4,3},{5,4},{6,5},{7,6},{8,15},{9,8},{10,9... | collective-permute-start | bytes 1032200 | tf_op jit(solution)/shard_map/ppermute | solution.py:21
  66.7 21.6 %collective-permute-start.22 = (bf16[24,7168]{1,0:T(8,128)(2,1)S(1)}, bf16[24,7168]{1,0:T(8,128)(2,1)S(1)}, u32[]{:S(2)}, u32[]{:S(2)}) collective-permute-start(bf16[24,7168]{1,0:T(8,128)(2,1)S(1)} %collective-permute-done.20.refs_1_), channel_id=1, source_target_pairs={{0,1},{1,2},{2,3},{3,4},{4,5},{5,6},{6,7},{7,0},{8,9},{9,10},{10,1... | collective-permute-start | bytes 1032200 | tf_op jit(solution)/shard_map/ppermute | solution.py:21
  73.3 15.0 %collective-permute-start.23 = (bf16[24,7168]{1,0:T(8,128)(2,1)S(1)}, bf16[24,7168]{1,0:T(8,128)(2,1)S(1)}, u32[]{:S(2)}, u32[]{:S(2)}) collective-permute-start(bf16[24,7168]{1,0:T(8,128)(2,1)S(1)} %collective-permute-done.21.refs_2_), channel_id=1, source_target_pairs={{0,7},{1,0},{2,1},{3,2},{4,3},{5,4},{6,5},{7,6},{8,15},{9,8},{10,9... | collective-permute-start | bytes 1032200 | tf_op jit(solution)/shard_map/ppermute | solution.py:21
  77.0 15.4 %collective-permute-start.9 = (bf16[24,7168]{1,0:T(8,128)(2,1)S(1)}, bf16[24,7168]{1,0:T(8,128)(2,1)S(1)}, u32[]{:S(2)}, u32[]{:S(2)}) collective-permute-start(bf16[24,7168]{1,0:T(8,128)(2,1)S(1)} %collective-permute-done.5.refs_2_), channel_id=1, source_target_pairs={{0,7},{1,0},{2,1},{3,2},{4,3},{5,4},{6,5},{7,6},{8,15},{9,8},{10,9... | collective-permute-start | bytes 1032200 | tf_op jit(solution)/shard_map/ppermute | solution.py:21
  80.9 14.7 %collective-permute-start.6 = (bf16[24,7168]{1,0:T(8,128)(2,1)S(1)}, bf16[24,7168]{1,0:T(8,128)(2,1)S(1)}, u32[]{:S(2)}, u32[]{:S(2)}) collective-permute-start(bf16[24,7168]{1,0:T(8,128)(2,1)S(1)} %collective-permute-done.4.refs_1_), channel_id=1, source_target_pairs={{0,1},{1,2},{2,3},{3,4},{4,5},{5,6},{6,7},{7,0},{8,9},{9,10},{10,1... | collective-permute-start | bytes 1032200 | tf_op jit(solution)/shard_map/ppermute | solution.py:21
  80.9 22.1 %collective-permute-start.33 = (bf16[24,7168]{1,0:T(8,128)(2,1)S(1)}, bf16[24,7168]{1,0:T(8,128)(2,1)S(1)}, u32[]{:S(2)}, u32[]{:S(2)}) collective-permute-start(bf16[24,7168]{1,0:T(8,128)(2,1)S(1)} %collective-permute-done.31.refs_5_), channel_id=1, source_target_pairs={{0,1},{1,2},{2,3},{3,4},{4,5},{5,6},{6,7},{7,0},{8,9},{9,10},{10,1... | collective-permute-start | bytes 1032200 | tf_op jit(solution)/shard_map/ppermute | solution.py:21
  88.3 19.4 %collective-permute-start.24 = (bf16[24,7168]{1,0:T(8,128)(2,1)S(1)}, bf16[24,7168]{1,0:T(8,128)(2,1)S(1)}, u32[]{:S(2)}, u32[]{:S(2)}) collective-permute-start(bf16[24,7168]{1,0:T(8,128)(2,1)S(1)} %collective-permute-done.22.refs_3_), channel_id=1, source_target_pairs={{0,1},{1,2},{2,3},{3,4},{4,5},{5,6},{6,7},{7,0},{8,9},{9,10},{10,1... | collective-permute-start | bytes 1032200 | tf_op jit(solution)/shard_map/ppermute | solution.py:21
  88.3 34.7 %collective-permute-start.7 = (bf16[64,7168]{1,0:T(8,128)(2,1)}, bf16[64,7168]{1,0:T(8,128)(2,1)S(1)}, u32[]{:S(2)}, u32[]{:S(2)}) collective-permute-start(bf16[64,7168]{1,0:T(8,128)(2,1)} %bitcast.22), channel_id=1, source_target_pairs={{0,64},{64,128},{128,192},{192,0},{1,65},{65,129},{129,193},{193,1... | collective-permute-start | bytes 2752520 | tf_op jit(solution)/shard_map/ppermute | solution.py:21
  92.4 30.6 %collective-permute-start.8 = (bf16[64,7168]{1,0:T(8,128)(2,1)}, bf16[64,7168]{1,0:T(8,128)(2,1)S(1)}, u32[]{:S(2)}, u32[]{:S(2)}) collective-permute-start(bf16[64,7168]{1,0:T(8,128)(2,1)} %bitcast.24), channel_id=1, source_target_pairs={{0,192},{64,0},{128,64},{192,128},{1,193},{65,1},{129,65},{193,129... | collective-permute-start | bytes 2752520 | tf_op jit(solution)/shard_map/ppermute | solution.py:21
  95.7 16.8 %collective-permute-start.25 = (bf16[24,7168]{1,0:T(8,128)(2,1)S(1)}, bf16[24,7168]{1,0:T(8,128)(2,1)S(1)}, u32[]{:S(2)}, u32[]{:S(2)}) collective-permute-start(bf16[24,7168]{1,0:T(8,128)(2,1)S(1)} %collective-permute-done.23.refs_4_), channel_id=1, source_target_pairs={{0,7},{1,0},{2,1},{3,2},{4,3},{5,4},{6,5},{7,6},{8,15},{9,8},{10,9... | collective-permute-start | bytes 1032200 | tf_op jit(solution)/shard_map/ppermute | solution.py:21
  103.0 9.5 %collective-permute-start.11 = (bf16[24,7168]{1,0:T(8,128)(2,1)S(1)}, bf16[24,7168]{1,0:T(8,128)(2,1)S(1)}, u32[]{:S(2)}, u32[]{:S(2)}) collective-permute-start(bf16[24,7168]{1,0:T(8,128)(2,1)S(1)} %collective-permute-done.9.refs_4_), channel_id=1, source_target_pairs={{0,7},{1,0},{2,1},{3,2},{4,3},{5,4},{6,5},{7,6},{8,15},{9,8},{10,9... | collective-permute-start | bytes 1032200 | tf_op jit(solution)/shard_map/ppermute | solution.py:21
  107.7 11.0 %collective-permute-start.26 = (bf16[24,7168]{1,0:T(8,128)(2,1)S(1)}, bf16[24,7168]{1,0:T(8,128)(2,1)S(1)}, u32[]{:S(2)}, u32[]{:S(2)}) collective-permute-start(bf16[24,7168]{1,0:T(8,128)(2,1)S(1)} %collective-permute-done.24.refs_5_), channel_id=1, source_target_pairs={{0,1},{1,2},{2,3},{3,4},{4,5},{5,6},{6,7},{7,0},{8,9},{9,10},{10,1... | collective-permute-start | bytes 1032200 | tf_op jit(solution)/shard_map/ppermute | solution.py:21
  112.5 12.6 %collective-permute-start.10 = (bf16[24,7168]{1,0:T(8,128)(2,1)S(1)}, bf16[24,7168]{1,0:T(8,128)(2,1)S(1)}, u32[]{:S(2)}, u32[]{:S(2)}) collective-permute-start(bf16[24,7168]{1,0:T(8,128)(2,1)S(1)} %collective-permute-done.6.refs_3_), channel_id=1, source_target_pairs={{0,1},{1,2},{2,3},{3,4},{4,5},{5,6},{6,7},{7,0},{8,9},{9,10},{10,1... | collective-permute-start | bytes 1032200 | tf_op jit(solution)/shard_map/ppermute | solution.py:21
  112.6 12.5 %collective-permute-start.12 = (bf16[24,7168]{1,0:T(8,128)(2,1)S(1)}, bf16[24,7168]{1,0:T(8,128)(2,1)S(1)}, u32[]{:S(2)}, u32[]{:S(2)}) collective-permute-start(bf16[24,7168]{1,0:T(8,128)(2,1)S(1)} %collective-permute-done.11.refs_6_), channel_id=1, source_target_pairs={{0,7},{1,0},{2,1},{3,2},{4,3},{5,4},{6,5},{7,6},{8,15},{9,8},{10,9... | collective-permute-start | bytes 1032200 | tf_op jit(solution)/shard_map/ppermute | solution.py:21
  123.0 9.6 %collective-permute-start.38 = (bf16[24,7168]{1,0:T(8,128)(2,1)S(1)}, bf16[24,7168]{1,0:T(8,128)(2,1)S(1)}, u32[]{:S(2)}, u32[]{:S(2)}) collective-permute-start(bf16[24,7168]{1,0:T(8,128)(2,1)S(1)} %get-tuple-element.77), channel_id=1, source_target_pairs={{0,7},{1,0},{2,1},{3,2},{4,3},{5,4},{6,5},{7,6},{8,15},{9,8},{10,9... | collective-permute-start | bytes 1032200 | tf_op jit(solution)/shard_map/ppermute | solution.py:21
  123.1 11.5 %collective-permute-start.34 = (bf16[24,7168]{1,0:T(8,128)(2,1)S(1)}, bf16[24,7168]{1,0:T(8,128)(2,1)S(1)}, u32[]{:S(2)}, u32[]{:S(2)}) collective-permute-start(bf16[24,7168]{1,0:T(8,128)(2,1)S(1)} %get-tuple-element.73), channel_id=1, source_target_pairs={{0,1},{1,2},{2,3},{3,4},{4,5},{5,6},{6,7},{7,0},{8,9},{9,10},{10,1... | collective-permute-start | bytes 1032200 | tf_op jit(solution)/shard_map/ppermute | solution.py:21
  128.8 12.6 %collective-permute-start.17 = (bf16[24,7168]{1,0:T(8,128)(2,1)S(1)}, bf16[24,7168]{1,0:T(8,128)(2,1)S(1)}, u32[]{:S(2)}, u32[]{:S(2)}) collective-permute-start(bf16[24,7168]{1,0:T(8,128)(2,1)S(1)} %get-tuple-element.52), channel_id=1, source_target_pairs={{0,1},{1,2},{2,3},{3,4},{4,5},{5,6},{6,7},{7,0},{8,9},{9,10},{10,1... | collective-permute-start | bytes 1032200 | tf_op jit(solution)/shard_map/ppermute | solution.py:21
  131.0 12.5 %collective-permute-start.13 = (bf16[24,7168]{1,0:T(8,128)(2,1)S(1)}, bf16[24,7168]{1,0:T(8,128)(2,1)S(1)}, u32[]{:S(2)}, u32[]{:S(2)}) collective-permute-start(bf16[24,7168]{1,0:T(8,128)(2,1)S(1)} %get-tuple-element.48), channel_id=1, source_target_pairs={{0,7},{1,0},{2,1},{3,2},{4,3},{5,4},{6,5},{7,6},{8,15},{9,8},{10,9... | collective-permute-start | bytes 1032200 | tf_op jit(solution)/shard_map/ppermute | solution.py:21
  132.6 16.8 %collective-permute-start.39 = (bf16[24,7168]{1,0:T(8,128)(2,1)S(1)}, bf16[24,7168]{1,0:T(8,128)(2,1)S(1)}, u32[]{:S(2)}, u32[]{:S(2)}) collective-permute-start(bf16[24,7168]{1,0:T(8,128)(2,1)S(1)} %add_convert_fusion.1), channel_id=1, source_target_pairs={{0,7},{1,0},{2,1},{3,2},{4,3},{5,4},{6,5},{7,6},{8,15},{9,8},{10,9... | collective-permute-start | bytes 1032200 | tf_op jit(solution)/shard_map/ppermute | solution.py:21
  134.6 17.4 %collective-permute-start.35 = (bf16[24,7168]{1,0:T(8,128)(2,1)S(1)}, bf16[24,7168]{1,0:T(8,128)(2,1)S(1)}, u32[]{:S(2)}, u32[]{:S(2)}) collective-permute-start(bf16[24,7168]{1,0:T(8,128)(2,1)S(1)} %add_convert_fusion.4), channel_id=1, source_target_pairs={{0,1},{1,2},{2,3},{3,4},{4,5},{5,6},{6,7},{7,0},{8,9},{9,10},{10,1... | collective-permute-start | bytes 1032200 | tf_op jit(solution)/shard_map/ppermute | solution.py:21
  141.5 14.7 %collective-permute-start.18 = (bf16[24,7168]{1,0:T(8,128)(2,1)S(1)}, bf16[24,7168]{1,0:T(8,128)(2,1)S(1)}, u32[]{:S(2)}, u32[]{:S(2)}) collective-permute-start(bf16[24,7168]{1,0:T(8,128)(2,1)S(1)} %add_convert_fusion.6), channel_id=1, source_target_pairs={{0,1},{1,2},{2,3},{3,4},{4,5},{5,6},{6,7},{7,0},{8,9},{9,10},{10,1... | collective-permute-start | bytes 1032200 | tf_op jit(solution)/shard_map/ppermute | solution.py:21
  143.5 14.7 %collective-permute-start.14 = (bf16[24,7168]{1,0:T(8,128)(2,1)S(1)}, bf16[24,7168]{1,0:T(8,128)(2,1)S(1)}, u32[]{:S(2)}, u32[]{:S(2)}) collective-permute-start(bf16[24,7168]{1,0:T(8,128)(2,1)S(1)} %add_convert_fusion.9), channel_id=1, source_target_pairs={{0,7},{1,0},{2,1},{3,2},{4,3},{5,4},{6,5},{7,6},{8,15},{9,8},{10,9... | collective-permute-start | bytes 1032200 | tf_op jit(solution)/shard_map/ppermute | solution.py:21
  149.5 20.8 %collective-permute-start.40 = (bf16[24,7168]{1,0:T(8,128)(2,1)S(1)}, bf16[24,7168]{1,0:T(8,128)(2,1)S(1)}, u32[]{:S(2)}, u32[]{:S(2)}) collective-permute-start(bf16[24,7168]{1,0:T(8,128)(2,1)S(1)} %add_convert_fusion), channel_id=1, source_target_pairs={{0,7},{1,0},{2,1},{3,2},{4,3},{5,4},{6,5},{7,6},{8,15},{9,8},{10,9... | collective-permute-start | bytes 1032200 | tf_op jit(solution)/shard_map/ppermute | solution.py:21
  152.2 12.3 %collective-permute-start.36 = (bf16[24,7168]{1,0:T(8,128)(2,1)S(1)}, bf16[24,7168]{1,0:T(8,128)(2,1)S(1)}, u32[]{:S(2)}, u32[]{:S(2)}) collective-permute-start(bf16[24,7168]{1,0:T(8,128)(2,1)S(1)} %add_convert_fusion.3), channel_id=1, source_target_pairs={{0,1},{1,2},{2,3},{3,4},{4,5},{5,6},{6,7},{7,0},{8,9},{9,10},{10,1... | collective-permute-start | bytes 1032200 | tf_op jit(solution)/shard_map/ppermute | solution.py:21
  156.3 15.6 %collective-permute-start.19 = (bf16[24,7168]{1,0:T(8,128)(2,1)S(1)}, bf16[24,7168]{1,0:T(8,128)(2,1)S(1)}, u32[]{:S(2)}, u32[]{:S(2)}) collective-permute-start(bf16[24,7168]{1,0:T(8,128)(2,1)S(1)} %add_convert_fusion.5), channel_id=1, source_target_pairs={{0,1},{1,2},{2,3},{3,4},{4,5},{5,6},{6,7},{7,0},{8,9},{9,10},{10,1... | collective-permute-start | bytes 1032200 | tf_op jit(solution)/shard_map/ppermute | solution.py:21
  158.3 10.3 %collective-permute-start.15 = (bf16[24,7168]{1,0:T(8,128)(2,1)S(1)}, bf16[24,7168]{1,0:T(8,128)(2,1)S(1)}, u32[]{:S(2)}, u32[]{:S(2)}) collective-permute-start(bf16[24,7168]{1,0:T(8,128)(2,1)S(1)} %add_convert_fusion.8), channel_id=1, source_target_pairs={{0,7},{1,0},{2,1},{3,2},{4,3},{5,4},{6,5},{7,6},{8,15},{9,8},{10,9... | collective-permute-start | bytes 1032200 | tf_op jit(solution)/shard_map/ppermute | solution.py:21
  164.5 11.3 %collective-permute-start.37 = (bf16[24,7168]{1,0:T(8,128)(2,1)S(1)}, bf16[24,7168]{1,0:T(8,128)(2,1)S(1)}, u32[]{:S(2)}, u32[]{:S(2)}) collective-permute-start(bf16[24,7168]{1,0:T(8,128)(2,1)S(1)} %add_convert_fusion.2), channel_id=1, source_target_pairs={{0,1},{1,2},{2,3},{3,4},{4,5},{5,6},{6,7},{7,0},{8,9},{9,10},{10,1... | collective-permute-start | bytes 1032200 | tf_op jit(solution)/shard_map/ppermute | solution.py:21
  168.6 7.3 %collective-permute-start.16 = (bf16[24,7168]{1,0:T(8,128)(2,1)S(1)}, bf16[24,7168]{1,0:T(8,128)(2,1)S(1)}, u32[]{:S(2)}, u32[]{:S(2)}) collective-permute-start(bf16[24,7168]{1,0:T(8,128)(2,1)S(1)} %add_convert_fusion.7), channel_id=1, source_target_pairs={{0,7},{1,0},{2,1},{3,2},{4,3},{5,4},{6,5},{7,6},{8,15},{9,8},{10,9... | collective-permute-start | bytes 1032200 | tf_op jit(solution)/shard_map/ppermute | solution.py:21
  176.0 18.5 %copy-start.10 = (f32[1,7168]{1,0:T(1,128)S(1)}, f32[1,7168]{1,0:T(1,128)}, u32[]{:S(2)}) copy-start(f32[1,7168]{1,0:T(1,128)} %gain_ref.5) | copy-start | bytes 86020
  176.0 18.5 %copy-start.12 = (s32[1,64,1]{1,2,0:T(1,128)S(1)}, s32[1,64,1]{1,2,0:T(1,128)}, u32[]{:S(2)}) copy-start(s32[1,64,1]{1,2,0:T(1,128)} %param.16) | copy-start | bytes 772
  176.0 18.5 %copy-start.14 = (s32[1,64,1]{1,2,0:T(1,128)S(1)}, s32[1,64,1]{1,2,0:T(1,128)}, u32[]{:S(2)}) copy-start(s32[1,64,1]{1,2,0:T(1,128)} %param.12) | copy-start | bytes 772
  176.0 18.5 %copy-start.15 = (f32[1,64,1]{1,2,0:T(1,128)S(1)}, f32[1,64,1]{1,2,0:T(1,128)}, u32[]{:S(2)}) copy-start(f32[1,64,1]{1,2,0:T(1,128)} %param.13) | copy-start | bytes 772
  (11 other events, 70.5 us)
